TPU v7x, 128 devices: a whole 4x4x4 slice. The times are simulated.
128 devices in a mesh: gx: 4 (over x), gy: 32 (over y, z, core).
Axes of the slice: x: 4, y: 4, z: 4, core: 2. Of those that a mesh axis runs over, the one named last changes fastest.
Arguments:
- velocity: float32 [3, 32, 1024, 128], P(None, 'gx', 'gy'), may hold values from -4 to 4
- basis: bfloat16 [64, 3, 32, 1024, 128], P(None, None, 'gx', 'gy'), may hold values from -100 to 100
- snapshots: bfloat16 [63, 3, 32, 1024, 128], P(None, None, 'gx', 'gy'), may hold values from -100 to 100
Outputs:
- advanced: float32 [3, 32, 1024, 128], P(None, 'gx', 'gy')
- factor: float32 [128, 128], replicated
All inputs are finite; a program needn't handle non-finite values.
Results may differ from a plain program's by a relative error of at most 0.0003.
Values sent between devices are 32-bit elements; how exact they have to be, the bound alone decides.
No kernel may reach another device: no remote copies, remote signals or barrier semaphores. Data moves between devices by JAX's collectives and lax.ppermute only.
A program may use at most 128 MiB of HBM per device.

v0:
```python
import math

import jax
import jax.numpy as jnp
from jax import lax
from jax.sharding import PartitionSpec as P

TIME_STEP = 0.0002
VISCOSITY = 0.005
STEP_X = 0.0123
STEP_Z = 0.0092
STRETCH = 2.0


def with_halo(cells, sides, width):
    for axis, dim in sides:
        count = lax.axis_size(axis)
        head = lax.slice_in_dim(cells, 0, width, axis=dim)
        tail = lax.slice_in_dim(cells, cells.shape[dim] - width, cells.shape[dim], axis=dim)
        cells = jnp.concatenate(
            [
                lax.ppermute(tail, axis, [(i, (i + 1) % count) for i in range(count)]),
                cells,
                lax.ppermute(head, axis, [((i + 1) % count, i) for i in range(count)]),
            ],
            axis=dim,
        )
    return cells


def wall_weights(points):
    positions = jnp.arange(points + 2, dtype=jnp.float32)
    nodes = -jnp.tanh(STRETCH * (1.0 - 2.0 * positions / (points + 1))) / math.tanh(STRETCH)
    below = nodes[1:-1] - nodes[:-2]
    above = nodes[2:] - nodes[1:-1]
    spread = above * below * (above + below)
    return (
        below * below / spread,
        -(above * above) / spread,
        (above * above - below * below) / spread,
        2.0 * below / spread,
        -2.0 * (above + below) / spread,
        2.0 * above / spread,
    )


def tendency(widened):
    weights = wall_weights(widened.shape[3])
    center = widened[:, 2:-2, 2:-2, :]
    length_x = center.shape[1]
    length_z = center.shape[2]

    def along_x(offset):
        return widened[:, 2 + offset : 2 + offset + length_x, 2:-2, :]

    def along_z(offset):
        return widened[:, 2:-2, 2 + offset : 2 + offset + length_z, :]

    slope_x = (-along_x(2) + 8.0 * along_x(1) - 8.0 * along_x(-1) + along_x(-2)) / (12.0 * STEP_X)
    curve_x = (
        -along_x(2) + 16.0 * along_x(1) - 30.0 * center + 16.0 * along_x(-1) - along_x(-2)
    ) / (12.0 * STEP_X * STEP_X)
    slope_z = (-along_z(2) + 8.0 * along_z(1) - 8.0 * along_z(-1) + along_z(-2)) / (12.0 * STEP_Z)
    curve_z = (
        -along_z(2) + 16.0 * along_z(1) - 30.0 * center + 16.0 * along_z(-1) - along_z(-2)
    ) / (12.0 * STEP_Z * STEP_Z)
    padded = jnp.pad(center, ((0, 0), (0, 0), (0, 0), (1, 1)))
    upper_vals = padded[..., 2:]
    lower_vals = padded[..., :-2]
    slope_y = weights[0] * upper_vals + weights[1] * lower_vals + weights[2] * center
    curve_y = weights[3] * upper_vals + weights[4] * center + weights[5] * lower_vals
    carried = center[0:1] * slope_x + center[1:2] * slope_y + center[2:3] * slope_z
    return -carried + VISCOSITY * (curve_x + curve_y + curve_z)


def inner(left, right):
    return lax.dot_general(
        left, right, (((1,), (1,)), ((), ())), preferred_element_type=jnp.float32
    )


def widen_once(field):
    return with_halo(field, (("gx", 1), ("gy", 2)), 2)


def upper_factor(gram):
    return jnp.linalg.cholesky(gram).T


def stacked_factor(pieces):
    gram = jnp.einsum("kij,kil->jl", pieces, pieces, precision=lax.Precision.HIGHEST)
    return upper_factor(gram)


def local(velocity, basis, snapshots):
    section_field = velocity + TIME_STEP * tendency(widen_once(velocity))
    advanced = 0.5 * (velocity + section_field + TIME_STEP * tendency(widen_once(section_field)))
    newest = advanced.astype(jnp.bfloat16).reshape(1, -1)
    block = jnp.concatenate(
        [basis.reshape(basis.shape[0], -1), snapshots.reshape(snapshots.shape[0], -1), newest], 0
    )
    total_rows = (
        3.0
        * velocity.shape[1]
        * lax.axis_size("gx")
        * velocity.shape[2]
        * lax.axis_size("gy")
        * velocity.shape[3]
    )
    local_gram = inner(block, block) * (1.0 / total_rows)
    local_factor = upper_factor(local_gram)
    pieces = lax.all_gather(local_factor[None], "gy", axis=0, tiled=True)
    group_factor = stacked_factor(pieces)
    pieces = lax.all_gather(group_factor[None], "gx", axis=0, tiled=True)
    factor = stacked_factor(pieces)
    return (advanced, factor)


def solution(mesh):
    return jax.shard_map(
        local,
        mesh=mesh,
        in_specs=(
            P(None, "gx", "gy", None),
            P(None, None, "gx", "gy", None),
            P(None, None, "gx", "gy", None),
        ),
        out_specs=(P(None, "gx", "gy", None), P()),
        check_vma=False,
    )
```

profile of v0, /device:TPU:1, one launch (start us, length us, event | category | flops | bytes accessed | tf_op | source)
XLA Modules:
  0.0 226.3 jit_solution(18059079550800627452)
XLA Ops:
  7.2 0.0 all-gather.4.cloned.1.call-start
  7.2 1.0 fusion.40
  8.2 2.1 collective-permute-start.1
  10.3 1.3 collective-permute-start
  11.6 1.1 multiply_bitcast_fusion.1
  12.7 0.1 multiply_divide_fusion.3
  12.8 0.8 collective-permute-done.1
  13.6 1.1 constant_dynamic-update-slice_fusion.1
  14.7 0.0 collective-permute-done
  14.8 3.6 %collective-permute-start.3 = (f32[3,12,2,128]{3,2,1,0:T(2,128)S(1)}, f32[3,12,2,128]{3,2,1,0:T(2,128)S(1)}, u32[]{:S(2)}, u32[]{:S(2)}) collective-permute-start(f32[3,12,2,128]{3,2,1,0:T(2,128)S(1)} %get-tuple-element.15), channel_id=1, source_target_pairs={{0,1},{1,2},{2,3},{3,4},{4,5},{5,6},{6,7},{7,8},{8,9},{9,10},{10,1... | collective-permute-start | bytes 110600 | tf_op jit(solution)/shard_map/ppermute | solution.py:22
  18.4 0.0 collective-permute-start.2
  18.4 1.0 collective-permute-done.3
  19.4 2.6 %collective-permute-done.2 = f32[3,12,2,128]{3,2,1,0:T(2,128)S(1)} collective-permute-done((f32[3,12,2,128]{3,2,1,0:T(2,128)S(1)}, f32[3,12,2,128]{3,2,1,0:T(2,128)S(1)}, u32[]{:S(2)}, u32[]{:S(2)}) %collective-permute-start.2) | collective-permute-done | bytes 36896 | tf_op jit(solution)/shard_map/ppermute | solution.py:24
  22.1 2.3 %multiply_add_fusion = f32[3,8,32,128]{3,2,1,0:T(8,128)S(1)} fusion(f32[3,8,32,128]{3,2,1,0:T(8,128)} %param.4, f32[3,12,32,128]{3,2,1,0:T(8,128)S(1)} %get-tuple-element.30, f32[3,12,2,128]{3,2,1,0:T(2,128)S(1)} %collective-permute-done.3, f32[3,12,2,128]{3,2,1,0:T(2,128)S(1)} %collective-permute-done.2, f32[3,10,32,128]{3,2,1,0:T(8,128)S(1)} %get-tuple-element.26, ...), kind=kLoop, calls=%fused_computation.40 | loop fusion | flops 5210112 | bytes 3419136 | tf_op jit(solution)/shard_map/add | solution.py:96
  24.4 1.8 collective-permute-start.4
  26.3 0.0 collective-permute-start.5
  26.3 0.0 slice-start
  26.3 0.0 slice-start.1
  26.3 7.7 %pad.45 = bf16[64,768,128]{2,1,0:T(8,128)(2,1)S(1)} pad(bf16[63,768,128]{2,1,0:T(8,128)(2,1)} %bitcast.67, bf16[]{:T(256)} %constant.89), padding=0_1x0_0x0_0 | pad | bytes 24969218
  34.0 0.0 slice-start.2
  34.0 27.4 %copy.18 = bf16[8,8,768,128]{3,1,2,0:T(8,128)(2,1)} copy(bf16[8,8,768,128]{3,2,1,0:T(8,128)(2,1)S(1)} %bitcast.61) | data formatting | bytes 25165824
  61.4 0.0 slice-done
  61.4 0.0 slice-done.1
  61.4 0.0 slice-done.2
  61.4 0.0 copy-start
  61.4 27.4 %copy.30 = bf16[8,8,768,128]{3,1,2,0:T(8,128)(2,1)} copy(bf16[8,8,768,128]{3,2,1,0:T(8,128)(2,1)S(1)} %bitcast.64) | data formatting | bytes 25165824
  88.8 0.0 collective-permute-done.4
  88.8 0.0 collective-permute-done.5
  88.9 1.7 collective-permute-start.6
  90.6 0.1 collective-permute-start.7
  90.7 1.6 collective-permute-done.6
  92.3 3.8 %collective-permute-done.7 = f32[3,12,2,128]{3,2,1,0:T(2,128)S(1)} collective-permute-done((f32[3,12,2,128]{3,2,1,0:T(2,128)S(1)}, f32[3,12,2,128]{3,2,1,0:T(2,128)S(1)}, u32[]{:S(2)}, u32[]{:S(2)}) %collective-permute-start.7) | collective-permute-done | bytes 36896 | tf_op jit(solution)/shard_map/ppermute | solution.py:22
  96.1 0.1 pad_maximum_fusion
  96.2 0.0 copy-done
  96.2 1.5 fusion.37
  97.8 0.1 reshape.34
  97.8 19.0 %fusion.12 = f32[128,128]{0,1:T(8,128)S(1)} fusion(bf16[1,98304]{1,0:T(2,128)(2,1)S(1)} %reshape.34, bf16[63,98304]{1,0:T(8,128)(2,1)} %bitcast.65, bf16[64,98304]{1,0:T(8,128)(2,1)} %bitcast.66), kind=kOutput, calls=%fused_computation.22 | convolution fusion | flops 3296739328 | bytes 25231360 | tf_op jit(solution)/shard_map/dot_general | solution.py:77
  116.9 0.1 copy.6
  117.0 11.7 %cholesky.59 = f32[128,128]{1,0:T(8,128)S(1)} custom-call(f32[128,128]{1,0:T(8,128)S(1)} %fusion.27), custom_call_target="Cholesky" | custom-call | tf_op jit(solution)/shard_map/jit(cholesky)/cholesky | solution.py:87
  128.7 0.6 compare_reduce_fusion.2
  129.4 1.2 fusion.35
  130.6 0.0 all-gather.4.cloned.1.call-update
  130.6 46.8 %all-gather.4.cloned.1.call-done = f32[4096,128]{0,1:T(8,128)} async-done(((f32[128,128]{0,1:T(8,128)}), f32[4096,128]{0,1:T(8,128)}) %all-gather.4.cloned.1.call-update) | async-done | bytes 2097168 | tf_op jit(solution)/shard_map/all_gather | solution.py:112
  177.4 4.0 %fusion.9 = f32[128,128]{1,0:T(8,128)S(1)} fusion(f32[4096,128]{0,1:T(8,128)} %all-gather.4.cloned.1.call-done), kind=kOutput, calls=%fused_computation.10 | convolution fusion | flops 805306368 | bytes 2162688 | tf_op jit(solution)/shard_map/kij,kil->jl/dot_general | solution.py:91
  181.4 0.1 copy.9
  181.6 11.7 %cholesky.70 = f32[128,128]{1,0:T(8,128)S(1)} custom-call(f32[128,128]{1,0:T(8,128)S(1)} %fusion.26), custom_call_target="Cholesky" | custom-call | tf_op jit(solution)/shard_map/jit(cholesky)/cholesky | solution.py:87
  193.3 0.6 compare_reduce_fusion.1
  193.9 0.7 fusion.34
  194.6 10.6 %all-gather.1 = f32[512,128]{0,1:T(8,128)S(1)} all-gather(f32[128,128]{0,1:T(8,128)S(1)} %fusion.34), channel_id=3, replica_groups=mesh['gx'=4,'gy'=32] {'gx'}, dimensions={0}, use_global_device_ids=true | all-gather | bytes 327680 | tf_op jit(solution)/shard_map/all_gather | solution.py:114
  205.2 0.4 convolution_bitcast_fusion
  205.6 0.1 copy.12
  205.7 11.7 %cholesky.81 = f32[128,128]{1,0:T(8,128)S(1)} custom-call(f32[128,128]{1,0:T(8,128)S(1)} %fusion.25), custom_call_target="Cholesky" | custom-call | tf_op jit(solution)/shard_map/jit(cholesky)/cholesky | solution.py:87
  217.4 0.6 compare_reduce_fusion
  218.1 0.7 select_bitcast_fusion
  218.7 0.7 copy.13
  (15 shorter events, 0.3 us)
Async XLA Ops:
  7.2 170.2 %all-gather.4.cloned.1.call-start = ((), (), s32[]{:S(2)}) async-start(), calls=%async_computation | async-start | bytes 2162688 | tf_op jit(solution)/shard_map/all_gather | solution.py:112
  8.2 5.4 %collective-permute-start.1 = (f32[3,2,32,128]{3,2,1,0:T(8,128)S(1)}, f32[3,2,32,128]{3,2,1,0:T(8,128)S(1)}, u32[]{:S(2)}, u32[]{:S(2)}) collective-permute-start(f32[3,2,32,128]{3,2,1,0:T(8,128)S(1)} %get-tuple-element.28), channel_id=1, source_target_pairs={{0,32},{32,64},{64,96},{96,0},{1,33},{33,65},{65,97},{97,1},{2,34}... | collective-permute-start | bytes 294920 | tf_op jit(solution)/shard_map/ppermute | solution.py:22
  10.3 4.4 %collective-permute-start = (f32[3,2,32,128]{3,2,1,0:T(8,128)S(1)}, f32[3,2,32,128]{3,2,1,0:T(8,128)S(1)}, u32[]{:S(2)}, u32[]{:S(2)}) collective-permute-start(f32[3,2,32,128]{3,2,1,0:T(8,128)S(1)} %get-tuple-element.27), channel_id=1, source_target_pairs={{32,0},{64,32},{96,64},{0,96},{33,1},{65,33},{97,65},{1,97},{34,2}... | collective-permute-start | bytes 294920 | tf_op jit(solution)/shard_map/ppermute | solution.py:24
  14.8 4.7 %collective-permute-start.3 = (f32[3,12,2,128]{3,2,1,0:T(2,128)S(1)}, f32[3,12,2,128]{3,2,1,0:T(2,128)S(1)}, u32[]{:S(2)}, u32[]{:S(2)}) collective-permute-start(f32[3,12,2,128]{3,2,1,0:T(2,128)S(1)} %get-tuple-element.15), channel_id=1, source_target_pairs={{0,1},{1,2},{2,3},{3,4},{4,5},{5,6},{6,7},{7,8},{8,9},{9,10},{10,1... | collective-permute-start | bytes 110600 | tf_op jit(solution)/shard_map/ppermute | solution.py:22
  18.4 3.7 %collective-permute-start.2 = (f32[3,12,2,128]{3,2,1,0:T(2,128)S(1)}, f32[3,12,2,128]{3,2,1,0:T(2,128)S(1)}, u32[]{:S(2)}, u32[]{:S(2)}) collective-permute-start(f32[3,12,2,128]{3,2,1,0:T(2,128)S(1)} %get-tuple-element.14), channel_id=1, source_target_pairs={{1,0},{2,1},{3,2},{4,3},{5,4},{6,5},{7,6},{8,7},{9,8},{10,9},{11,1... | collective-permute-start | bytes 110600 | tf_op jit(solution)/shard_map/ppermute | solution.py:24
  24.4 64.4 %collective-permute-start.4 = (f32[3,2,32,128]{3,2,1,0:T(8,128)S(1)}, f32[3,2,32,128]{3,2,1,0:T(8,128)S(1)}, u32[]{:S(2)}, u32[]{:S(2)}) collective-permute-start(f32[3,2,32,128]{3,2,1,0:T(8,128)S(1)} %get-tuple-element.20), channel_id=1, source_target_pairs={{32,0},{64,32},{96,64},{0,96},{33,1},{65,33},{97,65},{1,97},{34,2}... | collective-permute-start | bytes 294920 | tf_op jit(solution)/shard_map/ppermute | solution.py:24
  26.3 62.6 %collective-permute-start.5 = (f32[3,2,32,128]{3,2,1,0:T(8,128)S(1)}, f32[3,2,32,128]{3,2,1,0:T(8,128)S(1)}, u32[]{:S(2)}, u32[]{:S(2)}) collective-permute-start(f32[3,2,32,128]{3,2,1,0:T(8,128)S(1)} %get-tuple-element.19), channel_id=1, source_target_pairs={{0,32},{32,64},{64,96},{96,0},{1,33},{33,65},{65,97},{97,1},{2,34}... | collective-permute-start | bytes 294920 | tf_op jit(solution)/shard_map/ppermute | solution.py:22
  26.3 35.1 %slice-start = ((s8[12582912]{0:T(1024)(128)(4,1)}), s8[4194304]{0:T(1024)(128)(4,1)S(1)}, s32[]{:S(2)}) async-start(s8[12582912]{0:T(1024)(128)(4,1)} %bitcast.62), calls=%async_computation.1 | async-start | bytes 8388608
  26.3 35.1 %slice-start.1 = ((s8[12582912]{0:T(1024)(128)(4,1)}), s8[4194304]{0:T(1024)(128)(4,1)S(1)}, s32[]{:S(2)}) async-start(s8[12582912]{0:T(1024)(128)(4,1)} %bitcast.62), calls=%async_computation.2 | async-start | bytes 8388608
  34.0 27.4 %slice-start.2 = ((s8[12582912]{0:T(1024)(128)(4,1)}), s8[4194304]{0:T(1024)(128)(4,1)S(1)}, s32[]{:S(2)}) async-start(s8[12582912]{0:T(1024)(128)(4,1)} %bitcast.62), calls=%async_computation.3 | async-start | bytes 8388608
  61.4 34.8 %copy-start = (f32[3,8,32,128]{3,2,1,0:T(8,128)S(1)}, f32[3,8,32,128]{3,2,1,0:T(8,128)}, u32[]{:S(2)}) copy-start(f32[3,8,32,128]{3,2,1,0:T(8,128)} %param.4) | copy-start | bytes 1179652
  88.9 3.5 %collective-permute-start.6 = (f32[3,12,2,128]{3,2,1,0:T(2,128)S(1)}, f32[3,12,2,128]{3,2,1,0:T(2,128)S(1)}, u32[]{:S(2)}, u32[]{:S(2)}) collective-permute-start(f32[3,12,2,128]{3,2,1,0:T(2,128)S(1)} %get-tuple-element.12), channel_id=1, source_target_pairs={{1,0},{2,1},{3,2},{4,3},{5,4},{6,5},{7,6},{8,7},{9,8},{10,9},{11,1... | collective-permute-start | bytes 110600 | tf_op jit(solution)/shard_map/ppermute | solution.py:24
  90.6 5.5 %collective-permute-start.7 = (f32[3,12,2,128]{3,2,1,0:T(2,128)S(1)}, f32[3,12,2,128]{3,2,1,0:T(2,128)S(1)}, u32[]{:S(2)}, u32[]{:S(2)}) collective-permute-start(f32[3,12,2,128]{3,2,1,0:T(2,128)S(1)} %get-tuple-element.13), channel_id=1, source_target_pairs={{0,1},{1,2},{2,3},{3,4},{4,5},{5,6},{6,7},{7,8},{8,9},{9,10},{10,1... | collective-permute-start | bytes 110600 | tf_op jit(solution)/shard_map/ppermute | solution.py:22
Sparse Core Ops, SparseCore 0:
  130.7 46.6 all-gather.3
where the time goes:
time: 228 us; the launch traced here: 226 us
  local copies, waits for them, and re-layouts  65.8 us (29%)
  waiting for transfers between devices  56.6 us (25%)
  other arithmetic  44.9 us (20%)
  matrix products  23.5 us (10%)
  between operations  14.3 us (6%)
  starting transfers between devices  10.8 us (5%)
  blocking collectives  10.6 us (5%)
    unnamed x14, local copies, waits for them, and re-layouts  64.4 us
    all_gather x1, waiting for transfers between devices, local(): pieces = lax.all_gather(local_factor[None], 'gy', axis=0, tiled=True)  46.8 us
    another operation x9, other arithmetic, upper_factor(): return jnp.linalg.cholesky(gram).T  37.2 us
    dot_general x1, matrix products, inner(): lax.dot_general(left, right, (((1,), (1,)), ((), ())), preferred_element_...  19 us
    all_gather x1, blocking collectives, local(): pieces = lax.all_gather(group_factor[None], 'gx', axis=0, tiled=True)  10.6 us
    ppermute x4, starting transfers between devices, with_halo(): lax.ppermute(tail, axis, [(i, (i + 1) % count) for i in range(count)])  5.78 us
    ppermute x4, waiting for transfers between devices, with_halo(): lax.ppermute(tail, axis, [(i, (i + 1) % count) for i in range(count)])  5.59 us
    ppermute x4, starting transfers between devices, with_halo(): lax.ppermute(head, axis, [((i + 1) % count, i) for i in range(count)])  4.94 us
  transfers between devices with their start and end apart: 9, of which 6 were waited for; matrix products, arithmetic and copies ran while one was open for 29% of the time, Pallas kernels for 0%

commit v1 on v0

--- a/solution.py
+++ b/solution.py
@@ -1,8 +1,11 @@
+import functools
 import math
 
 import jax
 import jax.numpy as jnp
 from jax import lax
+from jax.experimental import pallas as pl
+from jax.experimental.pallas import tpu as pltpu
 from jax.sharding import PartitionSpec as P
 
 TIME_STEP = 0.0002
@@ -73,32 +76,132 @@
     return -carried + VISCOSITY * (curve_x + curve_y + curve_z)
 
 
-def inner(left, right):
-    return lax.dot_general(
-        left, right, (((1,), (1,)), ((), ())), preferred_element_type=jnp.float32
-    )
+CHUNKS = (96, 96, 96, 96)
+MXU_STEP = 16
+
+
+def gram_kernel(scale, basis_ref, stored_ref, newest_ref, gram_ref, block, wide, folded, sems):
+    n_basis = basis_ref.shape[0]
+    n_stored = stored_ref.shape[0]
+    starts = [sum(CHUNKS[:q]) for q in range(len(CHUNKS))]
+
+    def issue(q):
+        span = pl.ds(starts[q], CHUNKS[q])
+
+        def send(source, column):
+            pltpu.make_async_copy(
+                source.at[span], block.at[span, pl.ds(pl.multiple_of(2 * column, 2), 2)], sems.at[q]
+            ).start()
+
+        @pl.loop(0, n_basis)
+        def _(c):
+            send(basis_ref.at[c], c)
+
+        @pl.loop(0, n_stored)
+        def _(c):
+            send(stored_ref.at[c], n_basis + c)
+
+        send(newest_ref, n_basis + n_stored)
+
+    def body(acc0, acc1):
+        accs = (acc0, acc1)
+        issue(0)
+        issue(1)
+        for q in range(len(CHUNKS)):
+            if q + 2 < len(CHUNKS):
+                issue(q + 2)
+            span = block.at[pl.ds(starts[q], CHUNKS[q])]
+            pltpu.make_async_copy(span, span, sems.at[q]).wait()
+
+            @pl.loop(0, CHUNKS[q] // MXU_STEP)
+            def _(t):
+                base = starts[q] + t * MXU_STEP
+                for u in range(MXU_STEP // 2):
+                    unit = u % 2
+                    register = (u // 2) % 2
+                    rows = jnp.concatenate([block[base + 2 * u], block[base + 2 * u + 1]], axis=1)
+                    pltpu.matmul_push_rhs(rows, register, unit, transpose=True)
+                    pltpu.matmul_acc_lhs(accs[unit], rows, load_staged_rhs=register)
+
+        total = pltpu.matmul_pop(acc0) + pltpu.matmul_pop(acc1)
+        for h in range(2):
+            wide[h] = total[:, 128 * h : 128 * (h + 1)]
+
+    pl.run_scoped(
+        body, pltpu.ACC(0)((256, 256), jnp.float32), pltpu.ACC(1)((256, 256), jnp.float32)
+    )
+    lane = lax.broadcasted_iota(jnp.int32, (128, 128), 1)
+    for h in range(2):
+        even = wide[h, pl.ds(0, 128, stride=2), :]
+        odd = wide[h, pl.ds(1, 128, stride=2), :]
+        folded[128 * h : 128 * (h + 1)] = (jnp.where(lane % 2 == 0, even, odd) * scale).T
+    gram_ref[...] = folded[pl.ds(0, 128, stride=2), :] + folded[pl.ds(1, 128, stride=2), :]
+
+
+def pair_rows(field, lead):
+    return field.reshape(*field.shape[:lead], -1, 2, field.shape[-1])
+
+
+def local_gram(basis, stored, newest, scale):
+    basis = pair_rows(basis, 1)
+    stored = pair_rows(stored, 1)
+    newest = pair_rows(newest, 0)
+    hbm = pl.BlockSpec(memory_space=pltpu.HBM)
+    return pl.pallas_call(
+        functools.partial(gram_kernel, scale),
+        out_shape=jax.ShapeDtypeStruct((128, 128), jnp.float32),
+        in_specs=[hbm, hbm, hbm],
+        out_specs=pl.BlockSpec(memory_space=pltpu.VMEM),
+        scratch_shapes=[
+            pltpu.VMEM((basis.shape[1], 256, 128), jnp.bfloat16),
+            pltpu.VMEM((2, 256, 128), jnp.float32),
+            pltpu.VMEM((256, 128), jnp.float32),
+            pltpu.SemaphoreType.DMA((len(CHUNKS),)),
+        ],
+        compiler_params=pltpu.CompilerParams(vmem_limit_bytes=40 * 2**20),
+        name="gram",
+    )(basis, stored, newest)
+
+
+def swap_cores(part, count):
+    return lax.ppermute(part, "gy", [(i, i ^ 1) for i in range(count)])
+
+
+def ring_sum(part, axis, count, stride):
+    def target(i, d):
+        place = (i // stride) % 4
+        return i + ((place + d) % 4 - place) * stride
+
+    moved = [
+        lax.ppermute(part, axis, [(i, target(i, d)) for i in range(count)]) for d in (1, 2, 3)
+    ]
+    return (part + moved[1]) + (moved[0] + moved[2])
+
+
+def total_gram(gram):
+    count = lax.axis_size("gy")
+    half = gram.shape[0] // 2
+    core = lax.axis_index("gy") % 2
+    mine = lax.dynamic_slice_in_dim(gram, core * half, half, 0)
+    other = lax.dynamic_slice_in_dim(gram, (1 - core) * half, half, 0)
+    part = mine + swap_cores(other, count)
+    part = ring_sum(part, "gy", count, 2)
+    part = ring_sum(part, "gy", count, 8)
+    part = ring_sum(part, "gx", 4, 1)
+    rest = swap_cores(part, count)
+    low = jnp.where(core == 0, part, rest)
+    high = jnp.where(core == 0, rest, part)
+    return jnp.concatenate([low, high], 0)
 
 
 def widen_once(field):
     return with_halo(field, (("gx", 1), ("gy", 2)), 2)
-
-
-def upper_factor(gram):
-    return jnp.linalg.cholesky(gram).T
-
-
-def stacked_factor(pieces):
-    gram = jnp.einsum("kij,kil->jl", pieces, pieces, precision=lax.Precision.HIGHEST)
-    return upper_factor(gram)
 
 
 def local(velocity, basis, snapshots):
     section_field = velocity + TIME_STEP * tendency(widen_once(velocity))
     advanced = 0.5 * (velocity + section_field + TIME_STEP * tendency(widen_once(section_field)))
-    newest = advanced.astype(jnp.bfloat16).reshape(1, -1)
-    block = jnp.concatenate(
-        [basis.reshape(basis.shape[0], -1), snapshots.reshape(snapshots.shape[0], -1), newest], 0
-    )
+    newest = advanced.astype(jnp.bfloat16)
     total_rows = (
         3.0
         * velocity.shape[1]
@@ -107,12 +210,8 @@
         * lax.axis_size("gy")
         * velocity.shape[3]
     )
-    local_gram = inner(block, block) * (1.0 / total_rows)
-    local_factor = upper_factor(local_gram)
-    pieces = lax.all_gather(local_factor[None], "gy", axis=0, tiled=True)
-    group_factor = stacked_factor(pieces)
-    pieces = lax.all_gather(group_factor[None], "gx", axis=0, tiled=True)
-    factor = stacked_factor(pieces)
+    gram = local_gram(basis, snapshots, newest, 1.0 / total_rows)
+    factor = jnp.linalg.cholesky(total_gram(gram)).T
     return (advanced, factor)
 
 

time: 228 us -> 111 us (0.49)
  local copies, waits for them, and re-layouts: 65.8 us -> 7.7 us
  waiting for transfers between devices: 56.6 us -> 21.5 us
  Pallas kernels: 0 us -> 26.2 us
  other arithmetic: 44.9 us -> 19.4 us
  starting transfers between devices: 10.8 us -> 34.9 us
  matrix products: 23.5 us -> 0 us
  between operations: 14.3 us -> 0.83 us
  blocking collectives: 10.6 us -> 0 us
    unnamed x14 -> x7, local copies, waits for them, and re-layouts: 64.4 us -> 6.58 us
    all_gather x1 -> x0, waiting for transfers between devices: 46.8 us -> none  [local(): pieces = lax.all_gather(local_factor[None], 'gy', axis=0, tiled=True)]
    pallas_call x0 -> x1, Pallas kernels: none -> 26.2 us  [local_gram(): pl.pallas_call(functools.partial(gram_kernel, scale), out_shape=jax.Shape...]
    another operation x9 -> x3, other arithmetic: 37.2 us -> 12.4 us  [local(): factor = jnp.linalg.cholesky(total_gram(gram)).T]
    dot_general x3 -> x0, matrix products: 23.5 us -> none  [the longest x1 19 us: inner(): lax.dot_general(left, right, (((1,), (1,)), ((), ())), preferred_element_...]
    ppermute x0 -> x11, starting transfers between devices: none -> 18.7 us  [the longest x2 10.3 us: swap_cores(): return lax.ppermute(part, 'gy', [(i, i ^ 1) for i in range(count)])]
    ppermute x0 -> x11, waiting for transfers between devices: none -> 11 us  [the longest x9 9.32 us: ring_sum(): lax.ppermute(part, axis, [(i, target(i, d)) for i in range(count)])]
    all_gather x1 -> x0, blocking collectives: 10.6 us -> none  [local(): pieces = lax.all_gather(group_factor[None], 'gx', axis=0, tiled=True)]
  transfers between devices with their start and end apart: 9 -> 19, of which waited for: 6 -> 16; matrix products, arithmetic and copies ran while one was open for 29% -> 2% of each run, Pallas kernels for 0% -> 0%
where the time goes in v1:
time: 111 us
  starting transfers between devices  34.9 us (31%)
  Pallas kernels  26.2 us (24%)
  waiting for transfers between devices  21.5 us (19%)
  other arithmetic  19.4 us (17%)
  local copies, waits for them, and re-layouts  7.7 us (7%)
    pallas_call x1, Pallas kernels, local_gram(): pl.pallas_call(functools.partial(gram_kernel, scale), out_shape=jax.Shape...  26.2 us
    another operation x3, other arithmetic, local(): factor = jnp.linalg.cholesky(total_gram(gram)).T  12.4 us
    ppermute x4, starting transfers between devices, with_halo(): lax.ppermute(head, axis, [((i + 1) % count, i) for i in range(count)])  12.4 us
    ppermute x2, starting transfers between devices, swap_cores(): return lax.ppermute(part, 'gy', [(i, i ^ 1) for i in range(count)])  10.3 us
    ppermute x9, waiting for transfers between devices, ring_sum(): lax.ppermute(part, axis, [(i, target(i, d)) for i in range(count)])  9.32 us
    ppermute x9, starting transfers between devices, ring_sum(): lax.ppermute(part, axis, [(i, target(i, d)) for i in range(count)])  8.39 us
    unnamed x7, local copies, waits for them, and re-layouts  6.58 us
    ppermute x4, waiting for transfers between devices, with_halo(): lax.ppermute(tail, axis, [(i, (i + 1) % count) for i in range(count)])  6.13 us
  transfers between devices with their start and end apart: 19, of which 16 were waited for; matrix products, arithmetic and copies ran while one was open for 2% of the time, Pallas kernels for 0%

profile of v1, /device:TPU:1, one launch (start us, length us, event | category | flops | bytes accessed | tf_op | source)
XLA Modules:
  0.0 110.6 jit_solution(12696445685624932344)
XLA Ops:
  0.6 1.0 fusion.12
  1.6 2.1 %collective-permute-start.1 = (f32[3,2,32,128]{3,2,1,0:T(8,128)S(1)}, f32[3,2,32,128]{3,2,1,0:T(8,128)S(1)}, u32[]{:S(2)}, u32[]{:S(2)}) collective-permute-start(f32[3,2,32,128]{3,2,1,0:T(8,128)S(1)} %get-tuple-element.27), channel_id=1, source_target_pairs={{0,32},{32,64},{64,96},{96,0},{1,33},{33,65},{65,97},{97,1},{2,34}... | collective-permute-start | bytes 294920 | tf_op jit(solution)/shard_map/ppermute | solution.py:25
  3.7 1.3 %collective-permute-start = (f32[3,2,32,128]{3,2,1,0:T(8,128)S(1)}, f32[3,2,32,128]{3,2,1,0:T(8,128)S(1)}, u32[]{:S(2)}, u32[]{:S(2)}) collective-permute-start(f32[3,2,32,128]{3,2,1,0:T(8,128)S(1)} %get-tuple-element.26), channel_id=1, source_target_pairs={{32,0},{64,32},{96,64},{0,96},{33,1},{65,33},{97,65},{1,97},{34,2}... | collective-permute-start | bytes 294920 | tf_op jit(solution)/shard_map/ppermute | solution.py:27
  5.1 1.1 multiply_bitcast_fusion.1
  6.1 0.1 multiply_divide_fusion.3
  6.2 0.8 collective-permute-done.1
  7.0 1.1 %constant_dynamic-update-slice_fusion.1 = (f32[3,10,32,128]{3,2,1,0:T(8,128)S(1)}, f32[3,12,32,128]{3,2,1,0:T(8,128)S(1)}, f32[3,10,32,128]{3,2,1,0:T(8,128)S(1)}) fusion(f32[3,8,32,128]{3,2,1,0:T(8,128)} %param.3, f32[3,12,32,128]{3,2,1,0:T(8,128)S(1)} %get-tuple-element.33, f32[3,10,32,128]{3,2,1,0:T(8,128)S(1)} %get-tuple-element.32), kind=kLoop, calls=%fused_computation.52 | loop fusion | bytes 1572864
  8.1 0.0 collective-permute-done
  8.2 2.0 %collective-permute-start.2 = (f32[3,12,2,128]{3,2,1,0:T(2,128)S(1)}, f32[3,12,2,128]{3,2,1,0:T(2,128)S(1)}, u32[]{:S(2)}, u32[]{:S(2)}) collective-permute-start(f32[3,12,2,128]{3,2,1,0:T(2,128)S(1)} %get-tuple-element.13), channel_id=1, source_target_pairs={{1,0},{2,1},{3,2},{4,3},{5,4},{6,5},{7,6},{8,7},{9,8},{10,9},{11,1... | collective-permute-start | bytes 110600 | tf_op jit(solution)/shard_map/ppermute | solution.py:27
  10.2 1.7 %collective-permute-start.3 = (f32[3,12,2,128]{3,2,1,0:T(2,128)S(1)}, f32[3,12,2,128]{3,2,1,0:T(2,128)S(1)}, u32[]{:S(2)}, u32[]{:S(2)}) collective-permute-start(f32[3,12,2,128]{3,2,1,0:T(2,128)S(1)} %get-tuple-element.14), channel_id=1, source_target_pairs={{0,1},{1,2},{2,3},{3,4},{4,5},{5,6},{6,7},{7,8},{8,9},{9,10},{10,1... | collective-permute-start | bytes 110600 | tf_op jit(solution)/shard_map/ppermute | solution.py:25
  11.9 1.6 %collective-permute-done.2 = f32[3,12,2,128]{3,2,1,0:T(2,128)S(1)} collective-permute-done((f32[3,12,2,128]{3,2,1,0:T(2,128)S(1)}, f32[3,12,2,128]{3,2,1,0:T(2,128)S(1)}, u32[]{:S(2)}, u32[]{:S(2)}) %collective-permute-start.2) | collective-permute-done | bytes 36896 | tf_op jit(solution)/shard_map/ppermute | solution.py:27
  13.4 2.3 %collective-permute-done.3 = f32[3,12,2,128]{3,2,1,0:T(2,128)S(1)} collective-permute-done((f32[3,12,2,128]{3,2,1,0:T(2,128)S(1)}, f32[3,12,2,128]{3,2,1,0:T(2,128)S(1)}, u32[]{:S(2)}, u32[]{:S(2)}) %collective-permute-start.3) | collective-permute-done | bytes 36896 | tf_op jit(solution)/shard_map/ppermute | solution.py:25
  15.8 2.3 %multiply_add_fusion = f32[3,8,32,128]{3,2,1,0:T(8,128)S(1)} fusion(f32[3,8,32,128]{3,2,1,0:T(8,128)} %param.3, f32[3,12,32,128]{3,2,1,0:T(8,128)S(1)} %get-tuple-element.31, f32[3,12,2,128]{3,2,1,0:T(2,128)S(1)} %collective-permute-done.3, f32[3,12,2,128]{3,2,1,0:T(2,128)S(1)} %collective-permute-done.2, f32[3,10,32,128]{3,2,1,0:T(8,128)S(1)} %get-tuple-element.25, ...), kind=kLoop, calls=%fused_computation.27 | loop fusion | flops 5210112 | bytes 3419136 | tf_op jit(solution)/shard_map/add | solution.py:202
  18.1 1.6 %collective-permute-start.4 = (f32[3,2,32,128]{3,2,1,0:T(8,128)S(1)}, f32[3,2,32,128]{3,2,1,0:T(8,128)S(1)}, u32[]{:S(2)}, u32[]{:S(2)}) collective-permute-start(f32[3,2,32,128]{3,2,1,0:T(8,128)S(1)} %get-tuple-element.19), channel_id=1, source_target_pairs={{32,0},{64,32},{96,64},{0,96},{33,1},{65,33},{97,65},{1,97},{34,2}... | collective-permute-start | bytes 294920 | tf_op jit(solution)/shard_map/ppermute | solution.py:27
  19.6 0.0 collective-permute-start.5
  19.6 2.0 %collective-permute-done.4 = f32[3,2,32,128]{3,2,1,0:T(8,128)S(1)} collective-permute-done((f32[3,2,32,128]{3,2,1,0:T(8,128)S(1)}, f32[3,2,32,128]{3,2,1,0:T(8,128)S(1)}, u32[]{:S(2)}, u32[]{:S(2)}) %collective-permute-start.4) | collective-permute-done | bytes 98336 | tf_op jit(solution)/shard_map/ppermute | solution.py:27
  21.6 2.7 %collective-permute-done.5 = f32[3,2,32,128]{3,2,1,0:T(8,128)S(1)} collective-permute-done((f32[3,2,32,128]{3,2,1,0:T(8,128)S(1)}, f32[3,2,32,128]{3,2,1,0:T(8,128)S(1)}, u32[]{:S(2)}, u32[]{:S(2)}) %collective-permute-start.5) | collective-permute-done | bytes 98336 | tf_op jit(solution)/shard_map/ppermute | solution.py:25
  24.3 7.5 %collective-permute-start.6 = (f32[3,12,2,128]{3,2,1,0:T(2,128)S(1)}, f32[3,12,2,128]{3,2,1,0:T(2,128)S(1)}, u32[]{:S(2)}, u32[]{:S(2)}) collective-permute-start(f32[3,12,2,128]{3,2,1,0:T(2,128)S(1)} %get-tuple-element.11), channel_id=1, source_target_pairs={{1,0},{2,1},{3,2},{4,3},{5,4},{6,5},{7,6},{8,7},{9,8},{10,9},{11,1... | collective-permute-start | bytes 110600 | tf_op jit(solution)/shard_map/ppermute | solution.py:27
  31.8 0.0 collective-permute-start.7
  31.9 0.8 collective-permute-done.6
  32.7 0.3 collective-permute-done.7
  33.1 0.1 pad_maximum_fusion
  33.2 2.5 %fusion.9 = (bf16[3,8,32,128]{3,2,1,0:T(8,128)(2,1)S(1)}, f32[3,8,32,128]{3,2,1,0:T(8,128)}) fusion(f32[128]{0:T(128)S(1)} %get-tuple-element.38, f32[3,8,32,128]{3,2,1,0:T(8,128)S(1)} %multiply_add_fusion, f32[128]{0:T(128)S(1)} %get-tuple-element.39, f32[128]{0:T(128)S(1)} %get-tuple-element.40, f32[8,32,128]{2,1,0:T(8,128)S(1)} %get-tuple-element.17, ...), kind=kLoop, calls=%fused_computation.71 | loop fusion | flops 5505024 | bytes 3542016 | tf_op jit(solution)/shard_map/convert_element_type | solution.py:204
  35.7 0.0 copy-start
  35.7 4.5 %copy-done = bf16[63,3,8,32,128]{4,3,2,1,0:T(8,128)(2,1)S(1)} copy-done((bf16[63,3,8,32,128]{4,3,2,1,0:T(8,128)(2,1)S(1)}, bf16[63,3,8,32,128]{4,3,2,1,0:T(8,128)(2,1)}, u32[]{:S(2)}) %copy-start) | copy-done | bytes 12386328
  40.2 26.2 %gram.1 = f32[128,128]{1,0:T(8,128)S(1)} custom-call(bf16[64,384,2,128]{3,2,1,0:T(2,128)(2,1)} %bitcast.23, bf16[63,384,2,128]{3,2,1,0:T(2,128)(2,1)S(1)} %bitcast.21, bf16[384,2,128]{2,1,0:T(2,128)(2,1)S(1)} %bitcast.22), custom_call_target="tpu_custom_call" | custom-call | tf_op jit(solution)/shard_map/gram/pallas_call | solution.py:150
  66.5 0.1 copy.10
  66.6 5.7 %collective-permute-start.8 = (f32[64,128]{0,1:T(8,128)S(1)}, f32[64,128]{0,1:T(8,128)S(1)}, u32[]{:S(2)}, u32[]{:S(2)}) collective-permute-start(f32[64,128]{0,1:T(8,128)S(1)} %copy.10), channel_id=1, source_target_pairs={{0,1},{1,0},{2,3},{3,2},{4,5},{5,4},{6,7},{7,6},{8,9},{9,8},{10,11... | collective-permute-start | bytes 98312 | tf_op jit(solution)/shard_map/ppermute | solution.py:167
  72.2 0.1 copy.9
  72.3 0.8 collective-permute-done.8
  73.1 0.1 collective-permute-start.10
  73.2 2.7 %collective-permute-start.11 = (f32[64,128]{0,1:T(8,128)S(1)}, f32[64,128]{0,1:T(8,128)S(1)}, u32[]{:S(2)}, u32[]{:S(2)}) collective-permute-start(f32[64,128]{0,1:T(8,128)S(1)} %add.233), channel_id=1, source_target_pairs={{0,6},{1,7},{2,0},{3,1},{4,2},{5,3},{6,4},{7,5},{8,14},{9,15},{10,... | collective-permute-start | bytes 98312 | tf_op jit(solution)/shard_map/ppermute | solution.py:176
  75.9 0.0 collective-permute-start.9
  75.9 1.6 %collective-permute-done.10 = f32[64,128]{0,1:T(8,128)S(1)} collective-permute-done((f32[64,128]{0,1:T(8,128)S(1)}, f32[64,128]{0,1:T(8,128)S(1)}, u32[]{:S(2)}, u32[]{:S(2)}) %collective-permute-start.10) | collective-permute-done | bytes 32800 | tf_op jit(solution)/shard_map/ppermute | solution.py:176
  77.5 0.4 collective-permute-done.11
  77.9 2.5 %collective-permute-done.9 = f32[64,128]{0,1:T(8,128)S(1)} collective-permute-done((f32[64,128]{0,1:T(8,128)S(1)}, f32[64,128]{0,1:T(8,128)S(1)}, u32[]{:S(2)}, u32[]{:S(2)}) %collective-permute-start.9) | collective-permute-done | bytes 32800 | tf_op jit(solution)/shard_map/ppermute | solution.py:176
  80.5 0.1 collective-permute-start.12
  80.6 0.1 collective-permute-start.13
  80.7 2.7 %collective-permute-start.14 = (f32[64,128]{0,1:T(8,128)S(1)}, f32[64,128]{0,1:T(8,128)S(1)}, u32[]{:S(2)}, u32[]{:S(2)}) collective-permute-start(f32[64,128]{0,1:T(8,128)S(1)} %add_add_fusion.2), channel_id=1, source_target_pairs={{0,24},{1,25},{2,26},{3,27},{4,28},{5,29},{6,30},{7,31},{8,0},{9,1... | collective-permute-start | bytes 98312 | tf_op jit(solution)/shard_map/ppermute | solution.py:176
  83.4 2.0 %collective-permute-done.12 = f32[64,128]{0,1:T(8,128)S(1)} collective-permute-done((f32[64,128]{0,1:T(8,128)S(1)}, f32[64,128]{0,1:T(8,128)S(1)}, u32[]{:S(2)}, u32[]{:S(2)}) %collective-permute-start.12) | collective-permute-done | bytes 32800 | tf_op jit(solution)/shard_map/ppermute | solution.py:176
  85.3 0.4 collective-permute-done.13
  85.7 0.0 collective-permute-done.14
  85.7 0.1 collective-permute-start.15
  85.8 0.3 collective-permute-start.16
  86.1 2.5 %collective-permute-start.17 = (f32[64,128]{0,1:T(8,128)S(1)}, f32[64,128]{0,1:T(8,128)S(1)}, u32[]{:S(2)}, u32[]{:S(2)}) collective-permute-start(f32[64,128]{0,1:T(8,128)S(1)} %add_add_fusion.1), channel_id=1, source_target_pairs={{0,96},{32,0},{64,32},{96,64},{1,97},{33,1},{65,33},{97,65},{2,98}... | collective-permute-start | bytes 98312 | tf_op jit(solution)/shard_map/ppermute | solution.py:176
  88.6 2.0 %collective-permute-done.15 = f32[64,128]{0,1:T(8,128)S(1)} collective-permute-done((f32[64,128]{0,1:T(8,128)S(1)}, f32[64,128]{0,1:T(8,128)S(1)}, u32[]{:S(2)}, u32[]{:S(2)}) %collective-permute-start.15) | collective-permute-done | bytes 32800 | tf_op jit(solution)/shard_map/ppermute | solution.py:176
  90.5 0.4 collective-permute-done.16
  90.9 0.0 collective-permute-done.17
  90.9 4.6 %collective-permute-start.18 = (f32[64,128]{0,1:T(8,128)S(1)}, f32[64,128]{0,1:T(8,128)S(1)}, u32[]{:S(2)}, u32[]{:S(2)}) collective-permute-start(f32[64,128]{0,1:T(8,128)S(1)} %add_add_fusion), channel_id=1, source_target_pairs={{0,1},{1,0},{2,3},{3,2},{4,5},{5,4},{6,7},{7,6},{8,9},{9,8},{10,11... | collective-permute-start | bytes 98312 | tf_op jit(solution)/shard_map/ppermute | solution.py:167
  95.6 0.9 collective-permute-done.18
  96.5 0.1 pad_maximum_fusion.5
  96.6 0.1 copy.7
  96.7 0.1 fusion.8
  96.8 11.7 %cholesky.18 = f32[128,128]{1,0:T(8,128)S(1)} custom-call(f32[128,128]{1,0:T(8,128)S(1)} %fusion.8), custom_call_target="Cholesky" | custom-call | tf_op jit(solution)/shard_map/jit(cholesky)/cholesky | solution.py:214
  108.5 0.6 compare_reduce_fusion
  109.2 0.7 select_bitcast_fusion
  109.8 0.7 copy.8
  (15 shorter events, 0.3 us)
Async XLA Ops:
  1.6 5.4 %collective-permute-start.1 = (f32[3,2,32,128]{3,2,1,0:T(8,128)S(1)}, f32[3,2,32,128]{3,2,1,0:T(8,128)S(1)}, u32[]{:S(2)}, u32[]{:S(2)}) collective-permute-start(f32[3,2,32,128]{3,2,1,0:T(8,128)S(1)} %get-tuple-element.27), channel_id=1, source_target_pairs={{0,32},{32,64},{64,96},{96,0},{1,33},{33,65},{65,97},{97,1},{2,34}... | collective-permute-start | bytes 294920 | tf_op jit(solution)/shard_map/ppermute | solution.py:25
  3.7 4.4 %collective-permute-start = (f32[3,2,32,128]{3,2,1,0:T(8,128)S(1)}, f32[3,2,32,128]{3,2,1,0:T(8,128)S(1)}, u32[]{:S(2)}, u32[]{:S(2)}) collective-permute-start(f32[3,2,32,128]{3,2,1,0:T(8,128)S(1)} %get-tuple-element.26), channel_id=1, source_target_pairs={{32,0},{64,32},{96,64},{0,96},{33,1},{65,33},{97,65},{1,97},{34,2}... | collective-permute-start | bytes 294920 | tf_op jit(solution)/shard_map/ppermute | solution.py:27
  8.2 5.3 %collective-permute-start.2 = (f32[3,12,2,128]{3,2,1,0:T(2,128)S(1)}, f32[3,12,2,128]{3,2,1,0:T(2,128)S(1)}, u32[]{:S(2)}, u32[]{:S(2)}) collective-permute-start(f32[3,12,2,128]{3,2,1,0:T(2,128)S(1)} %get-tuple-element.13), channel_id=1, source_target_pairs={{1,0},{2,1},{3,2},{4,3},{5,4},{6,5},{7,6},{8,7},{9,8},{10,9},{11,1... | collective-permute-start | bytes 110600 | tf_op jit(solution)/shard_map/ppermute | solution.py:27
  10.2 5.6 %collective-permute-start.3 = (f32[3,12,2,128]{3,2,1,0:T(2,128)S(1)}, f32[3,12,2,128]{3,2,1,0:T(2,128)S(1)}, u32[]{:S(2)}, u32[]{:S(2)}) collective-permute-start(f32[3,12,2,128]{3,2,1,0:T(2,128)S(1)} %get-tuple-element.14), channel_id=1, source_target_pairs={{0,1},{1,2},{2,3},{3,4},{4,5},{5,6},{6,7},{7,8},{8,9},{9,10},{10,1... | collective-permute-start | bytes 110600 | tf_op jit(solution)/shard_map/ppermute | solution.py:25
  18.1 3.5 %collective-permute-start.4 = (f32[3,2,32,128]{3,2,1,0:T(8,128)S(1)}, f32[3,2,32,128]{3,2,1,0:T(8,128)S(1)}, u32[]{:S(2)}, u32[]{:S(2)}) collective-permute-start(f32[3,2,32,128]{3,2,1,0:T(8,128)S(1)} %get-tuple-element.19), channel_id=1, source_target_pairs={{32,0},{64,32},{96,64},{0,96},{33,1},{65,33},{97,65},{1,97},{34,2}... | collective-permute-start | bytes 294920 | tf_op jit(solution)/shard_map/ppermute | solution.py:27
  19.6 4.7 %collective-permute-start.5 = (f32[3,2,32,128]{3,2,1,0:T(8,128)S(1)}, f32[3,2,32,128]{3,2,1,0:T(8,128)S(1)}, u32[]{:S(2)}, u32[]{:S(2)}) collective-permute-start(f32[3,2,32,128]{3,2,1,0:T(8,128)S(1)} %get-tuple-element.18), channel_id=1, source_target_pairs={{0,32},{32,64},{64,96},{96,0},{1,33},{33,65},{65,97},{97,1},{2,34}... | collective-permute-start | bytes 294920 | tf_op jit(solution)/shard_map/ppermute | solution.py:25
  24.3 8.4 %collective-permute-start.6 = (f32[3,12,2,128]{3,2,1,0:T(2,128)S(1)}, f32[3,12,2,128]{3,2,1,0:T(2,128)S(1)}, u32[]{:S(2)}, u32[]{:S(2)}) collective-permute-start(f32[3,12,2,128]{3,2,1,0:T(2,128)S(1)} %get-tuple-element.11), channel_id=1, source_target_pairs={{1,0},{2,1},{3,2},{4,3},{5,4},{6,5},{7,6},{8,7},{9,8},{10,9},{11,1... | collective-permute-start | bytes 110600 | tf_op jit(solution)/shard_map/ppermute | solution.py:27
  31.8 1.2 %collective-permute-start.7 = (f32[3,12,2,128]{3,2,1,0:T(2,128)S(1)}, f32[3,12,2,128]{3,2,1,0:T(2,128)S(1)}, u32[]{:S(2)}, u32[]{:S(2)}) collective-permute-start(f32[3,12,2,128]{3,2,1,0:T(2,128)S(1)} %get-tuple-element.12), channel_id=1, source_target_pairs={{0,1},{1,2},{2,3},{3,4},{4,5},{5,6},{6,7},{7,8},{8,9},{9,10},{10,1... | collective-permute-start | bytes 110600 | tf_op jit(solution)/shard_map/ppermute | solution.py:25
  35.7 4.5 %copy-start = (bf16[63,3,8,32,128]{4,3,2,1,0:T(8,128)(2,1)S(1)}, bf16[63,3,8,32,128]{4,3,2,1,0:T(8,128)(2,1)}, u32[]{:S(2)}) copy-start(bf16[63,3,8,32,128]{4,3,2,1,0:T(8,128)(2,1)} %param.5) | copy-start | bytes 37158916
  66.6 6.6 %collective-permute-start.8 = (f32[64,128]{0,1:T(8,128)S(1)}, f32[64,128]{0,1:T(8,128)S(1)}, u32[]{:S(2)}, u32[]{:S(2)}) collective-permute-start(f32[64,128]{0,1:T(8,128)S(1)} %copy.10), channel_id=1, source_target_pairs={{0,1},{1,0},{2,3},{3,2},{4,5},{5,4},{6,7},{7,6},{8,9},{9,8},{10,11... | collective-permute-start | bytes 98312 | tf_op jit(solution)/shard_map/ppermute | solution.py:167
  73.1 4.4 %collective-permute-start.10 = (f32[64,128]{0,1:T(8,128)S(1)}, f32[64,128]{0,1:T(8,128)S(1)}, u32[]{:S(2)}, u32[]{:S(2)}) collective-permute-start(f32[64,128]{0,1:T(8,128)S(1)} %add.233), channel_id=1, source_target_pairs={{0,2},{1,3},{2,4},{3,5},{4,6},{5,7},{6,0},{7,1},{8,10},{9,11},{10,... | collective-permute-start | bytes 98312 | tf_op jit(solution)/shard_map/ppermute | solution.py:176
  73.2 4.7 %collective-permute-start.11 = (f32[64,128]{0,1:T(8,128)S(1)}, f32[64,128]{0,1:T(8,128)S(1)}, u32[]{:S(2)}, u32[]{:S(2)}) collective-permute-start(f32[64,128]{0,1:T(8,128)S(1)} %add.233), channel_id=1, source_target_pairs={{0,6},{1,7},{2,0},{3,1},{4,2},{5,3},{6,4},{7,5},{8,14},{9,15},{10,... | collective-permute-start | bytes 98312 | tf_op jit(solution)/shard_map/ppermute | solution.py:176
  75.9 4.6 %collective-permute-start.9 = (f32[64,128]{0,1:T(8,128)S(1)}, f32[64,128]{0,1:T(8,128)S(1)}, u32[]{:S(2)}, u32[]{:S(2)}) collective-permute-start(f32[64,128]{0,1:T(8,128)S(1)} %add.233), channel_id=1, source_target_pairs={{0,4},{1,5},{2,6},{3,7},{4,0},{5,1},{6,2},{7,3},{8,12},{9,13},{10,... | collective-permute-start | bytes 98312 | tf_op jit(solution)/shard_map/ppermute | solution.py:176
  80.5 4.8 %collective-permute-start.12 = (f32[64,128]{0,1:T(8,128)S(1)}, f32[64,128]{0,1:T(8,128)S(1)}, u32[]{:S(2)}, u32[]{:S(2)}) collective-permute-start(f32[64,128]{0,1:T(8,128)S(1)} %add_add_fusion.2), channel_id=1, source_target_pairs={{0,16},{1,17},{2,18},{3,19},{4,20},{5,21},{6,22},{7,23},{8,24},{9,... | collective-permute-start | bytes 98312 | tf_op jit(solution)/shard_map/ppermute | solution.py:176
  80.6 5.1 %collective-permute-start.13 = (f32[64,128]{0,1:T(8,128)S(1)}, f32[64,128]{0,1:T(8,128)S(1)}, u32[]{:S(2)}, u32[]{:S(2)}) collective-permute-start(f32[64,128]{0,1:T(8,128)S(1)} %add_add_fusion.2), channel_id=1, source_target_pairs={{0,8},{1,9},{2,10},{3,11},{4,12},{5,13},{6,14},{7,15},{8,16},{9,17... | collective-permute-start | bytes 98312 | tf_op jit(solution)/shard_map/ppermute | solution.py:176
  80.7 5.0 %collective-permute-start.14 = (f32[64,128]{0,1:T(8,128)S(1)}, f32[64,128]{0,1:T(8,128)S(1)}, u32[]{:S(2)}, u32[]{:S(2)}) collective-permute-start(f32[64,128]{0,1:T(8,128)S(1)} %add_add_fusion.2), channel_id=1, source_target_pairs={{0,24},{1,25},{2,26},{3,27},{4,28},{5,29},{6,30},{7,31},{8,0},{9,1... | collective-permute-start | bytes 98312 | tf_op jit(solution)/shard_map/ppermute | solution.py:176
  85.7 4.8 %collective-permute-start.15 = (f32[64,128]{0,1:T(8,128)S(1)}, f32[64,128]{0,1:T(8,128)S(1)}, u32[]{:S(2)}, u32[]{:S(2)}) collective-permute-start(f32[64,128]{0,1:T(8,128)S(1)} %add_add_fusion.1), channel_id=1, source_target_pairs={{0,64},{32,96},{64,0},{96,32},{1,65},{33,97},{65,1},{97,33},{2,66}... | collective-permute-start | bytes 98312 | tf_op jit(solution)/shard_map/ppermute | solution.py:176
  85.8 5.1 %collective-permute-start.16 = (f32[64,128]{0,1:T(8,128)S(1)}, f32[64,128]{0,1:T(8,128)S(1)}, u32[]{:S(2)}, u32[]{:S(2)}) collective-permute-start(f32[64,128]{0,1:T(8,128)S(1)} %add_add_fusion.1), channel_id=1, source_target_pairs={{0,32},{32,64},{64,96},{96,0},{1,33},{33,65},{65,97},{97,1},{2,34}... | collective-permute-start | bytes 98312 | tf_op jit(solution)/shard_map/ppermute | solution.py:176
  86.1 4.8 %collective-permute-start.17 = (f32[64,128]{0,1:T(8,128)S(1)}, f32[64,128]{0,1:T(8,128)S(1)}, u32[]{:S(2)}, u32[]{:S(2)}) collective-permute-start(f32[64,128]{0,1:T(8,128)S(1)} %add_add_fusion.1), channel_id=1, source_target_pairs={{0,96},{32,0},{64,32},{96,64},{1,97},{33,1},{65,33},{97,65},{2,98}... | collective-permute-start | bytes 98312 | tf_op jit(solution)/shard_map/ppermute | solution.py:176
  90.9 5.5 %collective-permute-start.18 = (f32[64,128]{0,1:T(8,128)S(1)}, f32[64,128]{0,1:T(8,128)S(1)}, u32[]{:S(2)}, u32[]{:S(2)}) collective-permute-start(f32[64,128]{0,1:T(8,128)S(1)} %add_add_fusion), channel_id=1, source_target_pairs={{0,1},{1,0},{2,3},{3,2},{4,5},{5,4},{6,7},{7,6},{8,9},{9,8},{10,11... | collective-permute-start | bytes 98312 | tf_op jit(solution)/shard_map/ppermute | solution.py:167

commit v2 on v1

v2 whole, which is shorter than its diff:
```python
import functools
import math

import jax
import jax.numpy as jnp
from jax import lax
from jax.experimental import pallas as pl
from jax.experimental.pallas import tpu as pltpu
from jax.sharding import PartitionSpec as P

TIME_STEP = 0.0002
VISCOSITY = 0.005
STEP_X = 0.0123
STEP_Z = 0.0092
STRETCH = 2.0


def wall_weights(points):
    positions = jnp.arange(points + 2, dtype=jnp.float32)
    nodes = -jnp.tanh(STRETCH * (1.0 - 2.0 * positions / (points + 1))) / math.tanh(STRETCH)
    below = nodes[1:-1] - nodes[:-2]
    above = nodes[2:] - nodes[1:-1]
    spread = above * below * (above + below)
    return (
        below * below / spread,
        -(above * above) / spread,
        (above * above - below * below) / spread,
        2.0 * below / spread,
        -2.0 * (above + below) / spread,
        2.0 * above / spread,
    )


def tendency(field, place, first, count, weights):
    def rows(c, dx, dz):
        return field[c, place + dx, pl.ds(first + dz, count), :]

    centers = [rows(c, 0, 0) for c in range(3)]
    lanes = centers[0].shape[1]
    along_x = centers[0] * (1.0 / (12.0 * STEP_X))
    along_z = centers[2] * (1.0 / (12.0 * STEP_Z))
    results = []
    for c in range(3):
        center = centers[c]
        x2, x1, x_1, x_2 = (rows(c, d, 0) for d in (2, 1, -1, -2))
        z2, z1, z_1, z_2 = (rows(c, 0, d) for d in (2, 1, -1, -2))
        upper = pltpu.roll(center, lanes - 1, 1)
        lower = pltpu.roll(center, 1, 1)
        slope_x = 8.0 * (x1 - x_1) - (x2 - x_2)
        slope_z = 8.0 * (z1 - z_1) - (z2 - z_2)
        slope_y = weights[0] * upper + weights[1] * lower + weights[2] * center
        curve_x = 16.0 * (x1 + x_1) - (x2 + x_2) - 30.0 * center
        curve_z = 16.0 * (z1 + z_1) - (z2 + z_2) - 30.0 * center
        curve_y = weights[3] * upper + weights[4] * center + weights[5] * lower
        carried = along_x * slope_x + centers[1] * slope_y + along_z * slope_z
        spread = (
            curve_x * (VISCOSITY / (12.0 * STEP_X * STEP_X))
            + curve_z * (VISCOSITY / (12.0 * STEP_Z * STEP_Z))
            + curve_y
        )
        results.append((center, spread - carried))
    return results


CHUNKS = (160, 128, 96)
MXU_STEP = 32


def step_kernel(
    scale,
    velocity_ref,
    left_ref,
    right_ref,
    behind_ref,
    ahead_ref,
    weights_ref,
    basis_ref,
    stored_ref,
    advanced_ref,
    gram_ref,
    block,
    wide,
    folded,
    field,
    section,
    advanced,
    sems,
    halo_sems,
    out_sem,
):
    n_basis = basis_ref.shape[0]
    n_stored = stored_ref.shape[0]
    length_x, length_z = velocity_ref.shape[1:3]
    starts = [sum(CHUNKS[:q]) for q in range(len(CHUNKS))]

    halos = [
        pltpu.make_async_copy(source, target, halo_sems.at[i])
        for i, (source, target) in enumerate(
            (
                (velocity_ref, field.at[:, pl.ds(4, length_x), pl.ds(4, length_z)]),
                (left_ref, field.at[:, pl.ds(0, 4), pl.ds(4, length_z)]),
                (right_ref, field.at[:, pl.ds(4 + length_x, 4), pl.ds(4, length_z)]),
                (behind_ref, field.at[:, pl.ds(2, 4 + length_x), pl.ds(0, 4)]),
                (ahead_ref, field.at[:, pl.ds(2, 4 + length_x), pl.ds(4 + length_z, 4)]),
            )
        )
    ]
    for halo in halos:
        halo.start()

    def issue(q):
        span = pl.ds(starts[q], CHUNKS[q])

        def send(source, column):
            pltpu.make_async_copy(
                source.at[span], block.at[span, pl.ds(pl.multiple_of(2 * column, 2), 2)], sems.at[q]
            ).start()

        def from_basis(c, carry):
            send(basis_ref.at[c], c)
            return carry

        def from_stored(c, carry):
            send(stored_ref.at[c], n_basis + c)
            return carry

        lax.fori_loop(0, n_basis, from_basis, 0, unroll=8)
        lax.fori_loop(0, n_stored, from_stored, 0, unroll=9)

    for q in range(len(CHUNKS)):
        issue(q)
    for halo in halos:
        halo.wait()

    weights = [weights_ref[i : i + 1, :] for i in range(6)]

    @pl.loop(0, length_x + 4)
    def _(x):
        for c, (center, change) in enumerate(tendency(field, x + 2, 2, length_z + 8, weights)):
            section[c, x, pl.ds(0, length_z + 8), :] = center + TIME_STEP * change

    last = 2 * (n_basis + n_stored)

    @pl.loop(0, length_x)
    def _(x):
        for c, (center, change) in enumerate(tendency(section, x + 2, 2, length_z, weights)):
            begin = field[c, x + 4, pl.ds(4, length_z), :]
            end = 0.5 * (begin + center + TIME_STEP * change)
            advanced[c, x] = end
            rounded = end.astype(jnp.bfloat16)
            pair = (c * length_x + x) * (length_z // 2)
            for j in range(length_z // 2):
                block[pair + j, last : last + 2, :] = rounded[2 * j : 2 * j + 2, :]

    leave = pltpu.make_async_copy(advanced, advanced_ref, out_sem.at[0])
    leave.start()

    def body(acc0, acc1):
        accs = (acc0, acc1)
        for q in range(len(CHUNKS)):
            arrived = block.at[pl.ds(starts[q], CHUNKS[q]), pl.ds(0, last)]
            pltpu.make_async_copy(arrived, arrived, sems.at[q]).wait()

            @pl.loop(0, CHUNKS[q] // MXU_STEP)
            def _(t):
                base = starts[q] + t * MXU_STEP
                for u in range(MXU_STEP // 2):
                    unit = u % 2
                    register = (u // 2) % 2
                    rows = jnp.concatenate([block[base + 2 * u], block[base + 2 * u + 1]], axis=1)
                    pltpu.matmul_push_rhs(rows, register, unit, transpose=True)
                    pltpu.matmul_acc_lhs(accs[unit], rows, load_staged_rhs=register)

        total = pltpu.matmul_pop(acc0) + pltpu.matmul_pop(acc1)
        for h in range(2):
            wide[h] = total[:, 128 * h : 128 * (h + 1)]

    pl.run_scoped(
        body, pltpu.ACC(0)((256, 256), jnp.float32), pltpu.ACC(1)((256, 256), jnp.float32)
    )
    lane = lax.broadcasted_iota(jnp.int32, (128, 128), 1)
    for h in range(2):
        even = wide[h, pl.ds(0, 128, stride=2), :]
        odd = wide[h, pl.ds(1, 128, stride=2), :]
        folded[128 * h : 128 * (h + 1)] = (jnp.where(lane % 2 == 0, even, odd) * scale).T
    gram_ref[...] = folded[pl.ds(0, 128, stride=2), :] + folded[pl.ds(1, 128, stride=2), :]
    leave.wait()


def pair_rows(fields):
    return fields.reshape(fields.shape[0], -1, 2, fields.shape[-1])


def step_and_gram(velocity, halos, weights, basis, stored, scale):
    basis = pair_rows(basis)
    stored = pair_rows(stored)
    length_x, length_z, lanes = velocity.shape[1:]
    hbm = pl.BlockSpec(memory_space=pltpu.HBM)
    free = pl.BlockSpec(memory_space=pl.ANY)
    vmem = pl.BlockSpec(memory_space=pltpu.VMEM)
    return pl.pallas_call(
        functools.partial(step_kernel, scale),
        out_shape=(
            jax.ShapeDtypeStruct(velocity.shape, jnp.float32),
            jax.ShapeDtypeStruct((128, 128), jnp.float32),
        ),
        in_specs=[free, free, free, free, free, vmem, hbm, hbm],
        out_specs=(hbm, vmem),
        scratch_shapes=[
            pltpu.VMEM((basis.shape[1], 256, lanes), jnp.bfloat16),
            pltpu.VMEM((2, 256, 128), jnp.float32),
            pltpu.VMEM((256, 128), jnp.float32),
            pltpu.VMEM((3, length_x + 8, length_z + 16, lanes), jnp.float32),
            pltpu.VMEM((3, length_x + 4, length_z + 8, lanes), jnp.float32),
            pltpu.VMEM(velocity.shape, jnp.float32),
            pltpu.SemaphoreType.DMA((len(CHUNKS),)),
            pltpu.SemaphoreType.DMA((5,)),
            pltpu.SemaphoreType.DMA((1,)),
        ],
        compiler_params=pltpu.CompilerParams(vmem_limit_bytes=60 * 2**20),
        name="step_gram",
    )(velocity, *halos, weights, basis, stored)


def shift(part, axis, step):
    count = lax.axis_size(axis)
    return lax.ppermute(part, axis, [(i, (i + step) % count) for i in range(count)])


def exchange(velocity):
    left = shift(velocity[:, -4:], "gx", 1)
    right = shift(velocity[:, :4], "gx", -1)
    wide = jnp.concatenate([left[:, 2:], velocity, right[:, :2]], axis=1)
    behind = shift(wide[:, :, -4:], "gy", 1)
    ahead = shift(wide[:, :, :4], "gy", -1)
    return left, right, behind, ahead


def wall_rows(points):
    up, down, here, curve_down, curve_here, curve_up = wall_weights(points)
    lane = jnp.arange(points)
    has_up = lane < points - 1
    has_down = lane > 0
    return jnp.stack(
        [
            jnp.where(has_up, up, 0.0),
            jnp.where(has_down, down, 0.0),
            here,
            VISCOSITY * jnp.where(has_up, curve_down, 0.0),
            VISCOSITY * curve_here,
            VISCOSITY * jnp.where(has_down, curve_up, 0.0),
            jnp.zeros_like(here),
            jnp.zeros_like(here),
        ]
    )


def swap_cores(part, count):
    return lax.ppermute(part, "gy", [(i, i ^ 1) for i in range(count)])


def ring_sum(part, axis, count, stride):
    def target(i, d):
        place = (i // stride) % 4
        return i + ((place + d) % 4 - place) * stride

    moved = [
        lax.ppermute(part, axis, [(i, target(i, d)) for i in range(count)]) for d in (1, 2, 3)
    ]
    return (part + moved[1]) + (moved[0] + moved[2])


def total_gram(gram):
    count = lax.axis_size("gy")
    half = gram.shape[0] // 2
    core = lax.axis_index("gy") % 2
    mine = lax.dynamic_slice_in_dim(gram, core * half, half, 0)
    other = lax.dynamic_slice_in_dim(gram, (1 - core) * half, half, 0)
    part = mine + swap_cores(other, count)
    part = ring_sum(part, "gy", count, 2)
    part = ring_sum(part, "gy", count, 8)
    part = ring_sum(part, "gx", 4, 1)
    rest = swap_cores(part, count)
    low = jnp.where(core == 0, part, rest)
    high = jnp.where(core == 0, rest, part)
    return jnp.concatenate([low, high], 0)


def local(velocity, basis, snapshots):
    total_rows = (
        3.0
        * velocity.shape[1]
        * lax.axis_size("gx")
        * velocity.shape[2]
        * lax.axis_size("gy")
        * velocity.shape[3]
    )
    halos = exchange(velocity)
    weights = wall_rows(velocity.shape[3])
    advanced, gram = step_and_gram(velocity, halos, weights, basis, snapshots, 1.0 / total_rows)
    factor = jnp.linalg.cholesky(total_gram(gram)).T
    return (advanced, factor)


def solution(mesh):
    return jax.shard_map(
        local,
        mesh=mesh,
        in_specs=(
            P(None, "gx", "gy", None),
            P(None, None, "gx", "gy", None),
            P(None, None, "gx", "gy", None),
        ),
        out_specs=(P(None, "gx", "gy", None), P()),
        check_vma=False,
    )
```

time: 111 us -> 78.8 us (0.71)
  Pallas kernels: 26.2 us -> 13.7 us
  starting transfers between devices: 34.9 us -> 25.3 us
  other arithmetic: 19.4 us -> 14.5 us
  local copies, waits for them, and re-layouts: 7.7 us -> 4.14 us
  waiting for transfers between devices: 21.5 us -> 20.1 us
    pallas_call x1, Pallas kernels: 26.2 us -> 13.7 us  [step_and_gram(): pl.pallas_call(functools.partial(step_kernel, scale), out_shape=(jax.Shap...]
    ppermute x8 -> x4, starting transfers between devices: 16.2 us -> 6.85 us  [shift(): lax.ppermute(part, axis, [(i, (i + step) % count) for i in range(count)])]
    unnamed x7 -> x9, local copies, waits for them, and re-layouts: 6.58 us -> 1.36 us
    ppermute x2, starting transfers between devices: 10.3 us -> 6.3 us  [swap_cores(): return lax.ppermute(part, 'gy', [(i, i ^ 1) for i in range(count)])]
    ppermute x9, starting transfers between devices: 8.39 us -> 12.1 us  [ring_sum(): lax.ppermute(part, axis, [(i, target(i, d)) for i in range(count)])]
    ppermute x8 -> x4, waiting for transfers between devices: 10.5 us -> 7.48 us  [shift(): lax.ppermute(part, axis, [(i, (i + step) % count) for i in range(count)])]
    convert_element_type x1 -> x0, other arithmetic: 2.53 us -> none  [local(): newest = advanced.astype(jnp.bfloat16)]
    add x1 -> x0, other arithmetic: 2.27 us -> none  [local(): section_field = velocity + TIME_STEP * tendency(widen_once(velocity))]
  transfers between devices with their start and end apart: 19 -> 15, of which waited for: 16 -> 12; matrix products, arithmetic and copies ran while one was open for 2% -> 1% of each run, Pallas kernels for 0% -> 0%
where the time goes in v2:
time: 78.8 us; the launch traced here: 78.6 us
  starting transfers between devices  25.3 us (32%)
  waiting for transfers between devices  20.1 us (26%)
  other arithmetic  14.5 us (18%)
  Pallas kernels  13.7 us (17%)
  local copies, waits for them, and re-layouts  4.14 us (5%)
  between operations  0.79 us (1%)
    pallas_call x1, Pallas kernels, step_and_gram(): pl.pallas_call(functools.partial(step_kernel, scale), out_shape=(jax.Shap...  13.7 us
    another operation x3, other arithmetic, local(): factor = jnp.linalg.cholesky(total_gram(gram)).T  12.4 us
    ppermute x9, starting transfers between devices, ring_sum(): lax.ppermute(part, axis, [(i, target(i, d)) for i in range(count)])  12.1 us
    ppermute x9, waiting for transfers between devices, ring_sum(): lax.ppermute(part, axis, [(i, target(i, d)) for i in range(count)])  10.8 us
    ppermute x4, waiting for transfers between devices, shift(): lax.ppermute(part, axis, [(i, (i + step) % count) for i in range(count)])  7.48 us
    ppermute x4, starting transfers between devices, shift(): lax.ppermute(part, axis, [(i, (i + step) % count) for i in range(count)])  6.85 us
    ppermute x2, starting transfers between devices, swap_cores(): return lax.ppermute(part, 'gy', [(i, i ^ 1) for i in range(count)])  6.3 us
    ppermute x2, waiting for transfers between devices, swap_cores(): return lax.ppermute(part, 'gy', [(i, i ^ 1) for i in range(count)])  1.8 us
  transfers between devices with their start and end apart: 15, of which 12 were waited for; matrix products, arithmetic and copies ran while one was open for 1% of the time, Pallas kernels for 0%

profile of v2, /device:TPU:1, one launch (start us, length us, event | category | flops | bytes accessed | tf_op | source)
XLA Modules:
  0.0 78.6 jit_solution(5848250686174656132)
XLA Ops:
  0.6 1.1 %fusion.8 = (f32[3,4,32,128]{3,2,1,0:T(8,128)S(1)}, f32[3,4,32,128]{3,2,1,0:T(8,128)S(1)}) fusion(f32[3,8,32,128]{3,2,1,0:T(8,128)} %velocity_ref.1), kind=kLoop, calls=%fused_computation.36 | loop fusion | bytes 786432 | tf_op jit(solution)/shard_map/slice | solution.py:232
  1.7 2.1 %collective-permute-start = (f32[3,4,32,128]{3,2,1,0:T(8,128)S(1)}, f32[3,4,32,128]{3,2,1,0:T(8,128)S(1)}, u32[]{:S(2)}, u32[]{:S(2)}) collective-permute-start(f32[3,4,32,128]{3,2,1,0:T(8,128)S(1)} %get-tuple-element.14), channel_id=1, source_target_pairs={{0,32},{32,64},{64,96},{96,0},{1,33},{33,65},{65,97},{97,1},{2,34}... | collective-permute-start | bytes 589832 | tf_op jit(solution)/shard_map/ppermute | solution.py:227
  3.8 1.3 %collective-permute-start.1 = (f32[3,4,32,128]{3,2,1,0:T(8,128)S(1)}, f32[3,4,32,128]{3,2,1,0:T(8,128)S(1)}, u32[]{:S(2)}, u32[]{:S(2)}) collective-permute-start(f32[3,4,32,128]{3,2,1,0:T(8,128)S(1)} %get-tuple-element.13), channel_id=1, source_target_pairs={{0,96},{32,0},{64,32},{96,64},{1,97},{33,1},{65,33},{97,65},{2,98}... | collective-permute-start | bytes 589832 | tf_op jit(solution)/shard_map/ppermute | solution.py:227
  5.2 0.1 fusion.6
  5.2 4.1 %collective-permute-done.1.right_ref = f32[3,4,32,128]{3,2,1,0:T(8,128)S(1)} collective-permute-done((f32[3,4,32,128]{3,2,1,0:T(8,128)S(1)}, f32[3,4,32,128]{3,2,1,0:T(8,128)S(1)}, u32[]{:S(2)}, u32[]{:S(2)}) %collective-permute-start.1) | collective-permute-done | bytes 196640 | tf_op jit(solution)/shard_map/ppermute | solution.py:227
  9.3 0.0 copy-start.1
  9.3 0.0 collective-permute-done.left_ref
  9.3 0.0 copy-start
  9.3 1.1 %pad_maximum_fusion = (f32[3,12,4,128]{3,2,1,0:T(4,128)S(1)}, f32[3,12,4,128]{3,2,1,0:T(4,128)S(1)}) fusion(f32[3,2,32,128]{3,2,1,0:T(8,128)S(1)} %slice.74, f32[3,8,32,128]{3,2,1,0:T(8,128)} %velocity_ref.1, f32[3,2,32,128]{3,2,1,0:T(8,128)S(1)} %slice.73), kind=kLoop, calls=%fused_computation | loop fusion | flops 73728 | bytes 737280 | tf_op jit(solution)/shard_map/concatenate | solution.py:233
  10.4 3.4 %collective-permute-start.2 = (f32[3,12,4,128]{3,2,1,0:T(4,128)S(1)}, f32[3,12,4,128]{3,2,1,0:T(4,128)S(1)}, u32[]{:S(2)}, u32[]{:S(2)}) collective-permute-start(f32[3,12,4,128]{3,2,1,0:T(4,128)S(1)} %get-tuple-element.12), channel_id=1, source_target_pairs={{0,1},{1,2},{2,3},{3,4},{4,5},{5,6},{6,7},{7,8},{8,9},{9,10},{10,1... | collective-permute-start | bytes 221192 | tf_op jit(solution)/shard_map/ppermute | solution.py:227
  13.8 0.0 collective-permute-start.3
  13.9 0.6 stack.31.weights_ref
  14.5 0.8 collective-permute-done.2.behind_ref
  15.2 0.0 copy-start.2
  15.2 2.7 %collective-permute-done.3.ahead_ref = f32[3,12,4,128]{3,2,1,0:T(4,128)S(1)} collective-permute-done((f32[3,12,4,128]{3,2,1,0:T(4,128)S(1)}, f32[3,12,4,128]{3,2,1,0:T(4,128)S(1)}, u32[]{:S(2)}, u32[]{:S(2)}) %collective-permute-start.3) | collective-permute-done | bytes 73760 | tf_op jit(solution)/shard_map/ppermute | solution.py:227
  17.9 0.0 copy-start.3
  17.9 0.0 copy-done.1
  17.9 0.0 copy-done
  17.9 0.0 copy-done.2
  17.9 0.6 copy-done.3
  18.5 13.7 %step_gram.1 = (f32[3,8,32,128]{3,2,1,0:T(8,128)}, f32[128,128]{1,0:T(8,128)}) custom-call(f32[3,8,32,128]{3,2,1,0:T(8,128)} %velocity_ref.1, f32[3,4,32,128]{3,2,1,0:T(8,128)} %copy-done, f32[3,4,32,128]{3,2,1,0:T(8,128)} %copy-done.1, f32[3,12,4,128]{3,2,1,0:T(4,128)} %copy-done.2, f32[3,12,4,128]{3,2,1,0:T(4,128)} %copy-done.3, ...), custom_call_target="tpu_custom_call" | custom-call | tf_op jit(solution)/shard_map/step_gram/pallas_call | solution.py:201
  32.3 0.9 %copy.5 = f32[128,128]{0,1:T(8,128)S(1)} copy(f32[128,128]{1,0:T(8,128)} %get-tuple-element.5) | data formatting | bytes 131072 | tf_op jit(solution)/shard_map/step_gram/pallas_call | solution.py:201
  33.2 0.1 constant_dynamic-slice_fusion
  33.3 1.6 %collective-permute-start.4 = (f32[64,128]{0,1:T(8,128)S(1)}, f32[64,128]{0,1:T(8,128)S(1)}, u32[]{:S(2)}, u32[]{:S(2)}) collective-permute-start(f32[64,128]{0,1:T(8,128)S(1)} %constant_dynamic-slice_fusion), channel_id=1, source_target_pairs={{0,1},{1,0},{2,3},{3,2},{4,5},{5,4},{6,7},{7,6},{8,9},{9,8},{10,11... | collective-permute-start | bytes 98312 | tf_op jit(solution)/shard_map/ppermute | solution.py:259
  34.9 0.9 %collective-permute-done.4 = f32[64,128]{0,1:T(8,128)S(1)} collective-permute-done((f32[64,128]{0,1:T(8,128)S(1)}, f32[64,128]{0,1:T(8,128)S(1)}, u32[]{:S(2)}, u32[]{:S(2)}) %collective-permute-start.4) | collective-permute-done | bytes 32800 | tf_op jit(solution)/shard_map/ppermute | solution.py:259
  35.8 0.1 dynamic-slice_add_fusion
  35.9 0.2 collective-permute-start.6
  36.1 2.6 %collective-permute-start.7 = (f32[64,128]{0,1:T(8,128)S(1)}, f32[64,128]{0,1:T(8,128)S(1)}, u32[]{:S(2)}, u32[]{:S(2)}) collective-permute-start(f32[64,128]{0,1:T(8,128)S(1)} %dynamic-slice_add_fusion), channel_id=1, source_target_pairs={{0,6},{1,7},{2,0},{3,1},{4,2},{5,3},{6,4},{7,5},{8,14},{9,15},{10,... | collective-permute-start | bytes 98312 | tf_op jit(solution)/shard_map/ppermute | solution.py:268
  38.7 1.1 %collective-permute-start.5 = (f32[64,128]{0,1:T(8,128)S(1)}, f32[64,128]{0,1:T(8,128)S(1)}, u32[]{:S(2)}, u32[]{:S(2)}) collective-permute-start(f32[64,128]{0,1:T(8,128)S(1)} %dynamic-slice_add_fusion), channel_id=1, source_target_pairs={{0,4},{1,5},{2,6},{3,7},{4,0},{5,1},{6,2},{7,3},{8,12},{9,13},{10,... | collective-permute-start | bytes 98312 | tf_op jit(solution)/shard_map/ppermute | solution.py:268
  39.8 0.5 collective-permute-done.6
  40.3 0.0 collective-permute-done.7
  40.3 3.0 %collective-permute-done.5 = f32[64,128]{0,1:T(8,128)S(1)} collective-permute-done((f32[64,128]{0,1:T(8,128)S(1)}, f32[64,128]{0,1:T(8,128)S(1)}, u32[]{:S(2)}, u32[]{:S(2)}) %collective-permute-start.5) | collective-permute-done | bytes 32800 | tf_op jit(solution)/shard_map/ppermute | solution.py:268
  43.3 1.4 %collective-permute-start.9 = (f32[64,128]{0,1:T(8,128)S(1)}, f32[64,128]{0,1:T(8,128)S(1)}, u32[]{:S(2)}, u32[]{:S(2)}) collective-permute-start(f32[64,128]{0,1:T(8,128)S(1)} %add_add_fusion.2), channel_id=1, source_target_pairs={{0,8},{1,9},{2,10},{3,11},{4,12},{5,13},{6,14},{7,15},{8,16},{9,17... | collective-permute-start | bytes 98312 | tf_op jit(solution)/shard_map/ppermute | solution.py:268
  44.7 1.4 %collective-permute-start.10 = (f32[64,128]{0,1:T(8,128)S(1)}, f32[64,128]{0,1:T(8,128)S(1)}, u32[]{:S(2)}, u32[]{:S(2)}) collective-permute-start(f32[64,128]{0,1:T(8,128)S(1)} %add_add_fusion.2), channel_id=1, source_target_pairs={{0,24},{1,25},{2,26},{3,27},{4,28},{5,29},{6,30},{7,31},{8,0},{9,1... | collective-permute-start | bytes 98312 | tf_op jit(solution)/shard_map/ppermute | solution.py:268
  46.1 1.4 %collective-permute-start.8 = (f32[64,128]{0,1:T(8,128)S(1)}, f32[64,128]{0,1:T(8,128)S(1)}, u32[]{:S(2)}, u32[]{:S(2)}) collective-permute-start(f32[64,128]{0,1:T(8,128)S(1)} %add_add_fusion.2), channel_id=1, source_target_pairs={{0,16},{1,17},{2,18},{3,19},{4,20},{5,21},{6,22},{7,23},{8,24},{9,... | collective-permute-start | bytes 98312 | tf_op jit(solution)/shard_map/ppermute | solution.py:268
  47.5 0.2 collective-permute-done.9
  47.7 0.1 collective-permute-done.10
  47.8 3.4 %collective-permute-done.8 = f32[64,128]{0,1:T(8,128)S(1)} collective-permute-done((f32[64,128]{0,1:T(8,128)S(1)}, f32[64,128]{0,1:T(8,128)S(1)}, u32[]{:S(2)}, u32[]{:S(2)}) %collective-permute-start.8) | collective-permute-done | bytes 32800 | tf_op jit(solution)/shard_map/ppermute | solution.py:268
  51.3 1.3 %collective-permute-start.12 = (f32[64,128]{0,1:T(8,128)S(1)}, f32[64,128]{0,1:T(8,128)S(1)}, u32[]{:S(2)}, u32[]{:S(2)}) collective-permute-start(f32[64,128]{0,1:T(8,128)S(1)} %add_add_fusion.1), channel_id=1, source_target_pairs={{0,32},{32,64},{64,96},{96,0},{1,33},{33,65},{65,97},{97,1},{2,34}... | collective-permute-start | bytes 98312 | tf_op jit(solution)/shard_map/ppermute | solution.py:268
  52.5 1.7 %collective-permute-start.13 = (f32[64,128]{0,1:T(8,128)S(1)}, f32[64,128]{0,1:T(8,128)S(1)}, u32[]{:S(2)}, u32[]{:S(2)}) collective-permute-start(f32[64,128]{0,1:T(8,128)S(1)} %add_add_fusion.1), channel_id=1, source_target_pairs={{0,96},{32,0},{64,32},{96,64},{1,97},{33,1},{65,33},{97,65},{2,98}... | collective-permute-start | bytes 98312 | tf_op jit(solution)/shard_map/ppermute | solution.py:268
  54.2 1.1 %collective-permute-start.11 = (f32[64,128]{0,1:T(8,128)S(1)}, f32[64,128]{0,1:T(8,128)S(1)}, u32[]{:S(2)}, u32[]{:S(2)}) collective-permute-start(f32[64,128]{0,1:T(8,128)S(1)} %add_add_fusion.1), channel_id=1, source_target_pairs={{0,64},{32,96},{64,0},{96,32},{1,65},{33,97},{65,1},{97,33},{2,66}... | collective-permute-start | bytes 98312 | tf_op jit(solution)/shard_map/ppermute | solution.py:268
  55.3 0.5 collective-permute-done.12
  55.8 0.0 collective-permute-done.13
  55.8 3.1 %collective-permute-done.11 = f32[64,128]{0,1:T(8,128)S(1)} collective-permute-done((f32[64,128]{0,1:T(8,128)S(1)}, f32[64,128]{0,1:T(8,128)S(1)}, u32[]{:S(2)}, u32[]{:S(2)}) %collective-permute-start.11) | collective-permute-done | bytes 32800 | tf_op jit(solution)/shard_map/ppermute | solution.py:268
  58.9 4.7 %collective-permute-start.14 = (f32[64,128]{0,1:T(8,128)S(1)}, f32[64,128]{0,1:T(8,128)S(1)}, u32[]{:S(2)}, u32[]{:S(2)}) collective-permute-start(f32[64,128]{0,1:T(8,128)S(1)} %add_add_fusion), channel_id=1, source_target_pairs={{0,1},{1,0},{2,3},{3,2},{4,5},{5,4},{6,7},{7,6},{8,9},{9,8},{10,11... | collective-permute-start | bytes 98312 | tf_op jit(solution)/shard_map/ppermute | solution.py:259
  63.6 0.9 %collective-permute-done.14 = f32[64,128]{0,1:T(8,128)S(1)} collective-permute-done((f32[64,128]{0,1:T(8,128)S(1)}, f32[64,128]{0,1:T(8,128)S(1)}, u32[]{:S(2)}, u32[]{:S(2)}) %collective-permute-start.14) | collective-permute-done | bytes 32800 | tf_op jit(solution)/shard_map/ppermute | solution.py:259
  64.5 0.1 pad_maximum_fusion.3
  64.6 0.1 copy.7
  64.7 0.1 fusion
  64.8 11.7 %cholesky.18 = f32[128,128]{1,0:T(8,128)S(1)} custom-call(f32[128,128]{1,0:T(8,128)S(1)} %fusion), custom_call_target="Cholesky" | custom-call | tf_op jit(solution)/shard_map/jit(cholesky)/cholesky | solution.py:301
  76.5 0.6 compare_reduce_fusion
  77.2 0.7 select_bitcast_fusion
  77.8 0.7 copy.8
  (10 shorter events, 0.1 us)
Async XLA Ops:
  1.7 7.6 %collective-permute-start = (f32[3,4,32,128]{3,2,1,0:T(8,128)S(1)}, f32[3,4,32,128]{3,2,1,0:T(8,128)S(1)}, u32[]{:S(2)}, u32[]{:S(2)}) collective-permute-start(f32[3,4,32,128]{3,2,1,0:T(8,128)S(1)} %get-tuple-element.14), channel_id=1, source_target_pairs={{0,32},{32,64},{64,96},{96,0},{1,33},{33,65},{65,97},{97,1},{2,34}... | collective-permute-start | bytes 589832 | tf_op jit(solution)/shard_map/ppermute | solution.py:227
  3.8 5.5 %collective-permute-start.1 = (f32[3,4,32,128]{3,2,1,0:T(8,128)S(1)}, f32[3,4,32,128]{3,2,1,0:T(8,128)S(1)}, u32[]{:S(2)}, u32[]{:S(2)}) collective-permute-start(f32[3,4,32,128]{3,2,1,0:T(8,128)S(1)} %get-tuple-element.13), channel_id=1, source_target_pairs={{0,96},{32,0},{64,32},{96,64},{1,97},{33,1},{65,33},{97,65},{2,98}... | collective-permute-start | bytes 589832 | tf_op jit(solution)/shard_map/ppermute | solution.py:227
  9.3 8.6 %copy-start.1 = (f32[3,4,32,128]{3,2,1,0:T(8,128)}, f32[3,4,32,128]{3,2,1,0:T(8,128)S(1)}, u32[]{:S(2)}) copy-start(f32[3,4,32,128]{3,2,1,0:T(8,128)S(1)} %collective-permute-done.1.right_ref) | copy-start | bytes 589828
  9.3 8.6 %copy-start = (f32[3,4,32,128]{3,2,1,0:T(8,128)}, f32[3,4,32,128]{3,2,1,0:T(8,128)S(1)}, u32[]{:S(2)}) copy-start(f32[3,4,32,128]{3,2,1,0:T(8,128)S(1)} %collective-permute-done.left_ref) | copy-start | bytes 589828
  10.4 4.8 %collective-permute-start.2 = (f32[3,12,4,128]{3,2,1,0:T(4,128)S(1)}, f32[3,12,4,128]{3,2,1,0:T(4,128)S(1)}, u32[]{:S(2)}, u32[]{:S(2)}) collective-permute-start(f32[3,12,4,128]{3,2,1,0:T(4,128)S(1)} %get-tuple-element.12), channel_id=1, source_target_pairs={{0,1},{1,2},{2,3},{3,4},{4,5},{5,6},{6,7},{7,8},{8,9},{9,10},{10,1... | collective-permute-start | bytes 221192 | tf_op jit(solution)/shard_map/ppermute | solution.py:227
  13.8 4.1 %collective-permute-start.3 = (f32[3,12,4,128]{3,2,1,0:T(4,128)S(1)}, f32[3,12,4,128]{3,2,1,0:T(4,128)S(1)}, u32[]{:S(2)}, u32[]{:S(2)}) collective-permute-start(f32[3,12,4,128]{3,2,1,0:T(4,128)S(1)} %get-tuple-element.11), channel_id=1, source_target_pairs={{0,31},{1,0},{2,1},{3,2},{4,3},{5,4},{6,5},{7,6},{8,7},{9,8},{10,9... | collective-permute-start | bytes 221192 | tf_op jit(solution)/shard_map/ppermute | solution.py:227
  15.2 2.7 %copy-start.2 = (f32[3,12,4,128]{3,2,1,0:T(4,128)}, f32[3,12,4,128]{3,2,1,0:T(4,128)S(1)}, u32[]{:S(2)}) copy-start(f32[3,12,4,128]{3,2,1,0:T(4,128)S(1)} %collective-permute-done.2.behind_ref) | copy-start | bytes 221188
  17.9 0.6 copy-start.3
  33.3 2.5 %collective-permute-start.4 = (f32[64,128]{0,1:T(8,128)S(1)}, f32[64,128]{0,1:T(8,128)S(1)}, u32[]{:S(2)}, u32[]{:S(2)}) collective-permute-start(f32[64,128]{0,1:T(8,128)S(1)} %constant_dynamic-slice_fusion), channel_id=1, source_target_pairs={{0,1},{1,0},{2,3},{3,2},{4,5},{5,4},{6,7},{7,6},{8,9},{9,8},{10,11... | collective-permute-start | bytes 98312 | tf_op jit(solution)/shard_map/ppermute | solution.py:259
  35.9 4.4 %collective-permute-start.6 = (f32[64,128]{0,1:T(8,128)S(1)}, f32[64,128]{0,1:T(8,128)S(1)}, u32[]{:S(2)}, u32[]{:S(2)}) collective-permute-start(f32[64,128]{0,1:T(8,128)S(1)} %dynamic-slice_add_fusion), channel_id=1, source_target_pairs={{0,2},{1,3},{2,4},{3,5},{4,6},{5,7},{6,0},{7,1},{8,10},{9,11},{10,... | collective-permute-start | bytes 98312 | tf_op jit(solution)/shard_map/ppermute | solution.py:268
  36.1 4.2 %collective-permute-start.7 = (f32[64,128]{0,1:T(8,128)S(1)}, f32[64,128]{0,1:T(8,128)S(1)}, u32[]{:S(2)}, u32[]{:S(2)}) collective-permute-start(f32[64,128]{0,1:T(8,128)S(1)} %dynamic-slice_add_fusion), channel_id=1, source_target_pairs={{0,6},{1,7},{2,0},{3,1},{4,2},{5,3},{6,4},{7,5},{8,14},{9,15},{10,... | collective-permute-start | bytes 98312 | tf_op jit(solution)/shard_map/ppermute | solution.py:268
  38.7 4.6 %collective-permute-start.5 = (f32[64,128]{0,1:T(8,128)S(1)}, f32[64,128]{0,1:T(8,128)S(1)}, u32[]{:S(2)}, u32[]{:S(2)}) collective-permute-start(f32[64,128]{0,1:T(8,128)S(1)} %dynamic-slice_add_fusion), channel_id=1, source_target_pairs={{0,4},{1,5},{2,6},{3,7},{4,0},{5,1},{6,2},{7,3},{8,12},{9,13},{10,... | collective-permute-start | bytes 98312 | tf_op jit(solution)/shard_map/ppermute | solution.py:268
  43.3 4.4 %collective-permute-start.9 = (f32[64,128]{0,1:T(8,128)S(1)}, f32[64,128]{0,1:T(8,128)S(1)}, u32[]{:S(2)}, u32[]{:S(2)}) collective-permute-start(f32[64,128]{0,1:T(8,128)S(1)} %add_add_fusion.2), channel_id=1, source_target_pairs={{0,8},{1,9},{2,10},{3,11},{4,12},{5,13},{6,14},{7,15},{8,16},{9,17... | collective-permute-start | bytes 98312 | tf_op jit(solution)/shard_map/ppermute | solution.py:268
  44.7 3.1 %collective-permute-start.10 = (f32[64,128]{0,1:T(8,128)S(1)}, f32[64,128]{0,1:T(8,128)S(1)}, u32[]{:S(2)}, u32[]{:S(2)}) collective-permute-start(f32[64,128]{0,1:T(8,128)S(1)} %add_add_fusion.2), channel_id=1, source_target_pairs={{0,24},{1,25},{2,26},{3,27},{4,28},{5,29},{6,30},{7,31},{8,0},{9,1... | collective-permute-start | bytes 98312 | tf_op jit(solution)/shard_map/ppermute | solution.py:268
  46.1 5.1 %collective-permute-start.8 = (f32[64,128]{0,1:T(8,128)S(1)}, f32[64,128]{0,1:T(8,128)S(1)}, u32[]{:S(2)}, u32[]{:S(2)}) collective-permute-start(f32[64,128]{0,1:T(8,128)S(1)} %add_add_fusion.2), channel_id=1, source_target_pairs={{0,16},{1,17},{2,18},{3,19},{4,20},{5,21},{6,22},{7,23},{8,24},{9,... | collective-permute-start | bytes 98312 | tf_op jit(solution)/shard_map/ppermute | solution.py:268
  51.3 4.5 %collective-permute-start.12 = (f32[64,128]{0,1:T(8,128)S(1)}, f32[64,128]{0,1:T(8,128)S(1)}, u32[]{:S(2)}, u32[]{:S(2)}) collective-permute-start(f32[64,128]{0,1:T(8,128)S(1)} %add_add_fusion.1), channel_id=1, source_target_pairs={{0,32},{32,64},{64,96},{96,0},{1,33},{33,65},{65,97},{97,1},{2,34}... | collective-permute-start | bytes 98312 | tf_op jit(solution)/shard_map/ppermute | solution.py:268
  52.5 3.2 %collective-permute-start.13 = (f32[64,128]{0,1:T(8,128)S(1)}, f32[64,128]{0,1:T(8,128)S(1)}, u32[]{:S(2)}, u32[]{:S(2)}) collective-permute-start(f32[64,128]{0,1:T(8,128)S(1)} %add_add_fusion.1), channel_id=1, source_target_pairs={{0,96},{32,0},{64,32},{96,64},{1,97},{33,1},{65,33},{97,65},{2,98}... | collective-permute-start | bytes 98312 | tf_op jit(solution)/shard_map/ppermute | solution.py:268
  54.2 4.6 %collective-permute-start.11 = (f32[64,128]{0,1:T(8,128)S(1)}, f32[64,128]{0,1:T(8,128)S(1)}, u32[]{:S(2)}, u32[]{:S(2)}) collective-permute-start(f32[64,128]{0,1:T(8,128)S(1)} %add_add_fusion.1), channel_id=1, source_target_pairs={{0,64},{32,96},{64,0},{96,32},{1,65},{33,97},{65,1},{97,33},{2,66}... | collective-permute-start | bytes 98312 | tf_op jit(solution)/shard_map/ppermute | solution.py:268
  58.9 5.6 %collective-permute-start.14 = (f32[64,128]{0,1:T(8,128)S(1)}, f32[64,128]{0,1:T(8,128)S(1)}, u32[]{:S(2)}, u32[]{:S(2)}) collective-permute-start(f32[64,128]{0,1:T(8,128)S(1)} %add_add_fusion), channel_id=1, source_target_pairs={{0,1},{1,0},{2,3},{3,2},{4,5},{5,4},{6,7},{7,6},{8,9},{9,8},{10,11... | collective-permute-start | bytes 98312 | tf_op jit(solution)/shard_map/ppermute | solution.py:259

commit v3 on v2

--- a/solution.py
+++ b/solution.py
@@ -192,8 +192,8 @@
 
 
 def step_and_gram(velocity, halos, weights, basis, stored, scale):
-    basis = pair_rows(basis)
-    stored = pair_rows(stored)
+    basis = pltpu.with_memory_space_constraint(pair_rows(basis), pltpu.HBM)
+    stored = pltpu.with_memory_space_constraint(pair_rows(stored), pltpu.HBM)
     length_x, length_z, lanes = velocity.shape[1:]
     hbm = pl.BlockSpec(memory_space=pltpu.HBM)
     free = pl.BlockSpec(memory_space=pl.ANY)
@@ -217,7 +217,7 @@
             pltpu.SemaphoreType.DMA((5,)),
             pltpu.SemaphoreType.DMA((1,)),
         ],
-        compiler_params=pltpu.CompilerParams(vmem_limit_bytes=60 * 2**20),
+        compiler_params=pltpu.CompilerParams(vmem_limit_bytes=36 * 2**20),
         name="step_gram",
     )(velocity, *halos, weights, basis, stored)
 
@@ -228,11 +228,15 @@
 
 
 def exchange(velocity):
-    left = shift(velocity[:, -4:], "gx", 1)
-    right = shift(velocity[:, :4], "gx", -1)
-    wide = jnp.concatenate([left[:, 2:], velocity, right[:, :2]], axis=1)
-    behind = shift(wide[:, :, -4:], "gy", 1)
-    ahead = shift(wide[:, :, :4], "gy", -1)
+    tail, head, back, front = lax.optimization_barrier(
+        (velocity[:, -4:], velocity[:, :4], velocity[:, :, -4:], velocity[:, :, :4])
+    )
+    left = shift(tail, "gx", 1)
+    right = shift(head, "gx", -1)
+    back = jnp.concatenate([left[:, 2:, -4:], back, right[:, :2, -4:]], axis=1)
+    front = jnp.concatenate([left[:, 2:, :4], front, right[:, :2, :4]], axis=1)
+    behind = shift(back, "gy", 1)
+    ahead = shift(front, "gy", -1)
     return left, right, behind, ahead
 
 
@@ -255,35 +259,77 @@
     )
 
 
-def swap_cores(part, count):
-    return lax.ppermute(part, "gy", [(i, i ^ 1) for i in range(count)])
-
-
-def ring_sum(part, axis, count, stride):
+def ring_sum(part, size, stride):
     def target(i, d):
         place = (i // stride) % 4
         return i + ((place + d) % 4 - place) * stride
 
     moved = [
-        lax.ppermute(part, axis, [(i, target(i, d)) for i in range(count)]) for d in (1, 2, 3)
+        lax.ppermute(part, ("gx", "gy"), [(i, target(i, d)) for i in range(1, size, 2)])
+        for d in (1, 2, 3)
     ]
     return (part + moved[1]) + (moved[0] + moved[2])
 
 
 def total_gram(gram):
     count = lax.axis_size("gy")
-    half = gram.shape[0] // 2
-    core = lax.axis_index("gy") % 2
-    mine = lax.dynamic_slice_in_dim(gram, core * half, half, 0)
-    other = lax.dynamic_slice_in_dim(gram, (1 - core) * half, half, 0)
-    part = mine + swap_cores(other, count)
-    part = ring_sum(part, "gy", count, 2)
-    part = ring_sum(part, "gy", count, 8)
-    part = ring_sum(part, "gx", 4, 1)
-    rest = swap_cores(part, count)
-    low = jnp.where(core == 0, part, rest)
-    high = jnp.where(core == 0, rest, part)
-    return jnp.concatenate([low, high], 0)
+    size = count * lax.axis_size("gx")
+    part = gram + lax.ppermute(gram, "gy", [(i, i + 1) for i in range(0, count, 2)])
+    for stride in (2, 8, count):
+        part = ring_sum(part, size, stride)
+    rest = lax.ppermute(part, "gy", [(i + 1, i) for i in range(0, count, 2)])
+    return jnp.where(lax.axis_index("gy") % 2 == 1, part, rest)
+
+
+PANEL = 16
+
+
+def factor_kernel(gram_ref, factor_ref, work):
+    size = gram_ref.shape[0]
+    work[...] = gram_ref[...]
+    row = lax.broadcasted_iota(jnp.int32, (PANEL, size), 0)
+    lane = lax.broadcasted_iota(jnp.int32, (PANEL, size), 1)
+    for begin in range(0, size, PANEL):
+        end = begin + PANEL
+        rows = work[begin:end, :]
+        columns = [
+            jnp.broadcast_to(rows[:, begin + k : begin + k + 1], (PANEL, size))
+            for k in range(PANEL)
+        ]
+        scales = jnp.zeros((PANEL, size), jnp.float32)
+        for j in range(PANEL):
+            scale = lax.rsqrt(columns[j][j : j + 1, :])
+            below = jnp.where(row > j, columns[j] * scale, 0.0)
+            for k in range(j + 1, PANEL):
+                columns[k] = columns[k] - below * (columns[k][j : j + 1, :] * scale)
+            rows = rows - below * (rows[j : j + 1, :] * scale)
+            scales = jnp.where(row == j, jnp.broadcast_to(scale, (PANEL, size)), scales)
+        done = jnp.where(lane >= row + begin, rows * scales, 0.0)
+        factor_ref[begin:end, :] = done
+        if end < size:
+            high = done.astype(jnp.bfloat16)
+            left = done - high.astype(jnp.float32)
+            mid = left.astype(jnp.bfloat16)
+            low = (left - mid.astype(jnp.float32)).astype(jnp.bfloat16)
+            product = lax.dot_general(
+                jnp.concatenate([high, high, mid, high, low, mid], 0),
+                jnp.concatenate([high, mid, high, low, high, mid], 0),
+                (((0,), (0,)), ((), ())),
+                preferred_element_type=jnp.float32,
+            )
+            work[end:, :] = work[end:, :] - product[end:, :]
+
+
+def upper_factor(gram):
+    return pl.pallas_call(
+        factor_kernel,
+        out_shape=jax.ShapeDtypeStruct(gram.shape, jnp.float32),
+        in_specs=[pl.BlockSpec(memory_space=pltpu.VMEM)],
+        out_specs=pl.BlockSpec(memory_space=pltpu.VMEM),
+        scratch_shapes=[pltpu.VMEM(gram.shape, jnp.float32)],
+        compiler_params=pltpu.CompilerParams(vmem_limit_bytes=8 * 2**20),
+        name="upper_factor",
+    )(gram)
 
 
 def local(velocity, basis, snapshots):
@@ -298,7 +344,7 @@
     halos = exchange(velocity)
     weights = wall_rows(velocity.shape[3])
     advanced, gram = step_and_gram(velocity, halos, weights, basis, snapshots, 1.0 / total_rows)
-    factor = jnp.linalg.cholesky(total_gram(gram)).T
+    factor = upper_factor(total_gram(gram))
     return (advanced, factor)
 
 

time: 78.8 us -> 79.5 us (level)
  other arithmetic: 14.5 us -> 0.21 us
  starting transfers between devices: 25.3 us -> 35.7 us
  waiting for transfers between devices: 20.1 us -> 23.1 us
  Pallas kernels: 13.7 us -> 16.2 us
  local copies, waits for them, and re-layouts: 4.14 us -> 3.06 us
    another operation x3 -> x0, other arithmetic: 12.4 us -> none  [local(): factor = jnp.linalg.cholesky(total_gram(gram)).T]
    ppermute x11, starting transfers between devices: 18.4 us -> 28.8 us  [the longest x9 26.2 us: ring_sum(): lax.ppermute(part, ('gx', 'gy'), [(i, target(i, d)) for i in range(1, siz...]
    pallas_call x0 -> x1, Pallas kernels: none -> 3.84 us  [upper_factor(): pl.pallas_call(factor_kernel, out_shape=jax.ShapeDtypeStruct(gram.shape,...]
    ppermute x11, waiting for transfers between devices: 12.6 us -> 14.8 us  [the longest x1 7.06 us: total_gram(): lax.ppermute(gram, 'gy', [(i, i + 1) for i in range(0, count, 2)])]
    pallas_call x1, Pallas kernels: 13.7 us -> 12.3 us  [step_and_gram(): pl.pallas_call(functools.partial(step_kernel, scale), out_shape=(jax.Shap...]
    concatenate x2, other arithmetic: 1.16 us -> 0.04 us  [the longest x1 0.02 us: exchange(): front = jnp.concatenate([left[:, 2:, :4], front, right[:, :2, :4]], axis=1)]
    slice x3 -> x4, local copies, waits for them, and re-layouts: 1.07 us -> 2.03 us  [the longest x1 1.05 us: exchange(): velocity[:, :4]]
    pallas_call x1 -> x0, local copies, waits for them, and re-layouts: 0.93 us -> none  [step_and_gram(): pl.pallas_call(functools.partial(step_kernel, scale), out_shape=(jax.Shap...]
  transfers between devices with their start and end apart: 15 -> 15, of which waited for: 12 -> 9; matrix products, arithmetic and copies ran while one was open for 1% -> 0% of each run, Pallas kernels for 0% -> 0%
where the time goes in v3:
time: 79.5 us; the launch traced here: 79.1 us
  starting transfers between devices  35.7 us (45%)
  waiting for transfers between devices  23.1 us (29%)
  Pallas kernels  16.2 us (20%)
  local copies, waits for them, and re-layouts  3.06 us (4%)
  between operations  0.84 us (1%)
    ppermute x9, starting transfers between devices, ring_sum(): lax.ppermute(part, ('gx', 'gy'), [(i, target(i, d)) for i in range(1, siz...  26.2 us
    pallas_call x1, Pallas kernels, step_and_gram(): pl.pallas_call(functools.partial(step_kernel, scale), out_shape=(jax.Shap...  12.3 us
    ppermute x4, waiting for transfers between devices, shift(): lax.ppermute(part, axis, [(i, (i + step) % count) for i in range(count)])  8.31 us
    ppermute x1, waiting for transfers between devices, total_gram(): lax.ppermute(gram, 'gy', [(i, i + 1) for i in range(0, count, 2)])  7.06 us
    ppermute x4, starting transfers between devices, shift(): lax.ppermute(part, axis, [(i, (i + step) % count) for i in range(count)])  6.93 us
    ppermute x9, waiting for transfers between devices, ring_sum(): lax.ppermute(part, ('gx', 'gy'), [(i, target(i, d)) for i in range(1, siz...  6.89 us
    pallas_call x1, Pallas kernels, upper_factor(): pl.pallas_call(factor_kernel, out_shape=jax.ShapeDtypeStruct(gram.shape,...  3.84 us
  transfers between devices with their start and end apart: 15, of which 9 were waited for; matrix products, arithmetic and copies ran while one was open for 0% of the time, Pallas kernels for 0%

profile of v3, /device:TPU:1, one launch (start us, length us, event | category | flops | bytes accessed | tf_op | source)
XLA Modules:
  0.0 79.1 jit_solution(16851806742931891659)
XLA Ops:
  0.6 1.1 %fusion.8 = (f32[3,4,32,128]{3,2,1,0:T(8,128)S(1)}, f32[3,4,32,128]{3,2,1,0:T(8,128)S(1)}) fusion(f32[3,8,32,128]{3,2,1,0:T(8,128)} %velocity_ref.1), kind=kLoop, calls=%fused_computation.25 | loop fusion | bytes 786432 | tf_op jit(solution)/shard_map/slice | solution.py:232
  1.7 1.0 %fusion.7 = (f32[3,8,4,128]{3,2,1,0:T(4,128)S(1)}, f32[3,8,4,128]{3,2,1,0:T(4,128)S(1)}) fusion(f32[3,8,32,128]{3,2,1,0:T(8,128)} %velocity_ref.1), kind=kLoop, calls=%fused_computation.24 | loop fusion | bytes 196608 | tf_op jit(solution)/shard_map/slice | solution.py:232
  2.7 2.1 %collective-permute-start = (f32[3,4,32,128]{3,2,1,0:T(8,128)S(1)}, f32[3,4,32,128]{3,2,1,0:T(8,128)S(1)}, u32[]{:S(2)}, u32[]{:S(2)}) collective-permute-start(f32[3,4,32,128]{3,2,1,0:T(8,128)S(1)} %get-tuple-element.8), channel_id=1, source_target_pairs={{0,32},{32,64},{64,96},{96,0},{1,33},{33,65},{65,97},{97,1},{2,34}... | collective-permute-start | bytes 589832 | tf_op jit(solution)/shard_map/ppermute | solution.py:227
  4.8 1.3 %collective-permute-start.1 = (f32[3,4,32,128]{3,2,1,0:T(8,128)S(1)}, f32[3,4,32,128]{3,2,1,0:T(8,128)S(1)}, u32[]{:S(2)}, u32[]{:S(2)}) collective-permute-start(f32[3,4,32,128]{3,2,1,0:T(8,128)S(1)} %get-tuple-element.9), channel_id=1, source_target_pairs={{0,96},{32,0},{64,32},{96,64},{1,97},{33,1},{65,33},{97,65},{2,98}... | collective-permute-start | bytes 589832 | tf_op jit(solution)/shard_map/ppermute | solution.py:227
  6.1 0.1 fusion.5
  6.2 4.1 %collective-permute-done.left_ref = f32[3,4,32,128]{3,2,1,0:T(8,128)S(1)} collective-permute-done((f32[3,4,32,128]{3,2,1,0:T(8,128)S(1)}, f32[3,4,32,128]{3,2,1,0:T(8,128)S(1)}, u32[]{:S(2)}, u32[]{:S(2)}) %collective-permute-start) | collective-permute-done | bytes 196640 | tf_op jit(solution)/shard_map/ppermute | solution.py:227
  10.3 0.0 collective-permute-done.1.right_ref
  10.3 1.8 %collective-permute-start.3 = (f32[3,12,4,128]{3,2,1,0:T(4,128)S(1)}, f32[3,12,4,128]{3,2,1,0:T(4,128)S(1)}, u32[]{:S(2)}, u32[]{:S(2)}) collective-permute-start(f32[3,12,4,128]{3,2,1,0:T(4,128)S(1)} %pad_maximum_fusion.1), channel_id=1, source_target_pairs={{0,31},{1,0},{2,1},{3,2},{4,3},{5,4},{6,5},{7,6},{8,7},{9,8},{10,9... | collective-permute-start | bytes 221192 | tf_op jit(solution)/shard_map/ppermute | solution.py:227
  12.2 1.6 %collective-permute-start.2 = (f32[3,12,4,128]{3,2,1,0:T(4,128)S(1)}, f32[3,12,4,128]{3,2,1,0:T(4,128)S(1)}, u32[]{:S(2)}, u32[]{:S(2)}) collective-permute-start(f32[3,12,4,128]{3,2,1,0:T(4,128)S(1)} %pad_maximum_fusion), channel_id=1, source_target_pairs={{0,1},{1,2},{2,3},{3,4},{4,5},{5,6},{6,7},{7,8},{8,9},{9,10},{10,1... | collective-permute-start | bytes 221192 | tf_op jit(solution)/shard_map/ppermute | solution.py:227
  13.9 1.9 %collective-permute-done.3.ahead_ref = f32[3,12,4,128]{3,2,1,0:T(4,128)S(1)} collective-permute-done((f32[3,12,4,128]{3,2,1,0:T(4,128)S(1)}, f32[3,12,4,128]{3,2,1,0:T(4,128)S(1)}, u32[]{:S(2)}, u32[]{:S(2)}) %collective-permute-start.3) | collective-permute-done | bytes 73760 | tf_op jit(solution)/shard_map/ppermute | solution.py:227
  15.8 2.4 %collective-permute-done.2.behind_ref = f32[3,12,4,128]{3,2,1,0:T(4,128)S(1)} collective-permute-done((f32[3,12,4,128]{3,2,1,0:T(4,128)S(1)}, f32[3,12,4,128]{3,2,1,0:T(4,128)S(1)}, u32[]{:S(2)}, u32[]{:S(2)}) %collective-permute-start.2) | collective-permute-done | bytes 73760 | tf_op jit(solution)/shard_map/ppermute | solution.py:227
  18.1 0.0 copy-start
  18.1 1.0 %copy-done = f32[3,8,32,128]{3,2,1,0:T(8,128)S(1)} copy-done((f32[3,8,32,128]{3,2,1,0:T(8,128)S(1)}, f32[3,8,32,128]{3,2,1,0:T(8,128)}, u32[]{:S(2)}) %copy-start) | copy-done | bytes 393240
  19.1 12.3 %step_gram.1 = (f32[3,8,32,128]{3,2,1,0:T(8,128)}, f32[128,128]{1,0:T(8,128)S(1)}) custom-call(f32[3,8,32,128]{3,2,1,0:T(8,128)S(1)} %copy-done, f32[3,4,32,128]{3,2,1,0:T(8,128)S(1)} %collective-permute-done.left_ref, f32[3,4,32,128]{3,2,1,0:T(8,128)S(1)} %collective-permute-done.1.right_ref, f32[3,12,4,128]{3,2,1,0:T(4,128)S(1)} %collective-permute-done.2.behind_ref, ...), custom_call_target="tpu_custom_call" | custom-call | tf_op jit(solution)/shard_map/step_gram/pallas_call | solution.py:201
  31.5 1.3 %collective-permute-start.4 = (f32[128,128]{1,0:T(8,128)S(1)}, f32[128,128]{1,0:T(8,128)S(1)}, u32[]{:S(2)}, u32[]{:S(2)}) collective-permute-start(f32[128,128]{1,0:T(8,128)S(1)} %get-tuple-element.13), channel_id=1, source_target_pairs={{0,1},{2,3},{4,5},{6,7},{8,9},{10,11},{12,13},{14,15},{16,17},{18,... | collective-permute-start | bytes 196616 | tf_op jit(solution)/shard_map/ppermute | solution.py:277
  32.8 7.1 %collective-permute-done.4 = f32[128,128]{1,0:T(8,128)S(1)} collective-permute-done((f32[128,128]{1,0:T(8,128)S(1)}, f32[128,128]{1,0:T(8,128)S(1)}, u32[]{:S(2)}, u32[]{:S(2)}) %collective-permute-start.4) | collective-permute-done | bytes 65568 | tf_op jit(solution)/shard_map/ppermute | solution.py:277
  39.8 1.9 %collective-permute-start.5 = (f32[128,128]{1,0:T(8,128)S(1)}, f32[128,128]{1,0:T(8,128)S(1)}, u32[]{:S(2)}, u32[]{:S(2)}) collective-permute-start(f32[128,128]{1,0:T(8,128)S(1)} %add.50), channel_id=1, source_target_pairs={{1,5},{3,7},{5,1},{7,3},{9,13},{11,15},{13,9},{15,11},{17,21},{19,... | collective-permute-start | bytes 196616 | tf_op jit(solution)/shard_map/ppermute | solution.py:268
  41.8 1.9 %collective-permute-start.6 = (f32[128,128]{1,0:T(8,128)S(1)}, f32[128,128]{1,0:T(8,128)S(1)}, u32[]{:S(2)}, u32[]{:S(2)}) collective-permute-start(f32[128,128]{1,0:T(8,128)S(1)} %add.50), channel_id=1, source_target_pairs={{1,3},{3,5},{5,7},{7,1},{9,11},{11,13},{13,15},{15,9},{17,19},{19,... | collective-permute-start | bytes 196616 | tf_op jit(solution)/shard_map/ppermute | solution.py:268
  43.7 4.6 %collective-permute-start.7 = (f32[128,128]{1,0:T(8,128)S(1)}, f32[128,128]{1,0:T(8,128)S(1)}, u32[]{:S(2)}, u32[]{:S(2)}) collective-permute-start(f32[128,128]{1,0:T(8,128)S(1)} %add.50), channel_id=1, source_target_pairs={{1,7},{3,1},{5,3},{7,5},{9,15},{11,9},{13,11},{15,13},{17,23},{19,... | collective-permute-start | bytes 196616 | tf_op jit(solution)/shard_map/ppermute | solution.py:268
  48.3 0.0 collective-permute-done.5
  48.3 0.0 collective-permute-done.6
  48.3 1.6 %collective-permute-done.7 = f32[128,128]{1,0:T(8,128)S(1)} collective-permute-done((f32[128,128]{1,0:T(8,128)S(1)}, f32[128,128]{1,0:T(8,128)S(1)}, u32[]{:S(2)}, u32[]{:S(2)}) %collective-permute-start.7) | collective-permute-done | bytes 65568 | tf_op jit(solution)/shard_map/ppermute | solution.py:268
  49.9 2.2 %collective-permute-start.10 = (f32[128,128]{1,0:T(8,128)S(1)}, f32[128,128]{1,0:T(8,128)S(1)}, u32[]{:S(2)}, u32[]{:S(2)}) collective-permute-start(f32[128,128]{1,0:T(8,128)S(1)} %add_add_fusion.2), channel_id=1, source_target_pairs={{1,25},{3,27},{5,29},{7,31},{9,1},{11,3},{13,5},{15,7},{17,9},{19,... | collective-permute-start | bytes 196616 | tf_op jit(solution)/shard_map/ppermute | solution.py:268
  52.1 1.9 %collective-permute-start.8 = (f32[128,128]{1,0:T(8,128)S(1)}, f32[128,128]{1,0:T(8,128)S(1)}, u32[]{:S(2)}, u32[]{:S(2)}) collective-permute-start(f32[128,128]{1,0:T(8,128)S(1)} %add_add_fusion.2), channel_id=1, source_target_pairs={{1,17},{3,19},{5,21},{7,23},{9,25},{11,27},{13,29},{15,31},{17,1},... | collective-permute-start | bytes 196616 | tf_op jit(solution)/shard_map/ppermute | solution.py:268
  54.0 3.1 %collective-permute-start.9 = (f32[128,128]{1,0:T(8,128)S(1)}, f32[128,128]{1,0:T(8,128)S(1)}, u32[]{:S(2)}, u32[]{:S(2)}) collective-permute-start(f32[128,128]{1,0:T(8,128)S(1)} %add_add_fusion.2), channel_id=1, source_target_pairs={{1,9},{3,11},{5,13},{7,15},{9,17},{11,19},{13,21},{15,23},{17,25},... | collective-permute-start | bytes 196616 | tf_op jit(solution)/shard_map/ppermute | solution.py:268
  57.1 0.0 collective-permute-done.10
  57.1 1.5 %collective-permute-done.8 = f32[128,128]{1,0:T(8,128)S(1)} collective-permute-done((f32[128,128]{1,0:T(8,128)S(1)}, f32[128,128]{1,0:T(8,128)S(1)}, u32[]{:S(2)}, u32[]{:S(2)}) %collective-permute-start.8) | collective-permute-done | bytes 65568 | tf_op jit(solution)/shard_map/ppermute | solution.py:268
  58.6 2.5 %collective-permute-done.9 = f32[128,128]{1,0:T(8,128)S(1)} collective-permute-done((f32[128,128]{1,0:T(8,128)S(1)}, f32[128,128]{1,0:T(8,128)S(1)}, u32[]{:S(2)}, u32[]{:S(2)}) %collective-permute-start.9) | collective-permute-done | bytes 65568 | tf_op jit(solution)/shard_map/ppermute | solution.py:268
  61.2 4.1 %collective-permute-start.11 = (f32[128,128]{1,0:T(8,128)S(1)}, f32[128,128]{1,0:T(8,128)S(1)}, u32[]{:S(2)}, u32[]{:S(2)}) collective-permute-start(f32[128,128]{1,0:T(8,128)S(1)} %add_add_fusion.1), channel_id=1, source_target_pairs={{1,65},{3,67},{5,69},{7,71},{9,73},{11,75},{13,77},{15,79},{17,81}... | collective-permute-start | bytes 196616 | tf_op jit(solution)/shard_map/ppermute | solution.py:268
  65.2 2.7 %collective-permute-start.12 = (f32[128,128]{1,0:T(8,128)S(1)}, f32[128,128]{1,0:T(8,128)S(1)}, u32[]{:S(2)}, u32[]{:S(2)}) collective-permute-start(f32[128,128]{1,0:T(8,128)S(1)} %add_add_fusion.1), channel_id=1, source_target_pairs={{1,33},{3,35},{5,37},{7,39},{9,41},{11,43},{13,45},{15,47},{17,49}... | collective-permute-start | bytes 196616 | tf_op jit(solution)/shard_map/ppermute | solution.py:268
  67.9 3.8 %collective-permute-start.13 = (f32[128,128]{1,0:T(8,128)S(1)}, f32[128,128]{1,0:T(8,128)S(1)}, u32[]{:S(2)}, u32[]{:S(2)}) collective-permute-start(f32[128,128]{1,0:T(8,128)S(1)} %add_add_fusion.1), channel_id=1, source_target_pairs={{1,97},{3,99},{5,101},{7,103},{9,105},{11,107},{13,109},{15,111},{... | collective-permute-start | bytes 196616 | tf_op jit(solution)/shard_map/ppermute | solution.py:268
  71.7 0.0 collective-permute-done.11
  71.7 0.0 collective-permute-done.12
  71.8 1.3 %collective-permute-done.13 = f32[128,128]{1,0:T(8,128)S(1)} collective-permute-done((f32[128,128]{1,0:T(8,128)S(1)}, f32[128,128]{1,0:T(8,128)S(1)}, u32[]{:S(2)}, u32[]{:S(2)}) %collective-permute-start.13) | collective-permute-done | bytes 65568 | tf_op jit(solution)/shard_map/ppermute | solution.py:268
  73.1 1.3 %collective-permute-start.14 = (f32[128,128]{1,0:T(8,128)S(1)}, f32[128,128]{1,0:T(8,128)S(1)}, u32[]{:S(2)}, u32[]{:S(2)}) collective-permute-start(f32[128,128]{1,0:T(8,128)S(1)} %add_add_fusion), channel_id=1, source_target_pairs={{1,0},{3,2},{5,4},{7,6},{9,8},{11,10},{13,12},{15,14},{17,16},{19,... | collective-permute-start | bytes 196616 | tf_op jit(solution)/shard_map/ppermute | solution.py:280
  74.4 0.9 %collective-permute-done.14 = f32[128,128]{1,0:T(8,128)S(1)} collective-permute-done((f32[128,128]{1,0:T(8,128)S(1)}, f32[128,128]{1,0:T(8,128)S(1)}, u32[]{:S(2)}, u32[]{:S(2)}) %collective-permute-start.14) | collective-permute-done | bytes 65568 | tf_op jit(solution)/shard_map/ppermute | solution.py:280
  75.3 3.8 %upper_factor.1 = f32[128,128]{1,0:T(8,128)} custom-call(f32[128,128]{1,0:T(8,128)S(1)} %broadcast_select_fusion.gram_ref), custom_call_target="tpu_custom_call" | custom-call | tf_op jit(solution)/shard_map/upper_factor/pallas_call | solution.py:324
  (13 shorter events, 0.2 us)
Async XLA Ops:
  2.7 7.6 %collective-permute-start = (f32[3,4,32,128]{3,2,1,0:T(8,128)S(1)}, f32[3,4,32,128]{3,2,1,0:T(8,128)S(1)}, u32[]{:S(2)}, u32[]{:S(2)}) collective-permute-start(f32[3,4,32,128]{3,2,1,0:T(8,128)S(1)} %get-tuple-element.8), channel_id=1, source_target_pairs={{0,32},{32,64},{64,96},{96,0},{1,33},{33,65},{65,97},{97,1},{2,34}... | collective-permute-start | bytes 589832 | tf_op jit(solution)/shard_map/ppermute | solution.py:227
  4.8 5.5 %collective-permute-start.1 = (f32[3,4,32,128]{3,2,1,0:T(8,128)S(1)}, f32[3,4,32,128]{3,2,1,0:T(8,128)S(1)}, u32[]{:S(2)}, u32[]{:S(2)}) collective-permute-start(f32[3,4,32,128]{3,2,1,0:T(8,128)S(1)} %get-tuple-element.9), channel_id=1, source_target_pairs={{0,96},{32,0},{64,32},{96,64},{1,97},{33,1},{65,33},{97,65},{2,98}... | collective-permute-start | bytes 589832 | tf_op jit(solution)/shard_map/ppermute | solution.py:227
  10.3 5.4 %collective-permute-start.3 = (f32[3,12,4,128]{3,2,1,0:T(4,128)S(1)}, f32[3,12,4,128]{3,2,1,0:T(4,128)S(1)}, u32[]{:S(2)}, u32[]{:S(2)}) collective-permute-start(f32[3,12,4,128]{3,2,1,0:T(4,128)S(1)} %pad_maximum_fusion.1), channel_id=1, source_target_pairs={{0,31},{1,0},{2,1},{3,2},{4,3},{5,4},{6,5},{7,6},{8,7},{9,8},{10,9... | collective-permute-start | bytes 221192 | tf_op jit(solution)/shard_map/ppermute | solution.py:227
  12.2 5.9 %collective-permute-start.2 = (f32[3,12,4,128]{3,2,1,0:T(4,128)S(1)}, f32[3,12,4,128]{3,2,1,0:T(4,128)S(1)}, u32[]{:S(2)}, u32[]{:S(2)}) collective-permute-start(f32[3,12,4,128]{3,2,1,0:T(4,128)S(1)} %pad_maximum_fusion), channel_id=1, source_target_pairs={{0,1},{1,2},{2,3},{3,4},{4,5},{5,6},{6,7},{7,8},{8,9},{9,10},{10,1... | collective-permute-start | bytes 221192 | tf_op jit(solution)/shard_map/ppermute | solution.py:227
  18.1 1.0 %copy-start = (f32[3,8,32,128]{3,2,1,0:T(8,128)S(1)}, f32[3,8,32,128]{3,2,1,0:T(8,128)}, u32[]{:S(2)}) copy-start(f32[3,8,32,128]{3,2,1,0:T(8,128)} %velocity_ref.1) | copy-start | bytes 1179652
  31.5 8.4 %collective-permute-start.4 = (f32[128,128]{1,0:T(8,128)S(1)}, f32[128,128]{1,0:T(8,128)S(1)}, u32[]{:S(2)}, u32[]{:S(2)}) collective-permute-start(f32[128,128]{1,0:T(8,128)S(1)} %get-tuple-element.13), channel_id=1, source_target_pairs={{0,1},{2,3},{4,5},{6,7},{8,9},{10,11},{12,13},{14,15},{16,17},{18,... | collective-permute-start | bytes 196616 | tf_op jit(solution)/shard_map/ppermute | solution.py:277
  39.8 8.4 %collective-permute-start.5 = (f32[128,128]{1,0:T(8,128)S(1)}, f32[128,128]{1,0:T(8,128)S(1)}, u32[]{:S(2)}, u32[]{:S(2)}) collective-permute-start(f32[128,128]{1,0:T(8,128)S(1)} %add.50), channel_id=1, source_target_pairs={{1,5},{3,7},{5,1},{7,3},{9,13},{11,15},{13,9},{15,11},{17,21},{19,... | collective-permute-start | bytes 196616 | tf_op jit(solution)/shard_map/ppermute | solution.py:268
  41.8 6.5 %collective-permute-start.6 = (f32[128,128]{1,0:T(8,128)S(1)}, f32[128,128]{1,0:T(8,128)S(1)}, u32[]{:S(2)}, u32[]{:S(2)}) collective-permute-start(f32[128,128]{1,0:T(8,128)S(1)} %add.50), channel_id=1, source_target_pairs={{1,3},{3,5},{5,7},{7,1},{9,11},{11,13},{13,15},{15,9},{17,19},{19,... | collective-permute-start | bytes 196616 | tf_op jit(solution)/shard_map/ppermute | solution.py:268
  43.7 6.2 %collective-permute-start.7 = (f32[128,128]{1,0:T(8,128)S(1)}, f32[128,128]{1,0:T(8,128)S(1)}, u32[]{:S(2)}, u32[]{:S(2)}) collective-permute-start(f32[128,128]{1,0:T(8,128)S(1)} %add.50), channel_id=1, source_target_pairs={{1,7},{3,1},{5,3},{7,5},{9,15},{11,9},{13,11},{15,13},{17,23},{19,... | collective-permute-start | bytes 196616 | tf_op jit(solution)/shard_map/ppermute | solution.py:268
  49.9 7.2 %collective-permute-start.10 = (f32[128,128]{1,0:T(8,128)S(1)}, f32[128,128]{1,0:T(8,128)S(1)}, u32[]{:S(2)}, u32[]{:S(2)}) collective-permute-start(f32[128,128]{1,0:T(8,128)S(1)} %add_add_fusion.2), channel_id=1, source_target_pairs={{1,25},{3,27},{5,29},{7,31},{9,1},{11,3},{13,5},{15,7},{17,9},{19,... | collective-permute-start | bytes 196616 | tf_op jit(solution)/shard_map/ppermute | solution.py:268
  52.1 6.5 %collective-permute-start.8 = (f32[128,128]{1,0:T(8,128)S(1)}, f32[128,128]{1,0:T(8,128)S(1)}, u32[]{:S(2)}, u32[]{:S(2)}) collective-permute-start(f32[128,128]{1,0:T(8,128)S(1)} %add_add_fusion.2), channel_id=1, source_target_pairs={{1,17},{3,19},{5,21},{7,23},{9,25},{11,27},{13,29},{15,31},{17,1},... | collective-permute-start | bytes 196616 | tf_op jit(solution)/shard_map/ppermute | solution.py:268
  54.0 7.1 %collective-permute-start.9 = (f32[128,128]{1,0:T(8,128)S(1)}, f32[128,128]{1,0:T(8,128)S(1)}, u32[]{:S(2)}, u32[]{:S(2)}) collective-permute-start(f32[128,128]{1,0:T(8,128)S(1)} %add_add_fusion.2), channel_id=1, source_target_pairs={{1,9},{3,11},{5,13},{7,15},{9,17},{11,19},{13,21},{15,23},{17,25},... | collective-permute-start | bytes 196616 | tf_op jit(solution)/shard_map/ppermute | solution.py:268
  61.2 10.6 %collective-permute-start.11 = (f32[128,128]{1,0:T(8,128)S(1)}, f32[128,128]{1,0:T(8,128)S(1)}, u32[]{:S(2)}, u32[]{:S(2)}) collective-permute-start(f32[128,128]{1,0:T(8,128)S(1)} %add_add_fusion.1), channel_id=1, source_target_pairs={{1,65},{3,67},{5,69},{7,71},{9,73},{11,75},{13,77},{15,79},{17,81}... | collective-permute-start | bytes 196616 | tf_op jit(solution)/shard_map/ppermute | solution.py:268
  65.2 6.5 %collective-permute-start.12 = (f32[128,128]{1,0:T(8,128)S(1)}, f32[128,128]{1,0:T(8,128)S(1)}, u32[]{:S(2)}, u32[]{:S(2)}) collective-permute-start(f32[128,128]{1,0:T(8,128)S(1)} %add_add_fusion.1), channel_id=1, source_target_pairs={{1,33},{3,35},{5,37},{7,39},{9,41},{11,43},{13,45},{15,47},{17,49}... | collective-permute-start | bytes 196616 | tf_op jit(solution)/shard_map/ppermute | solution.py:268
  67.9 5.1 %collective-permute-start.13 = (f32[128,128]{1,0:T(8,128)S(1)}, f32[128,128]{1,0:T(8,128)S(1)}, u32[]{:S(2)}, u32[]{:S(2)}) collective-permute-start(f32[128,128]{1,0:T(8,128)S(1)} %add_add_fusion.1), channel_id=1, source_target_pairs={{1,97},{3,99},{5,101},{7,103},{9,105},{11,107},{13,109},{15,111},{... | collective-permute-start | bytes 196616 | tf_op jit(solution)/shard_map/ppermute | solution.py:268
  73.1 2.2 %collective-permute-start.14 = (f32[128,128]{1,0:T(8,128)S(1)}, f32[128,128]{1,0:T(8,128)S(1)}, u32[]{:S(2)}, u32[]{:S(2)}) collective-permute-start(f32[128,128]{1,0:T(8,128)S(1)} %add_add_fusion), channel_id=1, source_target_pairs={{1,0},{3,2},{5,4},{7,6},{9,8},{11,10},{13,12},{15,14},{17,16},{19,... | collective-permute-start | bytes 196616 | tf_op jit(solution)/shard_map/ppermute | solution.py:280

commit v4 on v3

--- a/solution.py
+++ b/solution.py
@@ -194,6 +194,7 @@
 def step_and_gram(velocity, halos, weights, basis, stored, scale):
     basis = pltpu.with_memory_space_constraint(pair_rows(basis), pltpu.HBM)
     stored = pltpu.with_memory_space_constraint(pair_rows(stored), pltpu.HBM)
+    velocity = pltpu.with_memory_space_constraint(velocity, pltpu.HBM)
     length_x, length_z, lanes = velocity.shape[1:]
     hbm = pl.BlockSpec(memory_space=pltpu.HBM)
     free = pl.BlockSpec(memory_space=pl.ANY)
@@ -204,7 +205,7 @@
             jax.ShapeDtypeStruct(velocity.shape, jnp.float32),
             jax.ShapeDtypeStruct((128, 128), jnp.float32),
         ),
-        in_specs=[free, free, free, free, free, vmem, hbm, hbm],
+        in_specs=[hbm, free, free, free, free, vmem, hbm, hbm],
         out_specs=(hbm, vmem),
         scratch_shapes=[
             pltpu.VMEM((basis.shape[1], 256, lanes), jnp.bfloat16),
@@ -228,11 +229,9 @@
 
 
 def exchange(velocity):
-    tail, head, back, front = lax.optimization_barrier(
-        (velocity[:, -4:], velocity[:, :4], velocity[:, :, -4:], velocity[:, :, :4])
-    )
-    left = shift(tail, "gx", 1)
-    right = shift(head, "gx", -1)
+    left = shift(velocity[:, -4:], "gx", 1)
+    right = shift(velocity[:, :4], "gx", -1)
+    back, front = lax.optimization_barrier((velocity[:, :, -4:], velocity[:, :, :4]))
     back = jnp.concatenate([left[:, 2:, -4:], back, right[:, :2, -4:]], axis=1)
     front = jnp.concatenate([left[:, 2:, :4], front, right[:, :2, :4]], axis=1)
     behind = shift(back, "gy", 1)
@@ -259,26 +258,35 @@
     )
 
 
-def ring_sum(part, size, stride):
+def swap_cores(part, count):
+    return lax.ppermute(part, "gy", [(i, i ^ 1) for i in range(count)])
+
+
+def ring_sum(part, axis, count, stride):
     def target(i, d):
         place = (i // stride) % 4
         return i + ((place + d) % 4 - place) * stride
 
     moved = [
-        lax.ppermute(part, ("gx", "gy"), [(i, target(i, d)) for i in range(1, size, 2)])
-        for d in (1, 2, 3)
+        lax.ppermute(part, axis, [(i, target(i, d)) for i in range(count)]) for d in (1, 2, 3)
     ]
     return (part + moved[1]) + (moved[0] + moved[2])
 
 
 def total_gram(gram):
     count = lax.axis_size("gy")
-    size = count * lax.axis_size("gx")
-    part = gram + lax.ppermute(gram, "gy", [(i, i + 1) for i in range(0, count, 2)])
-    for stride in (2, 8, count):
-        part = ring_sum(part, size, stride)
-    rest = lax.ppermute(part, "gy", [(i + 1, i) for i in range(0, count, 2)])
-    return jnp.where(lax.axis_index("gy") % 2 == 1, part, rest)
+    half = gram.shape[0] // 2
+    core = lax.axis_index("gy") % 2
+    mine = lax.dynamic_slice_in_dim(gram, core * half, half, 0)
+    other = lax.dynamic_slice_in_dim(gram, (1 - core) * half, half, 0)
+    part = mine + swap_cores(other, count)
+    part = ring_sum(part, "gy", count, 2)
+    part = ring_sum(part, "gy", count, 8)
+    part = ring_sum(part, "gx", 4, 1)
+    rest = swap_cores(part, count)
+    low = jnp.where(core == 0, part, rest)
+    high = jnp.where(core == 0, rest, part)
+    return jnp.concatenate([low, high], 0)
 
 
 PANEL = 16

time: 79.5 us -> 63.1 us (0.79)
  starting transfers between devices: 35.7 us -> 25.6 us
  waiting for transfers between devices: 23.1 us -> 18.2 us
  local copies, waits for them, and re-layouts: 3.06 us -> 2.07 us
    ppermute x11, starting transfers between devices: 28.8 us -> 18.7 us  [the longest x9 12.2 us: ring_sum(): lax.ppermute(part, axis, [(i, target(i, d)) for i in range(count)])]
    ppermute x11, waiting for transfers between devices: 14.8 us -> 11.1 us  [the longest x9 9.35 us: ring_sum(): lax.ppermute(part, axis, [(i, target(i, d)) for i in range(count)])]
    ppermute x4, waiting for transfers between devices: 8.31 us -> 7.09 us  [shift(): lax.ppermute(part, axis, [(i, (i + step) % count) for i in range(count)])]
    unnamed x2 -> x0, local copies, waits for them, and re-layouts: 1 us -> none
  transfers between devices with their start and end apart: 15 -> 15, of which waited for: 9 -> 10; matrix products, arithmetic and copies ran while one was open for 0% -> 2% of each run, Pallas kernels for 0% -> 0%
where the time goes in v4:
time: 63.1 us; the launch traced here: 62.9 us
  starting transfers between devices  25.6 us (41%)
  waiting for transfers between devices  18.2 us (29%)
  Pallas kernels  16.1 us (26%)
  local copies, waits for them, and re-layouts  2.07 us (3%)
  between operations  0.75 us (1%)
    pallas_call x1, Pallas kernels, step_and_gram(): pl.pallas_call(functools.partial(step_kernel, scale), out_shape=(jax.Shap...  12.3 us
    ppermute x9, starting transfers between devices, ring_sum(): lax.ppermute(part, axis, [(i, target(i, d)) for i in range(count)])  12.2 us
    ppermute x9, waiting for transfers between devices, ring_sum(): lax.ppermute(part, axis, [(i, target(i, d)) for i in range(count)])  9.35 us
    ppermute x4, waiting for transfers between devices, shift(): lax.ppermute(part, axis, [(i, (i + step) % count) for i in range(count)])  7.09 us
    ppermute x4, starting transfers between devices, shift(): lax.ppermute(part, axis, [(i, (i + step) % count) for i in range(count)])  6.92 us
    ppermute x2, starting transfers between devices, swap_cores(): return lax.ppermute(part, 'gy', [(i, i ^ 1) for i in range(count)])  6.55 us
    pallas_call x1, Pallas kernels, upper_factor(): pl.pallas_call(factor_kernel, out_shape=jax.ShapeDtypeStruct(gram.shape,...  3.84 us
    ppermute x2, waiting for transfers between devices, swap_cores(): return lax.ppermute(part, 'gy', [(i, i ^ 1) for i in range(count)])  1.72 us
  transfers between devices with their start and end apart: 15, of which 10 were waited for; matrix products, arithmetic and copies ran while one was open for 2% of the time, Pallas kernels for 0%

profile of v4, /device:TPU:1, one launch (start us, length us, event | category | flops | bytes accessed | tf_op | source)
XLA Modules:
  0.0 62.9 jit_solution(7024209121479354921)
XLA Ops:
  0.6 1.1 %fusion.8 = (f32[3,4,32,128]{3,2,1,0:T(8,128)S(1)}, f32[3,4,32,128]{3,2,1,0:T(8,128)S(1)}) fusion(f32[3,8,32,128]{3,2,1,0:T(8,128)} %velocity_ref.1), kind=kLoop, calls=%fused_computation.29 | loop fusion | bytes 786432 | tf_op jit(solution)/shard_map/slice | solution.py:233
  1.7 2.1 %collective-permute-start = (f32[3,4,32,128]{3,2,1,0:T(8,128)S(1)}, f32[3,4,32,128]{3,2,1,0:T(8,128)S(1)}, u32[]{:S(2)}, u32[]{:S(2)}) collective-permute-start(f32[3,4,32,128]{3,2,1,0:T(8,128)S(1)} %get-tuple-element.16), channel_id=1, source_target_pairs={{0,32},{32,64},{64,96},{96,0},{1,33},{33,65},{65,97},{97,1},{2,34}... | collective-permute-start | bytes 589832 | tf_op jit(solution)/shard_map/ppermute | solution.py:228
  3.8 1.3 %collective-permute-start.1 = (f32[3,4,32,128]{3,2,1,0:T(8,128)S(1)}, f32[3,4,32,128]{3,2,1,0:T(8,128)S(1)}, u32[]{:S(2)}, u32[]{:S(2)}) collective-permute-start(f32[3,4,32,128]{3,2,1,0:T(8,128)S(1)} %get-tuple-element.15), channel_id=1, source_target_pairs={{0,96},{32,0},{64,32},{96,64},{1,97},{33,1},{65,33},{97,65},{2,98}... | collective-permute-start | bytes 589832 | tf_op jit(solution)/shard_map/ppermute | solution.py:228
  5.1 1.0 %fusion.7 = (f32[3,8,4,128]{3,2,1,0:T(4,128)S(1)}, f32[3,8,4,128]{3,2,1,0:T(4,128)S(1)}) fusion(f32[3,8,32,128]{3,2,1,0:T(8,128)} %velocity_ref.1), kind=kLoop, calls=%fused_computation.28 | loop fusion | bytes 196608 | tf_op jit(solution)/shard_map/slice | solution.py:234
  6.1 0.1 fusion.5
  6.2 3.1 %collective-permute-done.1.right_ref = f32[3,4,32,128]{3,2,1,0:T(8,128)S(1)} collective-permute-done((f32[3,4,32,128]{3,2,1,0:T(8,128)S(1)}, f32[3,4,32,128]{3,2,1,0:T(8,128)S(1)}, u32[]{:S(2)}, u32[]{:S(2)}) %collective-permute-start.1) | collective-permute-done | bytes 196640 | tf_op jit(solution)/shard_map/ppermute | solution.py:228
  9.3 0.0 collective-permute-done.left_ref
  9.4 3.4 %collective-permute-start.2 = (f32[3,12,4,128]{3,2,1,0:T(4,128)S(1)}, f32[3,12,4,128]{3,2,1,0:T(4,128)S(1)}, u32[]{:S(2)}, u32[]{:S(2)}) collective-permute-start(f32[3,12,4,128]{3,2,1,0:T(4,128)S(1)} %pad_maximum_fusion), channel_id=1, source_target_pairs={{0,1},{1,2},{2,3},{3,4},{4,5},{5,6},{6,7},{7,8},{8,9},{9,10},{10,1... | collective-permute-start | bytes 221192 | tf_op jit(solution)/shard_map/ppermute | solution.py:228
  12.8 0.1 collective-permute-start.3
  12.9 1.2 %collective-permute-done.2.behind_ref = f32[3,12,4,128]{3,2,1,0:T(4,128)S(1)} collective-permute-done((f32[3,12,4,128]{3,2,1,0:T(4,128)S(1)}, f32[3,12,4,128]{3,2,1,0:T(4,128)S(1)}, u32[]{:S(2)}, u32[]{:S(2)}) %collective-permute-start.2) | collective-permute-done | bytes 73760 | tf_op jit(solution)/shard_map/ppermute | solution.py:228
  14.2 2.8 %collective-permute-done.3.ahead_ref = f32[3,12,4,128]{3,2,1,0:T(4,128)S(1)} collective-permute-done((f32[3,12,4,128]{3,2,1,0:T(4,128)S(1)}, f32[3,12,4,128]{3,2,1,0:T(4,128)S(1)}, u32[]{:S(2)}, u32[]{:S(2)}) %collective-permute-start.3) | collective-permute-done | bytes 73760 | tf_op jit(solution)/shard_map/ppermute | solution.py:228
  16.9 12.3 %step_gram.1 = (f32[3,8,32,128]{3,2,1,0:T(8,128)}, f32[128,128]{1,0:T(8,128)S(1)}) custom-call(f32[3,8,32,128]{3,2,1,0:T(8,128)} %velocity_ref.1, f32[3,4,32,128]{3,2,1,0:T(8,128)S(1)} %collective-permute-done.left_ref, f32[3,4,32,128]{3,2,1,0:T(8,128)S(1)} %collective-permute-done.1.right_ref, f32[3,12,4,128]{3,2,1,0:T(4,128)S(1)} %collective-permute-done.2.behind_ref, ...), custom_call_target="tpu_custom_call" | custom-call | tf_op jit(solution)/shard_map/step_gram/pallas_call | solution.py:202
  29.2 1.5 %collective-permute-start.4 = (f32[64,128]{1,0:T(8,128)S(1)}, f32[64,128]{1,0:T(8,128)S(1)}, u32[]{:S(2)}, u32[]{:S(2)}) collective-permute-start(f32[64,128]{1,0:T(8,128)S(1)} %constant_dynamic-slice_fusion), channel_id=1, source_target_pairs={{0,1},{1,0},{2,3},{3,2},{4,5},{5,4},{6,7},{7,6},{8,9},{9,8},{10,11... | collective-permute-start | bytes 98312 | tf_op jit(solution)/shard_map/ppermute | solution.py:262
  30.8 0.9 %collective-permute-done.4 = f32[64,128]{1,0:T(8,128)S(1)} collective-permute-done((f32[64,128]{1,0:T(8,128)S(1)}, f32[64,128]{1,0:T(8,128)S(1)}, u32[]{:S(2)}, u32[]{:S(2)}) %collective-permute-start.4) | collective-permute-done | bytes 32800 | tf_op jit(solution)/shard_map/ppermute | solution.py:262
  31.6 0.2 collective-permute-start.6
  31.9 2.6 %collective-permute-start.7 = (f32[64,128]{1,0:T(8,128)S(1)}, f32[64,128]{1,0:T(8,128)S(1)}, u32[]{:S(2)}, u32[]{:S(2)}) collective-permute-start(f32[64,128]{1,0:T(8,128)S(1)} %dynamic-slice_add_fusion), channel_id=1, source_target_pairs={{0,6},{1,7},{2,0},{3,1},{4,2},{5,3},{6,4},{7,5},{8,14},{9,15},{10,... | collective-permute-start | bytes 98312 | tf_op jit(solution)/shard_map/ppermute | solution.py:271
  34.5 1.1 %collective-permute-start.5 = (f32[64,128]{1,0:T(8,128)S(1)}, f32[64,128]{1,0:T(8,128)S(1)}, u32[]{:S(2)}, u32[]{:S(2)}) collective-permute-start(f32[64,128]{1,0:T(8,128)S(1)} %dynamic-slice_add_fusion), channel_id=1, source_target_pairs={{0,4},{1,5},{2,6},{3,7},{4,0},{5,1},{6,2},{7,3},{8,12},{9,13},{10,... | collective-permute-start | bytes 98312 | tf_op jit(solution)/shard_map/ppermute | solution.py:271
  35.6 0.1 collective-permute-done.6
  35.7 0.0 collective-permute-done.7
  35.7 3.0 %collective-permute-done.5 = f32[64,128]{1,0:T(8,128)S(1)} collective-permute-done((f32[64,128]{1,0:T(8,128)S(1)}, f32[64,128]{1,0:T(8,128)S(1)}, u32[]{:S(2)}, u32[]{:S(2)}) %collective-permute-start.5) | collective-permute-done | bytes 32800 | tf_op jit(solution)/shard_map/ppermute | solution.py:271
  38.7 1.4 %collective-permute-start.9 = (f32[64,128]{1,0:T(8,128)S(1)}, f32[64,128]{1,0:T(8,128)S(1)}, u32[]{:S(2)}, u32[]{:S(2)}) collective-permute-start(f32[64,128]{1,0:T(8,128)S(1)} %add_add_fusion.2), channel_id=1, source_target_pairs={{0,8},{1,9},{2,10},{3,11},{4,12},{5,13},{6,14},{7,15},{8,16},{9,17... | collective-permute-start | bytes 98312 | tf_op jit(solution)/shard_map/ppermute | solution.py:271
  40.1 1.4 %collective-permute-start.10 = (f32[64,128]{1,0:T(8,128)S(1)}, f32[64,128]{1,0:T(8,128)S(1)}, u32[]{:S(2)}, u32[]{:S(2)}) collective-permute-start(f32[64,128]{1,0:T(8,128)S(1)} %add_add_fusion.2), channel_id=1, source_target_pairs={{0,24},{1,25},{2,26},{3,27},{4,28},{5,29},{6,30},{7,31},{8,0},{9,1... | collective-permute-start | bytes 98312 | tf_op jit(solution)/shard_map/ppermute | solution.py:271
  41.5 1.4 %collective-permute-start.8 = (f32[64,128]{1,0:T(8,128)S(1)}, f32[64,128]{1,0:T(8,128)S(1)}, u32[]{:S(2)}, u32[]{:S(2)}) collective-permute-start(f32[64,128]{1,0:T(8,128)S(1)} %add_add_fusion.2), channel_id=1, source_target_pairs={{0,16},{1,17},{2,18},{3,19},{4,20},{5,21},{6,22},{7,23},{8,24},{9,... | collective-permute-start | bytes 98312 | tf_op jit(solution)/shard_map/ppermute | solution.py:271
  42.9 0.0 collective-permute-done.9
  42.9 0.0 collective-permute-done.10
  42.9 3.0 %collective-permute-done.8 = f32[64,128]{1,0:T(8,128)S(1)} collective-permute-done((f32[64,128]{1,0:T(8,128)S(1)}, f32[64,128]{1,0:T(8,128)S(1)}, u32[]{:S(2)}, u32[]{:S(2)}) %collective-permute-start.8) | collective-permute-done | bytes 32800 | tf_op jit(solution)/shard_map/ppermute | solution.py:271
  45.9 1.3 %collective-permute-start.12 = (f32[64,128]{1,0:T(8,128)S(1)}, f32[64,128]{1,0:T(8,128)S(1)}, u32[]{:S(2)}, u32[]{:S(2)}) collective-permute-start(f32[64,128]{1,0:T(8,128)S(1)} %add_add_fusion.1), channel_id=1, source_target_pairs={{0,32},{32,64},{64,96},{96,0},{1,33},{33,65},{65,97},{97,1},{2,34}... | collective-permute-start | bytes 98312 | tf_op jit(solution)/shard_map/ppermute | solution.py:271
  47.2 1.7 %collective-permute-start.13 = (f32[64,128]{1,0:T(8,128)S(1)}, f32[64,128]{1,0:T(8,128)S(1)}, u32[]{:S(2)}, u32[]{:S(2)}) collective-permute-start(f32[64,128]{1,0:T(8,128)S(1)} %add_add_fusion.1), channel_id=1, source_target_pairs={{0,96},{32,0},{64,32},{96,64},{1,97},{33,1},{65,33},{97,65},{2,98}... | collective-permute-start | bytes 98312 | tf_op jit(solution)/shard_map/ppermute | solution.py:271
  48.9 1.1 %collective-permute-start.11 = (f32[64,128]{1,0:T(8,128)S(1)}, f32[64,128]{1,0:T(8,128)S(1)}, u32[]{:S(2)}, u32[]{:S(2)}) collective-permute-start(f32[64,128]{1,0:T(8,128)S(1)} %add_add_fusion.1), channel_id=1, source_target_pairs={{0,64},{32,96},{64,0},{96,32},{1,65},{33,97},{65,1},{97,33},{2,66}... | collective-permute-start | bytes 98312 | tf_op jit(solution)/shard_map/ppermute | solution.py:271
  50.0 0.1 collective-permute-done.12
  50.1 0.0 collective-permute-done.13
  50.1 3.0 %collective-permute-done.11 = f32[64,128]{1,0:T(8,128)S(1)} collective-permute-done((f32[64,128]{1,0:T(8,128)S(1)}, f32[64,128]{1,0:T(8,128)S(1)}, u32[]{:S(2)}, u32[]{:S(2)}) %collective-permute-start.11) | collective-permute-done | bytes 32800 | tf_op jit(solution)/shard_map/ppermute | solution.py:271
  53.2 5.0 %collective-permute-start.14 = (f32[64,128]{1,0:T(8,128)S(1)}, f32[64,128]{1,0:T(8,128)S(1)}, u32[]{:S(2)}, u32[]{:S(2)}) collective-permute-start(f32[64,128]{1,0:T(8,128)S(1)} %add_add_fusion), channel_id=1, source_target_pairs={{0,1},{1,0},{2,3},{3,2},{4,5},{5,4},{6,7},{7,6},{8,9},{9,8},{10,11... | collective-permute-start | bytes 98312 | tf_op jit(solution)/shard_map/ppermute | solution.py:262
  58.2 0.9 %collective-permute-done.14 = f32[64,128]{1,0:T(8,128)S(1)} collective-permute-done((f32[64,128]{1,0:T(8,128)S(1)}, f32[64,128]{1,0:T(8,128)S(1)}, u32[]{:S(2)}, u32[]{:S(2)}) %collective-permute-start.14) | collective-permute-done | bytes 32800 | tf_op jit(solution)/shard_map/ppermute | solution.py:262
  59.1 3.8 %upper_factor.1 = f32[128,128]{1,0:T(8,128)} custom-call(f32[128,128]{1,0:T(8,128)S(1)} %pad_maximum_fusion.2.gram_ref), custom_call_target="tpu_custom_call" | custom-call | tf_op jit(solution)/shard_map/upper_factor/pallas_call | solution.py:332
  (15 shorter events, 0.2 us)
Async XLA Ops:
  1.7 7.6 %collective-permute-start = (f32[3,4,32,128]{3,2,1,0:T(8,128)S(1)}, f32[3,4,32,128]{3,2,1,0:T(8,128)S(1)}, u32[]{:S(2)}, u32[]{:S(2)}) collective-permute-start(f32[3,4,32,128]{3,2,1,0:T(8,128)S(1)} %get-tuple-element.16), channel_id=1, source_target_pairs={{0,32},{32,64},{64,96},{96,0},{1,33},{33,65},{65,97},{97,1},{2,34}... | collective-permute-start | bytes 589832 | tf_op jit(solution)/shard_map/ppermute | solution.py:228
  3.8 5.5 %collective-permute-start.1 = (f32[3,4,32,128]{3,2,1,0:T(8,128)S(1)}, f32[3,4,32,128]{3,2,1,0:T(8,128)S(1)}, u32[]{:S(2)}, u32[]{:S(2)}) collective-permute-start(f32[3,4,32,128]{3,2,1,0:T(8,128)S(1)} %get-tuple-element.15), channel_id=1, source_target_pairs={{0,96},{32,0},{64,32},{96,64},{1,97},{33,1},{65,33},{97,65},{2,98}... | collective-permute-start | bytes 589832 | tf_op jit(solution)/shard_map/ppermute | solution.py:228
  9.4 4.8 %collective-permute-start.2 = (f32[3,12,4,128]{3,2,1,0:T(4,128)S(1)}, f32[3,12,4,128]{3,2,1,0:T(4,128)S(1)}, u32[]{:S(2)}, u32[]{:S(2)}) collective-permute-start(f32[3,12,4,128]{3,2,1,0:T(4,128)S(1)} %pad_maximum_fusion), channel_id=1, source_target_pairs={{0,1},{1,2},{2,3},{3,4},{4,5},{5,6},{6,7},{7,8},{8,9},{9,10},{10,1... | collective-permute-start | bytes 221192 | tf_op jit(solution)/shard_map/ppermute | solution.py:228
  12.8 4.1 %collective-permute-start.3 = (f32[3,12,4,128]{3,2,1,0:T(4,128)S(1)}, f32[3,12,4,128]{3,2,1,0:T(4,128)S(1)}, u32[]{:S(2)}, u32[]{:S(2)}) collective-permute-start(f32[3,12,4,128]{3,2,1,0:T(4,128)S(1)} %pad_maximum_fusion.1), channel_id=1, source_target_pairs={{0,31},{1,0},{2,1},{3,2},{4,3},{5,4},{6,5},{7,6},{8,7},{9,8},{10,9... | collective-permute-start | bytes 221192 | tf_op jit(solution)/shard_map/ppermute | solution.py:228
  29.2 2.4 %collective-permute-start.4 = (f32[64,128]{1,0:T(8,128)S(1)}, f32[64,128]{1,0:T(8,128)S(1)}, u32[]{:S(2)}, u32[]{:S(2)}) collective-permute-start(f32[64,128]{1,0:T(8,128)S(1)} %constant_dynamic-slice_fusion), channel_id=1, source_target_pairs={{0,1},{1,0},{2,3},{3,2},{4,5},{5,4},{6,7},{7,6},{8,9},{9,8},{10,11... | collective-permute-start | bytes 98312 | tf_op jit(solution)/shard_map/ppermute | solution.py:262
  31.6 4.1 %collective-permute-start.6 = (f32[64,128]{1,0:T(8,128)S(1)}, f32[64,128]{1,0:T(8,128)S(1)}, u32[]{:S(2)}, u32[]{:S(2)}) collective-permute-start(f32[64,128]{1,0:T(8,128)S(1)} %dynamic-slice_add_fusion), channel_id=1, source_target_pairs={{0,2},{1,3},{2,4},{3,5},{4,6},{5,7},{6,0},{7,1},{8,10},{9,11},{10,... | collective-permute-start | bytes 98312 | tf_op jit(solution)/shard_map/ppermute | solution.py:271
  31.9 3.8 %collective-permute-start.7 = (f32[64,128]{1,0:T(8,128)S(1)}, f32[64,128]{1,0:T(8,128)S(1)}, u32[]{:S(2)}, u32[]{:S(2)}) collective-permute-start(f32[64,128]{1,0:T(8,128)S(1)} %dynamic-slice_add_fusion), channel_id=1, source_target_pairs={{0,6},{1,7},{2,0},{3,1},{4,2},{5,3},{6,4},{7,5},{8,14},{9,15},{10,... | collective-permute-start | bytes 98312 | tf_op jit(solution)/shard_map/ppermute | solution.py:271
  34.5 4.3 %collective-permute-start.5 = (f32[64,128]{1,0:T(8,128)S(1)}, f32[64,128]{1,0:T(8,128)S(1)}, u32[]{:S(2)}, u32[]{:S(2)}) collective-permute-start(f32[64,128]{1,0:T(8,128)S(1)} %dynamic-slice_add_fusion), channel_id=1, source_target_pairs={{0,4},{1,5},{2,6},{3,7},{4,0},{5,1},{6,2},{7,3},{8,12},{9,13},{10,... | collective-permute-start | bytes 98312 | tf_op jit(solution)/shard_map/ppermute | solution.py:271
  38.7 4.2 %collective-permute-start.9 = (f32[64,128]{1,0:T(8,128)S(1)}, f32[64,128]{1,0:T(8,128)S(1)}, u32[]{:S(2)}, u32[]{:S(2)}) collective-permute-start(f32[64,128]{1,0:T(8,128)S(1)} %add_add_fusion.2), channel_id=1, source_target_pairs={{0,8},{1,9},{2,10},{3,11},{4,12},{5,13},{6,14},{7,15},{8,16},{9,17... | collective-permute-start | bytes 98312 | tf_op jit(solution)/shard_map/ppermute | solution.py:271
  40.1 2.8 %collective-permute-start.10 = (f32[64,128]{1,0:T(8,128)S(1)}, f32[64,128]{1,0:T(8,128)S(1)}, u32[]{:S(2)}, u32[]{:S(2)}) collective-permute-start(f32[64,128]{1,0:T(8,128)S(1)} %add_add_fusion.2), channel_id=1, source_target_pairs={{0,24},{1,25},{2,26},{3,27},{4,28},{5,29},{6,30},{7,31},{8,0},{9,1... | collective-permute-start | bytes 98312 | tf_op jit(solution)/shard_map/ppermute | solution.py:271
  41.5 4.4 %collective-permute-start.8 = (f32[64,128]{1,0:T(8,128)S(1)}, f32[64,128]{1,0:T(8,128)S(1)}, u32[]{:S(2)}, u32[]{:S(2)}) collective-permute-start(f32[64,128]{1,0:T(8,128)S(1)} %add_add_fusion.2), channel_id=1, source_target_pairs={{0,16},{1,17},{2,18},{3,19},{4,20},{5,21},{6,22},{7,23},{8,24},{9,... | collective-permute-start | bytes 98312 | tf_op jit(solution)/shard_map/ppermute | solution.py:271
  45.9 4.2 %collective-permute-start.12 = (f32[64,128]{1,0:T(8,128)S(1)}, f32[64,128]{1,0:T(8,128)S(1)}, u32[]{:S(2)}, u32[]{:S(2)}) collective-permute-start(f32[64,128]{1,0:T(8,128)S(1)} %add_add_fusion.1), channel_id=1, source_target_pairs={{0,32},{32,64},{64,96},{96,0},{1,33},{33,65},{65,97},{97,1},{2,34}... | collective-permute-start | bytes 98312 | tf_op jit(solution)/shard_map/ppermute | solution.py:271
  47.2 2.9 %collective-permute-start.13 = (f32[64,128]{1,0:T(8,128)S(1)}, f32[64,128]{1,0:T(8,128)S(1)}, u32[]{:S(2)}, u32[]{:S(2)}) collective-permute-start(f32[64,128]{1,0:T(8,128)S(1)} %add_add_fusion.1), channel_id=1, source_target_pairs={{0,96},{32,0},{64,32},{96,64},{1,97},{33,1},{65,33},{97,65},{2,98}... | collective-permute-start | bytes 98312 | tf_op jit(solution)/shard_map/ppermute | solution.py:271
  48.9 4.3 %collective-permute-start.11 = (f32[64,128]{1,0:T(8,128)S(1)}, f32[64,128]{1,0:T(8,128)S(1)}, u32[]{:S(2)}, u32[]{:S(2)}) collective-permute-start(f32[64,128]{1,0:T(8,128)S(1)} %add_add_fusion.1), channel_id=1, source_target_pairs={{0,64},{32,96},{64,0},{96,32},{1,65},{33,97},{65,1},{97,33},{2,66}... | collective-permute-start | bytes 98312 | tf_op jit(solution)/shard_map/ppermute | solution.py:271
  53.2 5.9 %collective-permute-start.14 = (f32[64,128]{1,0:T(8,128)S(1)}, f32[64,128]{1,0:T(8,128)S(1)}, u32[]{:S(2)}, u32[]{:S(2)}) collective-permute-start(f32[64,128]{1,0:T(8,128)S(1)} %add_add_fusion), channel_id=1, source_target_pairs={{0,1},{1,0},{2,3},{3,2},{4,5},{5,4},{6,7},{7,6},{8,9},{9,8},{10,11... | collective-permute-start | bytes 98312 | tf_op jit(solution)/shard_map/ppermute | solution.py:262

commit v5 on v4

--- a/solution.py
+++ b/solution.py
@@ -62,6 +62,32 @@
     return results
 
 
+PACKED_ROWS = 80
+
+
+def pack_gram(gram, packed_ref):
+    half = gram.shape[0] // 2
+    first, second = gram[:half], gram[half:]
+    row = lax.broadcasted_iota(jnp.int32, first.shape, 0)
+    lane = lax.broadcasted_iota(jnp.int32, first.shape, 1)
+    packed_ref[0:half, :] = jnp.where(lane < row, pltpu.roll(second, half, 1), first)
+    diagonal = jnp.sum(jnp.where(lane == row + half, second, 0.0), axis=0, keepdims=True)
+    packed_ref[half:, :] = jnp.broadcast_to(diagonal, (PACKED_ROWS - half, gram.shape[1]))
+
+
+def unpack_gram(packed_ref, gram_ref):
+    size = gram_ref.shape[0]
+    half = size // 2
+    kept = packed_ref[0:half, :]
+    turned = jnp.concatenate([kept, jnp.zeros_like(kept)], 0).T[0:half]
+    row = lax.broadcasted_iota(jnp.int32, kept.shape, 0)
+    lane = lax.broadcasted_iota(jnp.int32, kept.shape, 1)
+    gram_ref[0:half, :] = jnp.where(lane < row, turned, kept)
+    second = pltpu.roll(jnp.where(lane < row, kept, turned), half, 1)
+    diagonal = jnp.broadcast_to(packed_ref[half : half + 1, :], kept.shape)
+    gram_ref[half:, :] = jnp.where(lane == row + half, diagonal, second)
+
+
 CHUNKS = (160, 128, 96)
 MXU_STEP = 32
 
@@ -77,7 +103,7 @@
     basis_ref,
     stored_ref,
     advanced_ref,
-    gram_ref,
+    packed_ref,
     block,
     wide,
     folded,
@@ -183,7 +209,8 @@
         even = wide[h, pl.ds(0, 128, stride=2), :]
         odd = wide[h, pl.ds(1, 128, stride=2), :]
         folded[128 * h : 128 * (h + 1)] = (jnp.where(lane % 2 == 0, even, odd) * scale).T
-    gram_ref[...] = folded[pl.ds(0, 128, stride=2), :] + folded[pl.ds(1, 128, stride=2), :]
+    gram = folded[pl.ds(0, 128, stride=2), :] + folded[pl.ds(1, 128, stride=2), :]
+    pack_gram(gram, packed_ref)
     leave.wait()
 
 
@@ -203,7 +230,7 @@
         functools.partial(step_kernel, scale),
         out_shape=(
             jax.ShapeDtypeStruct(velocity.shape, jnp.float32),
-            jax.ShapeDtypeStruct((128, 128), jnp.float32),
+            jax.ShapeDtypeStruct((PACKED_ROWS, 128), jnp.float32),
         ),
         in_specs=[hbm, free, free, free, free, vmem, hbm, hbm],
         out_specs=(hbm, vmem),
@@ -262,27 +289,20 @@
     return lax.ppermute(part, "gy", [(i, i ^ 1) for i in range(count)])
 
 
-def ring_sum(part, axis, count, stride):
-    def target(i, d):
-        place = (i // stride) % 4
-        return i + ((place + d) % 4 - place) * stride
-
-    moved = [
-        lax.ppermute(part, axis, [(i, target(i, d)) for i in range(count)]) for d in (1, 2, 3)
-    ]
-    return (part + moved[1]) + (moved[0] + moved[2])
-
-
-def total_gram(gram):
+def group_sum(part, axis, members, groups=None):
+    copies = jnp.broadcast_to(part[None], (members, *part.shape))
+    return lax.all_to_all(copies, axis, 0, 0, axis_index_groups=groups).sum(0)
+
+
+def total_gram(packed):
     count = lax.axis_size("gy")
-    half = gram.shape[0] // 2
+    half = packed.shape[0] // 2
     core = lax.axis_index("gy") % 2
-    mine = lax.dynamic_slice_in_dim(gram, core * half, half, 0)
-    other = lax.dynamic_slice_in_dim(gram, (1 - core) * half, half, 0)
+    mine = lax.dynamic_slice_in_dim(packed, core * half, half, 0)
+    other = lax.dynamic_slice_in_dim(packed, (1 - core) * half, half, 0)
     part = mine + swap_cores(other, count)
-    part = ring_sum(part, "gy", count, 2)
-    part = ring_sum(part, "gy", count, 8)
-    part = ring_sum(part, "gx", 4, 1)
+    part = group_sum(part, "gy", count // 2, [list(range(c, count, 2)) for c in range(2)])
+    part = group_sum(part, "gx", lax.axis_size("gx"))
     rest = swap_cores(part, count)
     low = jnp.where(core == 0, part, rest)
     high = jnp.where(core == 0, rest, part)
@@ -292,9 +312,9 @@
 PANEL = 16
 
 
-def factor_kernel(gram_ref, factor_ref, work):
-    size = gram_ref.shape[0]
-    work[...] = gram_ref[...]
+def factor_kernel(packed_ref, factor_ref, work):
+    size = work.shape[0]
+    unpack_gram(packed_ref, work)
     row = lax.broadcasted_iota(jnp.int32, (PANEL, size), 0)
     lane = lax.broadcasted_iota(jnp.int32, (PANEL, size), 1)
     for begin in range(0, size, PANEL):
@@ -328,16 +348,17 @@
             work[end:, :] = work[end:, :] - product[end:, :]
 
 
-def upper_factor(gram):
+def upper_factor(packed):
+    shape = (packed.shape[1], packed.shape[1])
     return pl.pallas_call(
         factor_kernel,
-        out_shape=jax.ShapeDtypeStruct(gram.shape, jnp.float32),
+        out_shape=jax.ShapeDtypeStruct(shape, jnp.float32),
         in_specs=[pl.BlockSpec(memory_space=pltpu.VMEM)],
         out_specs=pl.BlockSpec(memory_space=pltpu.VMEM),
-        scratch_shapes=[pltpu.VMEM(gram.shape, jnp.float32)],
+        scratch_shapes=[pltpu.VMEM(shape, jnp.float32)],
         compiler_params=pltpu.CompilerParams(vmem_limit_bytes=8 * 2**20),
         name="upper_factor",
-    )(gram)
+    )(packed)
 
 
 def local(velocity, basis, snapshots):
@@ -351,8 +372,8 @@
     )
     halos = exchange(velocity)
     weights = wall_rows(velocity.shape[3])
-    advanced, gram = step_and_gram(velocity, halos, weights, basis, snapshots, 1.0 / total_rows)
-    factor = upper_factor(total_gram(gram))
+    advanced, packed = step_and_gram(velocity, halos, weights, basis, snapshots, 1.0 / total_rows)
+    factor = upper_factor(total_gram(packed))
     return (advanced, factor)
 
 

time: 63.1 us -> 63.9 us (1.013)
  blocking collectives: 0 us -> 21.4 us
  starting transfers between devices: 25.6 us -> 11.6 us
  waiting for transfers between devices: 18.2 us -> 11.3 us
    all_to_all x0 -> x2, blocking collectives: none -> 21.4 us  [group_sum(): return lax.all_to_all(copies, axis, 0, 0, axis_index_groups=groups).sum(0)]
    ppermute x9 -> x0, starting transfers between devices: 12.2 us -> none  [ring_sum(): lax.ppermute(part, axis, [(i, target(i, d)) for i in range(count)])]
    ppermute x9 -> x0, waiting for transfers between devices: 9.35 us -> none  [ring_sum(): lax.ppermute(part, axis, [(i, target(i, d)) for i in range(count)])]
    ppermute x4, waiting for transfers between devices: 7.09 us -> 9.63 us  [shift(): lax.ppermute(part, axis, [(i, (i + step) % count) for i in range(count)])]
    ppermute x2, starting transfers between devices: 6.55 us -> 4.72 us  [swap_cores(): return lax.ppermute(part, 'gy', [(i, i ^ 1) for i in range(count)])]
  transfers between devices with their start and end apart: 15 -> 6, of which waited for: 10 -> 6; matrix products, arithmetic and copies ran while one was open for 2% -> 2% of each run, Pallas kernels for 0% -> 0%
where the time goes in v5:
time: 63.9 us; the launch traced here: 63.7 us
  blocking collectives  21.4 us (33%)
  Pallas kernels  16.4 us (26%)
  starting transfers between devices  11.6 us (18%)
  waiting for transfers between devices  11.3 us (18%)
  local copies, waits for them, and re-layouts  2.11 us (3%)
  between operations  0.73 us (1%)
    all_to_all x2, blocking collectives, group_sum(): return lax.all_to_all(copies, axis, 0, 0, axis_index_groups=groups).sum(0)  21.4 us
    pallas_call x1, Pallas kernels, step_and_gram(): pl.pallas_call(functools.partial(step_kernel, scale), out_shape=(jax.Shap...  12.3 us
    ppermute x4, waiting for transfers between devices, shift(): lax.ppermute(part, axis, [(i, (i + step) % count) for i in range(count)])  9.63 us
    ppermute x4, starting transfers between devices, shift(): lax.ppermute(part, axis, [(i, (i + step) % count) for i in range(count)])  6.84 us
    ppermute x2, starting transfers between devices, swap_cores(): return lax.ppermute(part, 'gy', [(i, i ^ 1) for i in range(count)])  4.72 us
    pallas_call x1, Pallas kernels, upper_factor(): pl.pallas_call(factor_kernel, out_shape=jax.ShapeDtypeStruct(shape, jnp.f...  4.04 us
    ppermute x2, waiting for transfers between devices, swap_cores(): return lax.ppermute(part, 'gy', [(i, i ^ 1) for i in range(count)])  1.69 us
  transfers between devices with their start and end apart: 6, of which 6 were waited for; matrix products, arithmetic and copies ran while one was open for 2% of the time, Pallas kernels for 0%

profile of v5, /device:TPU:1, one launch (start us, length us, event | category | flops | bytes accessed | tf_op | source)
XLA Modules:
  0.0 63.7 jit_solution(10500333900803306062)
XLA Ops:
  0.6 1.1 %fusion.8 = (f32[3,4,32,128]{3,2,1,0:T(8,128)S(1)}, f32[3,4,32,128]{3,2,1,0:T(8,128)S(1)}) fusion(f32[3,8,32,128]{3,2,1,0:T(8,128)} %velocity_ref.1), kind=kLoop, calls=%fused_computation.26 | loop fusion | bytes 786432 | tf_op jit(solution)/shard_map/slice | solution.py:260
  1.7 3.4 %collective-permute-start.1 = (f32[3,4,32,128]{3,2,1,0:T(8,128)S(1)}, f32[3,4,32,128]{3,2,1,0:T(8,128)S(1)}, u32[]{:S(2)}, u32[]{:S(2)}) collective-permute-start(f32[3,4,32,128]{3,2,1,0:T(8,128)S(1)} %get-tuple-element.15), channel_id=1, source_target_pairs={{0,96},{32,0},{64,32},{96,64},{1,97},{33,1},{65,33},{97,65},{2,98}... | collective-permute-start | bytes 589832 | tf_op jit(solution)/shard_map/ppermute | solution.py:255
  5.1 0.0 collective-permute-start
  5.1 1.0 %fusion.7 = (f32[3,8,4,128]{3,2,1,0:T(4,128)S(1)}, f32[3,8,4,128]{3,2,1,0:T(4,128)S(1)}) fusion(f32[3,8,32,128]{3,2,1,0:T(8,128)} %velocity_ref.1), kind=kLoop, calls=%fused_computation.25 | loop fusion | bytes 196608 | tf_op jit(solution)/shard_map/slice | solution.py:261
  6.0 0.1 fusion.5
  6.1 2.5 %collective-permute-done.1.right_ref = f32[3,4,32,128]{3,2,1,0:T(8,128)S(1)} collective-permute-done((f32[3,4,32,128]{3,2,1,0:T(8,128)S(1)}, f32[3,4,32,128]{3,2,1,0:T(8,128)S(1)}, u32[]{:S(2)}, u32[]{:S(2)}) %collective-permute-start.1) | collective-permute-done | bytes 196640 | tf_op jit(solution)/shard_map/ppermute | solution.py:255
  8.6 3.1 %collective-permute-done.left_ref = f32[3,4,32,128]{3,2,1,0:T(8,128)S(1)} collective-permute-done((f32[3,4,32,128]{3,2,1,0:T(8,128)S(1)}, f32[3,4,32,128]{3,2,1,0:T(8,128)S(1)}, u32[]{:S(2)}, u32[]{:S(2)}) %collective-permute-start) | collective-permute-done | bytes 196640 | tf_op jit(solution)/shard_map/ppermute | solution.py:255
  11.8 3.4 %collective-permute-start.2 = (f32[3,12,4,128]{3,2,1,0:T(4,128)S(1)}, f32[3,12,4,128]{3,2,1,0:T(4,128)S(1)}, u32[]{:S(2)}, u32[]{:S(2)}) collective-permute-start(f32[3,12,4,128]{3,2,1,0:T(4,128)S(1)} %pad_maximum_fusion), channel_id=1, source_target_pairs={{0,1},{1,2},{2,3},{3,4},{4,5},{5,6},{6,7},{7,8},{8,9},{9,10},{10,1... | collective-permute-start | bytes 221192 | tf_op jit(solution)/shard_map/ppermute | solution.py:255
  15.2 0.1 collective-permute-start.3
  15.4 1.2 %collective-permute-done.2.behind_ref = f32[3,12,4,128]{3,2,1,0:T(4,128)S(1)} collective-permute-done((f32[3,12,4,128]{3,2,1,0:T(4,128)S(1)}, f32[3,12,4,128]{3,2,1,0:T(4,128)S(1)}, u32[]{:S(2)}, u32[]{:S(2)}) %collective-permute-start.2) | collective-permute-done | bytes 73760 | tf_op jit(solution)/shard_map/ppermute | solution.py:255
  16.6 2.8 %collective-permute-done.3.ahead_ref = f32[3,12,4,128]{3,2,1,0:T(4,128)S(1)} collective-permute-done((f32[3,12,4,128]{3,2,1,0:T(4,128)S(1)}, f32[3,12,4,128]{3,2,1,0:T(4,128)S(1)}, u32[]{:S(2)}, u32[]{:S(2)}) %collective-permute-start.3) | collective-permute-done | bytes 73760 | tf_op jit(solution)/shard_map/ppermute | solution.py:255
  19.4 12.3 %step_gram.1 = (f32[3,8,32,128]{3,2,1,0:T(8,128)}, f32[80,128]{1,0:T(8,128)S(1)}) custom-call(f32[3,8,32,128]{3,2,1,0:T(8,128)} %velocity_ref.1, f32[3,4,32,128]{3,2,1,0:T(8,128)S(1)} %collective-permute-done.left_ref, f32[3,4,32,128]{3,2,1,0:T(8,128)S(1)} %collective-permute-done.1.right_ref, f32[3,12,4,128]{3,2,1,0:T(4,128)S(1)} %collective-permute-done.2.behind_ref, ...), custom_call_target="tpu_custom_call" | custom-call | tf_op jit(solution)/shard_map/step_gram/pallas_call | solution.py:229
  31.7 1.5 %collective-permute-start.4 = (f32[40,128]{1,0:T(8,128)S(1)}, f32[40,128]{1,0:T(8,128)S(1)}, u32[]{:S(2)}, u32[]{:S(2)}) collective-permute-start(f32[40,128]{1,0:T(8,128)S(1)} %constant_dynamic-slice_fusion), channel_id=1, source_target_pairs={{0,1},{1,0},{2,3},{3,2},{4,5},{5,4},{6,7},{7,6},{8,9},{9,8},{10,11... | collective-permute-start | bytes 61448 | tf_op jit(solution)/shard_map/ppermute | solution.py:289
  33.3 0.8 %collective-permute-done.4 = f32[40,128]{1,0:T(8,128)S(1)} collective-permute-done((f32[40,128]{1,0:T(8,128)S(1)}, f32[40,128]{1,0:T(8,128)S(1)}, u32[]{:S(2)}, u32[]{:S(2)}) %collective-permute-start.4) | collective-permute-done | bytes 20512 | tf_op jit(solution)/shard_map/ppermute | solution.py:289
  34.2 14.4 %all_to_all.10 = f32[16,40,128]{2,1,0:T(8,128)S(1)} all-to-all(f32[16,40,128]{2,1,0:T(8,128)S(1)} %broadcast_in_dim.20), channel_id=1, replica_groups={{0,2,4,6,8,10,12,14,16,18,20,22,24,26,28,30},{1,3,5,7,9,11,13,15,17,19,..., dimensions={0} | all-to-all | bytes 655360 | tf_op jit(solution)/shard_map/all_to_all | solution.py:294
  48.6 6.9 %all_to_all.11 = f32[4,40,128]{2,1,0:T(8,128)S(1)} all-to-all(f32[4,40,128]{2,1,0:T(8,128)S(1)} %broadcast_in_dim.21), channel_id=1, replica_groups=mesh['gx'=4,'gy'=32] {'gx'}, dimensions={0} | all-to-all | bytes 163840 | tf_op jit(solution)/shard_map/all_to_all | solution.py:294
  55.6 3.2 %collective-permute-start.5 = (f32[40,128]{1,0:T(8,128)S(1)}, f32[40,128]{1,0:T(8,128)S(1)}, u32[]{:S(2)}, u32[]{:S(2)}) collective-permute-start(f32[40,128]{1,0:T(8,128)S(1)} %reduce_sum.19), channel_id=1, source_target_pairs={{0,1},{1,0},{2,3},{3,2},{4,5},{5,4},{6,7},{7,6},{8,9},{9,8},{10,11... | collective-permute-start | bytes 61448 | tf_op jit(solution)/shard_map/ppermute | solution.py:289
  58.8 0.8 %collective-permute-done.5 = f32[40,128]{1,0:T(8,128)S(1)} collective-permute-done((f32[40,128]{1,0:T(8,128)S(1)}, f32[40,128]{1,0:T(8,128)S(1)}, u32[]{:S(2)}, u32[]{:S(2)}) %collective-permute-start.5) | collective-permute-done | bytes 20512 | tf_op jit(solution)/shard_map/ppermute | solution.py:289
  59.6 4.0 %upper_factor.1 = f32[128,128]{1,0:T(8,128)} custom-call(f32[80,128]{1,0:T(8,128)S(1)} %pad_maximum_fusion.2.packed_ref), custom_call_target="tpu_custom_call" | custom-call | tf_op jit(solution)/shard_map/upper_factor/pallas_call | solution.py:353
  (16 shorter events, 0.2 us)
Async XLA Ops:
  1.7 7.0 %collective-permute-start.1 = (f32[3,4,32,128]{3,2,1,0:T(8,128)S(1)}, f32[3,4,32,128]{3,2,1,0:T(8,128)S(1)}, u32[]{:S(2)}, u32[]{:S(2)}) collective-permute-start(f32[3,4,32,128]{3,2,1,0:T(8,128)S(1)} %get-tuple-element.15), channel_id=1, source_target_pairs={{0,96},{32,0},{64,32},{96,64},{1,97},{33,1},{65,33},{97,65},{2,98}... | collective-permute-start | bytes 589832 | tf_op jit(solution)/shard_map/ppermute | solution.py:255
  5.1 6.7 %collective-permute-start = (f32[3,4,32,128]{3,2,1,0:T(8,128)S(1)}, f32[3,4,32,128]{3,2,1,0:T(8,128)S(1)}, u32[]{:S(2)}, u32[]{:S(2)}) collective-permute-start(f32[3,4,32,128]{3,2,1,0:T(8,128)S(1)} %get-tuple-element.16), channel_id=1, source_target_pairs={{0,32},{32,64},{64,96},{96,0},{1,33},{33,65},{65,97},{97,1},{2,34}... | collective-permute-start | bytes 589832 | tf_op jit(solution)/shard_map/ppermute | solution.py:255
  11.8 4.8 %collective-permute-start.2 = (f32[3,12,4,128]{3,2,1,0:T(4,128)S(1)}, f32[3,12,4,128]{3,2,1,0:T(4,128)S(1)}, u32[]{:S(2)}, u32[]{:S(2)}) collective-permute-start(f32[3,12,4,128]{3,2,1,0:T(4,128)S(1)} %pad_maximum_fusion), channel_id=1, source_target_pairs={{0,1},{1,2},{2,3},{3,4},{4,5},{5,6},{6,7},{7,8},{8,9},{9,10},{10,1... | collective-permute-start | bytes 221192 | tf_op jit(solution)/shard_map/ppermute | solution.py:255
  15.2 4.1 %collective-permute-start.3 = (f32[3,12,4,128]{3,2,1,0:T(4,128)S(1)}, f32[3,12,4,128]{3,2,1,0:T(4,128)S(1)}, u32[]{:S(2)}, u32[]{:S(2)}) collective-permute-start(f32[3,12,4,128]{3,2,1,0:T(4,128)S(1)} %pad_maximum_fusion.1), channel_id=1, source_target_pairs={{0,31},{1,0},{2,1},{3,2},{4,3},{5,4},{6,5},{7,6},{8,7},{9,8},{10,9... | collective-permute-start | bytes 221192 | tf_op jit(solution)/shard_map/ppermute | solution.py:255
  31.7 2.4 %collective-permute-start.4 = (f32[40,128]{1,0:T(8,128)S(1)}, f32[40,128]{1,0:T(8,128)S(1)}, u32[]{:S(2)}, u32[]{:S(2)}) collective-permute-start(f32[40,128]{1,0:T(8,128)S(1)} %constant_dynamic-slice_fusion), channel_id=1, source_target_pairs={{0,1},{1,0},{2,3},{3,2},{4,5},{5,4},{6,7},{7,6},{8,9},{9,8},{10,11... | collective-permute-start | bytes 61448 | tf_op jit(solution)/shard_map/ppermute | solution.py:289
  55.6 4.0 %collective-permute-start.5 = (f32[40,128]{1,0:T(8,128)S(1)}, f32[40,128]{1,0:T(8,128)S(1)}, u32[]{:S(2)}, u32[]{:S(2)}) collective-permute-start(f32[40,128]{1,0:T(8,128)S(1)} %reduce_sum.19), channel_id=1, source_target_pairs={{0,1},{1,0},{2,3},{3,2},{4,5},{5,4},{6,7},{7,6},{8,9},{9,8},{10,11... | collective-permute-start | bytes 61448 | tf_op jit(solution)/shard_map/ppermute | solution.py:289

commit v6 on v5

--- a/solution.py
+++ b/solution.py
@@ -7,6 +7,7 @@
 from jax.experimental import pallas as pl
 from jax.experimental.pallas import tpu as pltpu
 from jax.sharding import PartitionSpec as P
+
 
 TIME_STEP = 0.0002
 VISCOSITY = 0.005
@@ -88,7 +89,7 @@
     gram_ref[half:, :] = jnp.where(lane == row + half, diagonal, second)
 
 
-CHUNKS = (160, 128, 96)
+CHUNKS = (128, 128, 128)
 MXU_STEP = 32
 
 
@@ -134,41 +135,55 @@
     for halo in halos:
         halo.start()
 
-    def issue(q):
+    def send(q, source, column, place):
         span = pl.ds(starts[q], CHUNKS[q])
-
-        def send(source, column):
-            pltpu.make_async_copy(
-                source.at[span], block.at[span, pl.ds(pl.multiple_of(2 * column, 2), 2)], sems.at[q]
-            ).start()
-
-        def from_basis(c, carry):
-            send(basis_ref.at[c], c)
-            return carry
-
-        def from_stored(c, carry):
-            send(stored_ref.at[c], n_basis + c)
-            return carry
-
-        lax.fori_loop(0, n_basis, from_basis, 0, unroll=8)
-        lax.fori_loop(0, n_stored, from_stored, 0, unroll=9)
-
-    for q in range(len(CHUNKS)):
-        issue(q)
+        pltpu.make_async_copy(
+            source.at[column, span],
+            block.at[span, pl.ds(pl.multiple_of(2 * (place + column), 2), 2)],
+            sems.at[q],
+        ).start()
+
+    def issue_part(q, part, parts):
+        for source, place in ((basis_ref, 0), (stored_ref, n_basis)):
+            share = source.shape[0] // parts
+            for i in range(share):
+                send(q, source, part * share + i, place)
+
+    def issue_rest(q, parts):
+        for source, place in ((basis_ref, 0), (stored_ref, n_basis)):
+            for column in range(source.shape[0] // parts * parts, source.shape[0]):
+                send(q, source, column, place)
+
+    def section_plane(x):
+        for c, (center, change) in enumerate(tendency(field, x + 2, 2, length_z + 8, weights)):
+            section[c, x, pl.ds(0, length_z + 8), :] = center + TIME_STEP * change
+
+    @pl.loop(0, 8)
+    def _(part):
+        issue_part(0, part, 8)
+
+    issue_rest(0, 8)
     for halo in halos:
         halo.wait()
 
     weights = [weights_ref[i : i + 1, :] for i in range(6)]
 
-    @pl.loop(0, length_x + 4)
-    def _(x):
-        for c, (center, change) in enumerate(tendency(field, x + 2, 2, length_z + 8, weights)):
-            section[c, x, pl.ds(0, length_z + 8), :] = center + TIME_STEP * change
-
-    last = 2 * (n_basis + n_stored)
-
     @pl.loop(0, length_x)
     def _(x):
+        issue_part(1, x, length_x)
+        section_plane(x)
+
+    issue_rest(1, length_x)
+
+    @pl.loop(length_x, length_x + 4)
+    def _(x):
+        section_plane(x)
+
+    last = 2 * (n_basis + n_stored)
+
+    @pl.loop(0, length_x)
+    def _(x):
+        issue_part(2, x, length_x)
         for c, (center, change) in enumerate(tendency(section, x + 2, 2, length_z, weights)):
             begin = field[c, x + 4, pl.ds(4, length_z), :]
             end = 0.5 * (begin + center + TIME_STEP * change)
@@ -177,6 +192,8 @@
             pair = (c * length_x + x) * (length_z // 2)
             for j in range(length_z // 2):
                 block[pair + j, last : last + 2, :] = rounded[2 * j : 2 * j + 2, :]
+
+    issue_rest(2, length_x)
 
     leave = pltpu.make_async_copy(advanced, advanced_ref, out_sem.at[0])
     leave.start()

time: 63.9 us -> 63.2 us (0.989)
  Pallas kernels: 16.4 us -> 15.7 us
    pallas_call x1, Pallas kernels: 12.3 us -> 11.7 us  [step_and_gram(): pl.pallas_call(functools.partial(step_kernel, scale), out_shape=(jax.Shap...]
where the time goes in v6:
time: 63.2 us; the launch traced here: 63 us
  blocking collectives  21.4 us (34%)
  Pallas kernels  15.7 us (25%)
  starting transfers between devices  11.6 us (18%)
  waiting for transfers between devices  11.3 us (18%)
  local copies, waits for them, and re-layouts  2.11 us (3%)
  between operations  0.73 us (1%)
    all_to_all x2, blocking collectives, group_sum(): return lax.all_to_all(copies, axis, 0, 0, axis_index_groups=groups).sum(0)  21.4 us
    pallas_call x1, Pallas kernels, step_and_gram(): pl.pallas_call(functools.partial(step_kernel, scale), out_shape=(jax.Shap...  11.7 us
    ppermute x4, waiting for transfers between devices, shift(): lax.ppermute(part, axis, [(i, (i + step) % count) for i in range(count)])  9.63 us
    ppermute x4, starting transfers between devices, shift(): lax.ppermute(part, axis, [(i, (i + step) % count) for i in range(count)])  6.84 us
    ppermute x2, starting transfers between devices, swap_cores(): return lax.ppermute(part, 'gy', [(i, i ^ 1) for i in range(count)])  4.73 us
    pallas_call x1, Pallas kernels, upper_factor(): pl.pallas_call(factor_kernel, out_shape=jax.ShapeDtypeStruct(shape, jnp.f...  4.04 us
    ppermute x2, waiting for transfers between devices, swap_cores(): return lax.ppermute(part, 'gy', [(i, i ^ 1) for i in range(count)])  1.69 us
  transfers between devices with their start and end apart: 6, of which 6 were waited for; matrix products, arithmetic and copies ran while one was open for 2% of the time, Pallas kernels for 0%

profile of v6, /device:TPU:1, one launch (start us, length us, event | category | flops | bytes accessed | tf_op | source)
XLA Modules:
  0.0 63.0 jit_solution(6282417528245860361)
XLA Ops:
  0.6 1.1 %fusion.8 = (f32[3,4,32,128]{3,2,1,0:T(8,128)S(1)}, f32[3,4,32,128]{3,2,1,0:T(8,128)S(1)}) fusion(f32[3,8,32,128]{3,2,1,0:T(8,128)} %velocity_ref.1), kind=kLoop, calls=%fused_computation.26 | loop fusion | bytes 786432 | tf_op jit(solution)/shard_map/slice | solution.py:277
  1.7 3.4 %collective-permute-start.1 = (f32[3,4,32,128]{3,2,1,0:T(8,128)S(1)}, f32[3,4,32,128]{3,2,1,0:T(8,128)S(1)}, u32[]{:S(2)}, u32[]{:S(2)}) collective-permute-start(f32[3,4,32,128]{3,2,1,0:T(8,128)S(1)} %get-tuple-element.15), channel_id=1, source_target_pairs={{0,96},{32,0},{64,32},{96,64},{1,97},{33,1},{65,33},{97,65},{2,98}... | collective-permute-start | bytes 589832 | tf_op jit(solution)/shard_map/ppermute | solution.py:272
  5.1 0.0 collective-permute-start
  5.1 1.0 %fusion.7 = (f32[3,8,4,128]{3,2,1,0:T(4,128)S(1)}, f32[3,8,4,128]{3,2,1,0:T(4,128)S(1)}) fusion(f32[3,8,32,128]{3,2,1,0:T(8,128)} %velocity_ref.1), kind=kLoop, calls=%fused_computation.25 | loop fusion | bytes 196608 | tf_op jit(solution)/shard_map/slice | solution.py:278
  6.0 0.1 fusion.5
  6.1 2.5 %collective-permute-done.1.right_ref = f32[3,4,32,128]{3,2,1,0:T(8,128)S(1)} collective-permute-done((f32[3,4,32,128]{3,2,1,0:T(8,128)S(1)}, f32[3,4,32,128]{3,2,1,0:T(8,128)S(1)}, u32[]{:S(2)}, u32[]{:S(2)}) %collective-permute-start.1) | collective-permute-done | bytes 196640 | tf_op jit(solution)/shard_map/ppermute | solution.py:272
  8.6 3.1 %collective-permute-done.left_ref = f32[3,4,32,128]{3,2,1,0:T(8,128)S(1)} collective-permute-done((f32[3,4,32,128]{3,2,1,0:T(8,128)S(1)}, f32[3,4,32,128]{3,2,1,0:T(8,128)S(1)}, u32[]{:S(2)}, u32[]{:S(2)}) %collective-permute-start) | collective-permute-done | bytes 196640 | tf_op jit(solution)/shard_map/ppermute | solution.py:272
  11.8 3.4 %collective-permute-start.2 = (f32[3,12,4,128]{3,2,1,0:T(4,128)S(1)}, f32[3,12,4,128]{3,2,1,0:T(4,128)S(1)}, u32[]{:S(2)}, u32[]{:S(2)}) collective-permute-start(f32[3,12,4,128]{3,2,1,0:T(4,128)S(1)} %pad_maximum_fusion), channel_id=1, source_target_pairs={{0,1},{1,2},{2,3},{3,4},{4,5},{5,6},{6,7},{7,8},{8,9},{9,10},{10,1... | collective-permute-start | bytes 221192 | tf_op jit(solution)/shard_map/ppermute | solution.py:272
  15.2 0.1 collective-permute-start.3
  15.4 1.2 %collective-permute-done.2.behind_ref = f32[3,12,4,128]{3,2,1,0:T(4,128)S(1)} collective-permute-done((f32[3,12,4,128]{3,2,1,0:T(4,128)S(1)}, f32[3,12,4,128]{3,2,1,0:T(4,128)S(1)}, u32[]{:S(2)}, u32[]{:S(2)}) %collective-permute-start.2) | collective-permute-done | bytes 73760 | tf_op jit(solution)/shard_map/ppermute | solution.py:272
  16.6 2.8 %collective-permute-done.3.ahead_ref = f32[3,12,4,128]{3,2,1,0:T(4,128)S(1)} collective-permute-done((f32[3,12,4,128]{3,2,1,0:T(4,128)S(1)}, f32[3,12,4,128]{3,2,1,0:T(4,128)S(1)}, u32[]{:S(2)}, u32[]{:S(2)}) %collective-permute-start.3) | collective-permute-done | bytes 73760 | tf_op jit(solution)/shard_map/ppermute | solution.py:272
  19.4 11.7 %step_gram.1 = (f32[3,8,32,128]{3,2,1,0:T(8,128)}, f32[80,128]{1,0:T(8,128)S(1)}) custom-call(f32[3,8,32,128]{3,2,1,0:T(8,128)} %velocity_ref.1, f32[3,4,32,128]{3,2,1,0:T(8,128)S(1)} %collective-permute-done.left_ref, f32[3,4,32,128]{3,2,1,0:T(8,128)S(1)} %collective-permute-done.1.right_ref, f32[3,12,4,128]{3,2,1,0:T(4,128)S(1)} %collective-permute-done.2.behind_ref, ...), custom_call_target="tpu_custom_call" | custom-call | tf_op jit(solution)/shard_map/step_gram/pallas_call | solution.py:246
  31.1 1.5 %collective-permute-start.4 = (f32[40,128]{1,0:T(8,128)S(1)}, f32[40,128]{1,0:T(8,128)S(1)}, u32[]{:S(2)}, u32[]{:S(2)}) collective-permute-start(f32[40,128]{1,0:T(8,128)S(1)} %constant_dynamic-slice_fusion), channel_id=1, source_target_pairs={{0,1},{1,0},{2,3},{3,2},{4,5},{5,4},{6,7},{7,6},{8,9},{9,8},{10,11... | collective-permute-start | bytes 61448 | tf_op jit(solution)/shard_map/ppermute | solution.py:306
  32.6 0.8 %collective-permute-done.4 = f32[40,128]{1,0:T(8,128)S(1)} collective-permute-done((f32[40,128]{1,0:T(8,128)S(1)}, f32[40,128]{1,0:T(8,128)S(1)}, u32[]{:S(2)}, u32[]{:S(2)}) %collective-permute-start.4) | collective-permute-done | bytes 20512 | tf_op jit(solution)/shard_map/ppermute | solution.py:306
  33.5 14.4 %all_to_all.10 = f32[16,40,128]{2,1,0:T(8,128)S(1)} all-to-all(f32[16,40,128]{2,1,0:T(8,128)S(1)} %broadcast_in_dim.20), channel_id=1, replica_groups={{0,2,4,6,8,10,12,14,16,18,20,22,24,26,28,30},{1,3,5,7,9,11,13,15,17,19,..., dimensions={0} | all-to-all | bytes 655360 | tf_op jit(solution)/shard_map/all_to_all | solution.py:311
  48.0 6.9 %all_to_all.11 = f32[4,40,128]{2,1,0:T(8,128)S(1)} all-to-all(f32[4,40,128]{2,1,0:T(8,128)S(1)} %broadcast_in_dim.21), channel_id=1, replica_groups=mesh['gx'=4,'gy'=32] {'gx'}, dimensions={0} | all-to-all | bytes 163840 | tf_op jit(solution)/shard_map/all_to_all | solution.py:311
  54.9 3.2 %collective-permute-start.5 = (f32[40,128]{1,0:T(8,128)S(1)}, f32[40,128]{1,0:T(8,128)S(1)}, u32[]{:S(2)}, u32[]{:S(2)}) collective-permute-start(f32[40,128]{1,0:T(8,128)S(1)} %reduce_sum.19), channel_id=1, source_target_pairs={{0,1},{1,0},{2,3},{3,2},{4,5},{5,4},{6,7},{7,6},{8,9},{9,8},{10,11... | collective-permute-start | bytes 61448 | tf_op jit(solution)/shard_map/ppermute | solution.py:306
  58.1 0.8 %collective-permute-done.5 = f32[40,128]{1,0:T(8,128)S(1)} collective-permute-done((f32[40,128]{1,0:T(8,128)S(1)}, f32[40,128]{1,0:T(8,128)S(1)}, u32[]{:S(2)}, u32[]{:S(2)}) %collective-permute-start.5) | collective-permute-done | bytes 20512 | tf_op jit(solution)/shard_map/ppermute | solution.py:306
  59.0 4.0 %upper_factor.1 = f32[128,128]{1,0:T(8,128)} custom-call(f32[80,128]{1,0:T(8,128)S(1)} %pad_maximum_fusion.2.packed_ref), custom_call_target="tpu_custom_call" | custom-call | tf_op jit(solution)/shard_map/upper_factor/pallas_call | solution.py:370
  (16 shorter events, 0.2 us)
Async XLA Ops:
  1.7 7.0 %collective-permute-start.1 = (f32[3,4,32,128]{3,2,1,0:T(8,128)S(1)}, f32[3,4,32,128]{3,2,1,0:T(8,128)S(1)}, u32[]{:S(2)}, u32[]{:S(2)}) collective-permute-start(f32[3,4,32,128]{3,2,1,0:T(8,128)S(1)} %get-tuple-element.15), channel_id=1, source_target_pairs={{0,96},{32,0},{64,32},{96,64},{1,97},{33,1},{65,33},{97,65},{2,98}... | collective-permute-start | bytes 589832 | tf_op jit(solution)/shard_map/ppermute | solution.py:272
  5.1 6.7 %collective-permute-start = (f32[3,4,32,128]{3,2,1,0:T(8,128)S(1)}, f32[3,4,32,128]{3,2,1,0:T(8,128)S(1)}, u32[]{:S(2)}, u32[]{:S(2)}) collective-permute-start(f32[3,4,32,128]{3,2,1,0:T(8,128)S(1)} %get-tuple-element.16), channel_id=1, source_target_pairs={{0,32},{32,64},{64,96},{96,0},{1,33},{33,65},{65,97},{97,1},{2,34}... | collective-permute-start | bytes 589832 | tf_op jit(solution)/shard_map/ppermute | solution.py:272
  11.8 4.8 %collective-permute-start.2 = (f32[3,12,4,128]{3,2,1,0:T(4,128)S(1)}, f32[3,12,4,128]{3,2,1,0:T(4,128)S(1)}, u32[]{:S(2)}, u32[]{:S(2)}) collective-permute-start(f32[3,12,4,128]{3,2,1,0:T(4,128)S(1)} %pad_maximum_fusion), channel_id=1, source_target_pairs={{0,1},{1,2},{2,3},{3,4},{4,5},{5,6},{6,7},{7,8},{8,9},{9,10},{10,1... | collective-permute-start | bytes 221192 | tf_op jit(solution)/shard_map/ppermute | solution.py:272
  15.2 4.1 %collective-permute-start.3 = (f32[3,12,4,128]{3,2,1,0:T(4,128)S(1)}, f32[3,12,4,128]{3,2,1,0:T(4,128)S(1)}, u32[]{:S(2)}, u32[]{:S(2)}) collective-permute-start(f32[3,12,4,128]{3,2,1,0:T(4,128)S(1)} %pad_maximum_fusion.1), channel_id=1, source_target_pairs={{0,31},{1,0},{2,1},{3,2},{4,3},{5,4},{6,5},{7,6},{8,7},{9,8},{10,9... | collective-permute-start | bytes 221192 | tf_op jit(solution)/shard_map/ppermute | solution.py:272
  31.1 2.4 %collective-permute-start.4 = (f32[40,128]{1,0:T(8,128)S(1)}, f32[40,128]{1,0:T(8,128)S(1)}, u32[]{:S(2)}, u32[]{:S(2)}) collective-permute-start(f32[40,128]{1,0:T(8,128)S(1)} %constant_dynamic-slice_fusion), channel_id=1, source_target_pairs={{0,1},{1,0},{2,3},{3,2},{4,5},{5,4},{6,7},{7,6},{8,9},{9,8},{10,11... | collective-permute-start | bytes 61448 | tf_op jit(solution)/shard_map/ppermute | solution.py:306
  54.9 4.0 %collective-permute-start.5 = (f32[40,128]{1,0:T(8,128)S(1)}, f32[40,128]{1,0:T(8,128)S(1)}, u32[]{:S(2)}, u32[]{:S(2)}) collective-permute-start(f32[40,128]{1,0:T(8,128)S(1)} %reduce_sum.19), channel_id=1, source_target_pairs={{0,1},{1,0},{2,3},{3,2},{4,5},{5,4},{6,7},{7,6},{8,9},{9,8},{10,11... | collective-permute-start | bytes 61448 | tf_op jit(solution)/shard_map/ppermute | solution.py:306

commit v7 on v6

--- a/solution.py
+++ b/solution.py
@@ -278,8 +278,16 @@
     back, front = lax.optimization_barrier((velocity[:, :, -4:], velocity[:, :, :4]))
     back = jnp.concatenate([left[:, 2:, -4:], back, right[:, :2, -4:]], axis=1)
     front = jnp.concatenate([left[:, 2:, :4], front, right[:, :2, :4]], axis=1)
-    behind = shift(back, "gy", 1)
-    ahead = shift(front, "gy", -1)
+    count = lax.axis_size("gy")
+    first = lax.axis_index("gy") % 2 == 0
+    outer = lax.ppermute(
+        jnp.where(first, front, back),
+        "gy",
+        [(i, (i + 2 * (i % 2) - 1) % count) for i in range(count)],
+    )
+    inner = swap_cores(jnp.where(first, back, front), count)
+    behind = jnp.where(first, outer, inner)
+    ahead = jnp.where(first, inner, outer)
     return left, right, behind, ahead
 
 
@@ -311,6 +319,11 @@
     return lax.all_to_all(copies, axis, 0, 0, axis_index_groups=groups).sum(0)
 
 
+def ring_sum(part, axis):
+    moved = [shift(part, axis, d) for d in (1, 2, 3)]
+    return (part + moved[1]) + (moved[0] + moved[2])
+
+
 def total_gram(packed):
     count = lax.axis_size("gy")
     half = packed.shape[0] // 2
@@ -319,7 +332,7 @@
     other = lax.dynamic_slice_in_dim(packed, (1 - core) * half, half, 0)
     part = mine + swap_cores(other, count)
     part = group_sum(part, "gy", count // 2, [list(range(c, count, 2)) for c in range(2)])
-    part = group_sum(part, "gx", lax.axis_size("gx"))
+    part = ring_sum(part, "gx")
     rest = swap_cores(part, count)
     low = jnp.where(core == 0, part, rest)
     high = jnp.where(core == 0, rest, part)

time: 63.2 us -> 63.9 us (1.011)
  blocking collectives: 21.4 us -> 14.4 us
  starting transfers between devices: 11.6 us -> 17.1 us
  waiting for transfers between devices: 11.3 us -> 13.6 us
    all_to_all x2 -> x1, blocking collectives: 21.4 us -> 14.4 us  [group_sum(): return lax.all_to_all(copies, axis, 0, 0, axis_index_groups=groups).sum(0)]
    ppermute x2 -> x3, starting transfers between devices: 4.73 us -> 10.6 us  [swap_cores(): return lax.ppermute(part, 'gy', [(i, i ^ 1) for i in range(count)])]
    ppermute x0 -> x1, waiting for transfers between devices: none -> 2.1 us  [exchange(): lax.ppermute(jnp.where(first, front, back), 'gy', [(i, (i + 2 * (i % 2) -...]
    ppermute x4 -> x5, starting transfers between devices: 6.84 us -> 4.91 us  [shift(): lax.ppermute(part, axis, [(i, (i + step) % count) for i in range(count)])]
    ppermute x0 -> x1, starting transfers between devices: none -> 1.62 us  [exchange(): lax.ppermute(jnp.where(first, front, back), 'gy', [(i, (i + 2 * (i % 2) -...]
    ppermute x4 -> x5, waiting for transfers between devices: 9.63 us -> 9.77 us  [shift(): lax.ppermute(part, axis, [(i, (i + step) % count) for i in range(count)])]
    ppermute x2 -> x3, waiting for transfers between devices: 1.69 us -> 1.69 us  [swap_cores(): return lax.ppermute(part, 'gy', [(i, i ^ 1) for i in range(count)])]
  transfers between devices with their start and end apart: 6 -> 9, of which waited for: 6 -> 8; matrix products, arithmetic and copies ran while one was open for 2% -> 2% of each run, Pallas kernels for 0% -> 0%
where the time goes in v7:
time: 63.9 us; the launch traced here: 63.7 us
  starting transfers between devices  17.1 us (27%)
  Pallas kernels  15.7 us (25%)
  blocking collectives  14.4 us (23%)
  waiting for transfers between devices  13.6 us (21%)
  local copies, waits for them, and re-layouts  2.1 us (3%)
  between operations  0.71 us (1%)
    all_to_all x1, blocking collectives, group_sum(): return lax.all_to_all(copies, axis, 0, 0, axis_index_groups=groups).sum(0)  14.4 us
    pallas_call x1, Pallas kernels, step_and_gram(): pl.pallas_call(functools.partial(step_kernel, scale), out_shape=(jax.Shap...  11.7 us
    ppermute x3, starting transfers between devices, swap_cores(): return lax.ppermute(part, 'gy', [(i, i ^ 1) for i in range(count)])  10.6 us
    ppermute x5, waiting for transfers between devices, shift(): lax.ppermute(part, axis, [(i, (i + step) % count) for i in range(count)])  9.77 us
    ppermute x5, starting transfers between devices, shift(): lax.ppermute(part, axis, [(i, (i + step) % count) for i in range(count)])  4.91 us
    pallas_call x1, Pallas kernels, upper_factor(): pl.pallas_call(factor_kernel, out_shape=jax.ShapeDtypeStruct(shape, jnp.f...  4.04 us
    ppermute x1, waiting for transfers between devices, exchange(): lax.ppermute(jnp.where(first, front, back), 'gy', [(i, (i + 2 * (i % 2) -...  2.1 us
    ppermute x3, waiting for transfers between devices, swap_cores(): return lax.ppermute(part, 'gy', [(i, i ^ 1) for i in range(count)])  1.69 us
  transfers between devices with their start and end apart: 9, of which 8 were waited for; matrix products, arithmetic and copies ran while one was open for 2% of the time, Pallas kernels for 0%

profile of v7, /device:TPU:1, one launch (start us, length us, event | category | flops | bytes accessed | tf_op | source)
XLA Modules:
  0.0 63.7 jit_solution(1014686232366662929)
XLA Ops:
  0.6 1.1 %fusion.8 = (f32[3,4,32,128]{3,2,1,0:T(8,128)S(1)}, f32[3,4,32,128]{3,2,1,0:T(8,128)S(1)}) fusion(f32[3,8,32,128]{3,2,1,0:T(8,128)} %velocity_ref.1), kind=kLoop, calls=%fused_computation.31 | loop fusion | bytes 786432 | tf_op jit(solution)/shard_map/slice | solution.py:277
  1.7 3.4 %collective-permute-start.1 = (f32[3,4,32,128]{3,2,1,0:T(8,128)S(1)}, f32[3,4,32,128]{3,2,1,0:T(8,128)S(1)}, u32[]{:S(2)}, u32[]{:S(2)}) collective-permute-start(f32[3,4,32,128]{3,2,1,0:T(8,128)S(1)} %get-tuple-element.15), channel_id=1, source_target_pairs={{0,96},{32,0},{64,32},{96,64},{1,97},{33,1},{65,33},{97,65},{2,98}... | collective-permute-start | bytes 589832 | tf_op jit(solution)/shard_map/ppermute | solution.py:272
  5.1 0.0 collective-permute-start
  5.1 1.0 %fusion.7 = (f32[3,8,4,128]{3,2,1,0:T(4,128)S(1)}, f32[3,8,4,128]{3,2,1,0:T(4,128)S(1)}) fusion(f32[3,8,32,128]{3,2,1,0:T(8,128)} %velocity_ref.1), kind=kLoop, calls=%fused_computation.30 | loop fusion | bytes 196608 | tf_op jit(solution)/shard_map/slice | solution.py:278
  6.0 0.1 fusion.5
  6.1 2.5 %collective-permute-done.1.right_ref = f32[3,4,32,128]{3,2,1,0:T(8,128)S(1)} collective-permute-done((f32[3,4,32,128]{3,2,1,0:T(8,128)S(1)}, f32[3,4,32,128]{3,2,1,0:T(8,128)S(1)}, u32[]{:S(2)}, u32[]{:S(2)}) %collective-permute-start.1) | collective-permute-done | bytes 196640 | tf_op jit(solution)/shard_map/ppermute | solution.py:272
  8.6 3.1 %collective-permute-done.left_ref = f32[3,4,32,128]{3,2,1,0:T(8,128)S(1)} collective-permute-done((f32[3,4,32,128]{3,2,1,0:T(8,128)S(1)}, f32[3,4,32,128]{3,2,1,0:T(8,128)S(1)}, u32[]{:S(2)}, u32[]{:S(2)}) %collective-permute-start) | collective-permute-done | bytes 196640 | tf_op jit(solution)/shard_map/ppermute | solution.py:272
  11.8 1.9 %collective-permute-start.3 = (f32[3,12,4,128]{3,2,1,0:T(4,128)S(1)}, f32[3,12,4,128]{3,2,1,0:T(4,128)S(1)}, u32[]{:S(2)}, u32[]{:S(2)}) collective-permute-start(f32[3,12,4,128]{3,2,1,0:T(4,128)S(1)} %get-tuple-element.23), channel_id=1, source_target_pairs={{0,1},{1,0},{2,3},{3,2},{4,5},{5,4},{6,7},{7,6},{8,9},{9,8},{10,11... | collective-permute-start | bytes 221192 | tf_op jit(solution)/shard_map/ppermute | solution.py:314
  13.7 1.6 %collective-permute-start.2 = (f32[3,12,4,128]{3,2,1,0:T(4,128)S(1)}, f32[3,12,4,128]{3,2,1,0:T(4,128)S(1)}, u32[]{:S(2)}, u32[]{:S(2)}) collective-permute-start(f32[3,12,4,128]{3,2,1,0:T(4,128)S(1)} %get-tuple-element.24), channel_id=1, source_target_pairs={{0,31},{1,2},{2,1},{3,4},{4,3},{5,6},{6,5},{7,8},{8,7},{9,10},{10,... | collective-permute-start | bytes 221192 | tf_op jit(solution)/shard_map/ppermute | solution.py:283
  15.4 0.0 collective-permute-done.3
  15.4 2.1 %collective-permute-done.2 = f32[3,12,4,128]{3,2,1,0:T(4,128)S(1)} collective-permute-done((f32[3,12,4,128]{3,2,1,0:T(4,128)S(1)}, f32[3,12,4,128]{3,2,1,0:T(4,128)S(1)}, u32[]{:S(2)}, u32[]{:S(2)}) %collective-permute-start.2) | collective-permute-done | bytes 73760 | tf_op jit(solution)/shard_map/ppermute | solution.py:283
  17.5 11.7 %step_gram.1 = (f32[3,8,32,128]{3,2,1,0:T(8,128)}, f32[80,128]{1,0:T(8,128)S(1)}) custom-call(f32[3,8,32,128]{3,2,1,0:T(8,128)} %velocity_ref.1, f32[3,4,32,128]{3,2,1,0:T(8,128)S(1)} %collective-permute-done.left_ref, f32[3,4,32,128]{3,2,1,0:T(8,128)S(1)} %collective-permute-done.1.right_ref, f32[3,12,4,128]{3,2,1,0:T(4,128)S(1)} %bitcast.19, ...), custom_call_target="tpu_custom_call" | custom-call | tf_op jit(solution)/shard_map/step_gram/pallas_call | solution.py:246
  29.2 4.9 %collective-permute-start.4 = (f32[40,128]{1,0:T(8,128)S(1)}, f32[40,128]{1,0:T(8,128)S(1)}, u32[]{:S(2)}, u32[]{:S(2)}) collective-permute-start(f32[40,128]{1,0:T(8,128)S(1)} %constant_dynamic-slice_fusion), channel_id=1, source_target_pairs={{0,1},{1,0},{2,3},{3,2},{4,5},{5,4},{6,7},{7,6},{8,9},{9,8},{10,11... | collective-permute-start | bytes 61448 | tf_op jit(solution)/shard_map/ppermute | solution.py:314
  34.2 0.8 %collective-permute-done.4 = f32[40,128]{1,0:T(8,128)S(1)} collective-permute-done((f32[40,128]{1,0:T(8,128)S(1)}, f32[40,128]{1,0:T(8,128)S(1)}, u32[]{:S(2)}, u32[]{:S(2)}) %collective-permute-start.4) | collective-permute-done | bytes 20512 | tf_op jit(solution)/shard_map/ppermute | solution.py:314
  35.0 14.4 %all_to_all.5 = f32[16,40,128]{2,1,0:T(8,128)S(1)} all-to-all(f32[16,40,128]{2,1,0:T(8,128)S(1)} %broadcast_in_dim.14), channel_id=1, replica_groups={{0,2,4,6,8,10,12,14,16,18,20,22,24,26,28,30},{1,3,5,7,9,11,13,15,17,19,..., dimensions={0} | all-to-all | bytes 655360 | tf_op jit(solution)/shard_map/all_to_all | solution.py:319
  49.4 0.1 collective-permute-start.7
  49.5 1.4 %collective-permute-start.6 = (f32[40,128]{1,0:T(8,128)S(1)}, f32[40,128]{1,0:T(8,128)S(1)}, u32[]{:S(2)}, u32[]{:S(2)}) collective-permute-start(f32[40,128]{1,0:T(8,128)S(1)} %reduce_sum.9), channel_id=1, source_target_pairs={{0,32},{32,64},{64,96},{96,0},{1,33},{33,65},{65,97},{97,1},{2,34}... | collective-permute-start | bytes 61448 | tf_op jit(solution)/shard_map/ppermute | solution.py:272
  51.0 0.0 collective-permute-start.5
  51.0 1.2 %collective-permute-done.7 = f32[40,128]{1,0:T(8,128)S(1)} collective-permute-done((f32[40,128]{1,0:T(8,128)S(1)}, f32[40,128]{1,0:T(8,128)S(1)}, u32[]{:S(2)}, u32[]{:S(2)}) %collective-permute-start.7) | collective-permute-done | bytes 20512 | tf_op jit(solution)/shard_map/ppermute | solution.py:272
  52.1 1.3 %collective-permute-done.6 = f32[40,128]{1,0:T(8,128)S(1)} collective-permute-done((f32[40,128]{1,0:T(8,128)S(1)}, f32[40,128]{1,0:T(8,128)S(1)}, u32[]{:S(2)}, u32[]{:S(2)}) %collective-permute-start.6) | collective-permute-done | bytes 20512 | tf_op jit(solution)/shard_map/ppermute | solution.py:272
  53.4 1.7 %collective-permute-done.5 = f32[40,128]{1,0:T(8,128)S(1)} collective-permute-done((f32[40,128]{1,0:T(8,128)S(1)}, f32[40,128]{1,0:T(8,128)S(1)}, u32[]{:S(2)}, u32[]{:S(2)}) %collective-permute-start.5) | collective-permute-done | bytes 20512 | tf_op jit(solution)/shard_map/ppermute | solution.py:272
  55.1 3.7 %collective-permute-start.8 = (f32[40,128]{1,0:T(8,128)S(1)}, f32[40,128]{1,0:T(8,128)S(1)}, u32[]{:S(2)}, u32[]{:S(2)}) collective-permute-start(f32[40,128]{1,0:T(8,128)S(1)} %add_add_fusion), channel_id=1, source_target_pairs={{0,1},{1,0},{2,3},{3,2},{4,5},{5,4},{6,7},{7,6},{8,9},{9,8},{10,11... | collective-permute-start | bytes 61448 | tf_op jit(solution)/shard_map/ppermute | solution.py:314
  58.9 0.8 %collective-permute-done.8 = f32[40,128]{1,0:T(8,128)S(1)} collective-permute-done((f32[40,128]{1,0:T(8,128)S(1)}, f32[40,128]{1,0:T(8,128)S(1)}, u32[]{:S(2)}, u32[]{:S(2)}) %collective-permute-start.8) | collective-permute-done | bytes 20512 | tf_op jit(solution)/shard_map/ppermute | solution.py:314
  59.7 4.0 %upper_factor.1 = f32[128,128]{1,0:T(8,128)} custom-call(f32[80,128]{1,0:T(8,128)S(1)} %pad_maximum_fusion.2.packed_ref), custom_call_target="tpu_custom_call" | custom-call | tf_op jit(solution)/shard_map/upper_factor/pallas_call | solution.py:383
  (15 shorter events, 0.2 us)
Async XLA Ops:
  1.7 7.0 %collective-permute-start.1 = (f32[3,4,32,128]{3,2,1,0:T(8,128)S(1)}, f32[3,4,32,128]{3,2,1,0:T(8,128)S(1)}, u32[]{:S(2)}, u32[]{:S(2)}) collective-permute-start(f32[3,4,32,128]{3,2,1,0:T(8,128)S(1)} %get-tuple-element.15), channel_id=1, source_target_pairs={{0,96},{32,0},{64,32},{96,64},{1,97},{33,1},{65,33},{97,65},{2,98}... | collective-permute-start | bytes 589832 | tf_op jit(solution)/shard_map/ppermute | solution.py:272
  5.1 6.7 %collective-permute-start = (f32[3,4,32,128]{3,2,1,0:T(8,128)S(1)}, f32[3,4,32,128]{3,2,1,0:T(8,128)S(1)}, u32[]{:S(2)}, u32[]{:S(2)}) collective-permute-start(f32[3,4,32,128]{3,2,1,0:T(8,128)S(1)} %get-tuple-element.16), channel_id=1, source_target_pairs={{0,32},{32,64},{64,96},{96,0},{1,33},{33,65},{65,97},{97,1},{2,34}... | collective-permute-start | bytes 589832 | tf_op jit(solution)/shard_map/ppermute | solution.py:272
  11.8 3.6 %collective-permute-start.3 = (f32[3,12,4,128]{3,2,1,0:T(4,128)S(1)}, f32[3,12,4,128]{3,2,1,0:T(4,128)S(1)}, u32[]{:S(2)}, u32[]{:S(2)}) collective-permute-start(f32[3,12,4,128]{3,2,1,0:T(4,128)S(1)} %get-tuple-element.23), channel_id=1, source_target_pairs={{0,1},{1,0},{2,3},{3,2},{4,5},{5,4},{6,7},{7,6},{8,9},{9,8},{10,11... | collective-permute-start | bytes 221192 | tf_op jit(solution)/shard_map/ppermute | solution.py:314
  13.7 3.8 %collective-permute-start.2 = (f32[3,12,4,128]{3,2,1,0:T(4,128)S(1)}, f32[3,12,4,128]{3,2,1,0:T(4,128)S(1)}, u32[]{:S(2)}, u32[]{:S(2)}) collective-permute-start(f32[3,12,4,128]{3,2,1,0:T(4,128)S(1)} %get-tuple-element.24), channel_id=1, source_target_pairs={{0,31},{1,2},{2,1},{3,4},{4,3},{5,6},{6,5},{7,8},{8,7},{9,10},{10,... | collective-permute-start | bytes 221192 | tf_op jit(solution)/shard_map/ppermute | solution.py:283
  29.2 5.8 %collective-permute-start.4 = (f32[40,128]{1,0:T(8,128)S(1)}, f32[40,128]{1,0:T(8,128)S(1)}, u32[]{:S(2)}, u32[]{:S(2)}) collective-permute-start(f32[40,128]{1,0:T(8,128)S(1)} %constant_dynamic-slice_fusion), channel_id=1, source_target_pairs={{0,1},{1,0},{2,3},{3,2},{4,5},{5,4},{6,7},{7,6},{8,9},{9,8},{10,11... | collective-permute-start | bytes 61448 | tf_op jit(solution)/shard_map/ppermute | solution.py:314
  49.4 2.7 %collective-permute-start.7 = (f32[40,128]{1,0:T(8,128)S(1)}, f32[40,128]{1,0:T(8,128)S(1)}, u32[]{:S(2)}, u32[]{:S(2)}) collective-permute-start(f32[40,128]{1,0:T(8,128)S(1)} %reduce_sum.9), channel_id=1, source_target_pairs={{0,96},{32,0},{64,32},{96,64},{1,97},{33,1},{65,33},{97,65},{2,98}... | collective-permute-start | bytes 61448 | tf_op jit(solution)/shard_map/ppermute | solution.py:272
  49.5 3.9 %collective-permute-start.6 = (f32[40,128]{1,0:T(8,128)S(1)}, f32[40,128]{1,0:T(8,128)S(1)}, u32[]{:S(2)}, u32[]{:S(2)}) collective-permute-start(f32[40,128]{1,0:T(8,128)S(1)} %reduce_sum.9), channel_id=1, source_target_pairs={{0,32},{32,64},{64,96},{96,0},{1,33},{33,65},{65,97},{97,1},{2,34}... | collective-permute-start | bytes 61448 | tf_op jit(solution)/shard_map/ppermute | solution.py:272
  51.0 4.1 %collective-permute-start.5 = (f32[40,128]{1,0:T(8,128)S(1)}, f32[40,128]{1,0:T(8,128)S(1)}, u32[]{:S(2)}, u32[]{:S(2)}) collective-permute-start(f32[40,128]{1,0:T(8,128)S(1)} %reduce_sum.9), channel_id=1, source_target_pairs={{0,64},{32,96},{64,0},{96,32},{1,65},{33,97},{65,1},{97,33},{2,66}... | collective-permute-start | bytes 61448 | tf_op jit(solution)/shard_map/ppermute | solution.py:272
  55.1 4.6 %collective-permute-start.8 = (f32[40,128]{1,0:T(8,128)S(1)}, f32[40,128]{1,0:T(8,128)S(1)}, u32[]{:S(2)}, u32[]{:S(2)}) collective-permute-start(f32[40,128]{1,0:T(8,128)S(1)} %add_add_fusion), channel_id=1, source_target_pairs={{0,1},{1,0},{2,3},{3,2},{4,5},{5,4},{6,7},{7,6},{8,9},{9,8},{10,11... | collective-permute-start | bytes 61448 | tf_op jit(solution)/shard_map/ppermute | solution.py:314

commit v8 on v7

--- a/solution.py
+++ b/solution.py
@@ -90,7 +90,7 @@
 
 
 CHUNKS = (128, 128, 128)
-MXU_STEP = 32
+MXU_STEP = 64
 
 
 def step_kernel(
@@ -98,6 +98,8 @@
     velocity_ref,
     left_ref,
     right_ref,
+    far_left_ref,
+    far_right_ref,
     behind_ref,
     ahead_ref,
     weights_ref,
@@ -125,8 +127,10 @@
         for i, (source, target) in enumerate(
             (
                 (velocity_ref, field.at[:, pl.ds(4, length_x), pl.ds(4, length_z)]),
-                (left_ref, field.at[:, pl.ds(0, 4), pl.ds(4, length_z)]),
-                (right_ref, field.at[:, pl.ds(4 + length_x, 4), pl.ds(4, length_z)]),
+                (left_ref, field.at[:, pl.ds(2, 2), pl.ds(4, length_z)]),
+                (right_ref, field.at[:, pl.ds(4 + length_x, 2), pl.ds(4, length_z)]),
+                (far_left_ref, field.at[:, pl.ds(0, 2), pl.ds(4, length_z)]),
+                (far_right_ref, field.at[:, pl.ds(6 + length_x, 2), pl.ds(4, length_z)]),
                 (behind_ref, field.at[:, pl.ds(2, 4 + length_x), pl.ds(0, 4)]),
                 (ahead_ref, field.at[:, pl.ds(2, 4 + length_x), pl.ds(4 + length_z, 4)]),
             )
@@ -249,7 +253,7 @@
             jax.ShapeDtypeStruct(velocity.shape, jnp.float32),
             jax.ShapeDtypeStruct((PACKED_ROWS, 128), jnp.float32),
         ),
-        in_specs=[hbm, free, free, free, free, vmem, hbm, hbm],
+        in_specs=[hbm, free, free, free, free, free, free, vmem, hbm, hbm],
         out_specs=(hbm, vmem),
         scratch_shapes=[
             pltpu.VMEM((basis.shape[1], 256, lanes), jnp.bfloat16),
@@ -259,7 +263,7 @@
             pltpu.VMEM((3, length_x + 4, length_z + 8, lanes), jnp.float32),
             pltpu.VMEM(velocity.shape, jnp.float32),
             pltpu.SemaphoreType.DMA((len(CHUNKS),)),
-            pltpu.SemaphoreType.DMA((5,)),
+            pltpu.SemaphoreType.DMA((7,)),
             pltpu.SemaphoreType.DMA((1,)),
         ],
         compiler_params=pltpu.CompilerParams(vmem_limit_bytes=36 * 2**20),
@@ -273,11 +277,13 @@
 
 
 def exchange(velocity):
-    left = shift(velocity[:, -4:], "gx", 1)
-    right = shift(velocity[:, :4], "gx", -1)
+    left = shift(velocity[:, -2:], "gx", 1)
+    right = shift(velocity[:, :2], "gx", -1)
+    far_left = shift(velocity[:, -4:-2], "gx", 1)
+    far_right = shift(velocity[:, 2:4], "gx", -1)
     back, front = lax.optimization_barrier((velocity[:, :, -4:], velocity[:, :, :4]))
-    back = jnp.concatenate([left[:, 2:, -4:], back, right[:, :2, -4:]], axis=1)
-    front = jnp.concatenate([left[:, 2:, :4], front, right[:, :2, :4]], axis=1)
+    back = jnp.concatenate([left[:, :, -4:], back, right[:, :, -4:]], axis=1)
+    front = jnp.concatenate([left[:, :, :4], front, right[:, :, :4]], axis=1)
     count = lax.axis_size("gy")
     first = lax.axis_index("gy") % 2 == 0
     outer = lax.ppermute(
@@ -288,7 +294,7 @@
     inner = swap_cores(jnp.where(first, back, front), count)
     behind = jnp.where(first, outer, inner)
     ahead = jnp.where(first, inner, outer)
-    return left, right, behind, ahead
+    return left, right, far_left, far_right, behind, ahead
 
 
 def wall_rows(points):

time: 63.9 us -> 65.2 us (1.020)
  starting transfers between devices: 17.1 us -> 20.6 us
  waiting for transfers between devices: 13.6 us -> 11.5 us
    ppermute x5 -> x7, starting transfers between devices: 4.91 us -> 7.57 us  [shift(): lax.ppermute(part, axis, [(i, (i + step) % count) for i in range(count)])]
    ppermute x5 -> x7, waiting for transfers between devices: 9.77 us -> 7.75 us  [shift(): lax.ppermute(part, axis, [(i, (i + step) % count) for i in range(count)])]
    ppermute x3, starting transfers between devices: 10.6 us -> 11.4 us  [swap_cores(): return lax.ppermute(part, 'gy', [(i, i ^ 1) for i in range(count)])]
  transfers between devices with their start and end apart: 9 -> 11, of which waited for: 8 -> 8; matrix products, arithmetic and copies ran while one was open for 2% -> 2% of each run, Pallas kernels for 0% -> 0%
where the time goes in v8:
time: 65.2 us; the launch traced here: 65 us
  starting transfers between devices  20.6 us (32%)
  Pallas kernels  15.4 us (24%)
  blocking collectives  14.4 us (22%)
  waiting for transfers between devices  11.5 us (18%)
  local copies, waits for them, and re-layouts  2.12 us (3%)
  between operations  0.73 us (1%)
    all_to_all x1, blocking collectives, group_sum(): return lax.all_to_all(copies, axis, 0, 0, axis_index_groups=groups).sum(0)  14.4 us
    ppermute x3, starting transfers between devices, swap_cores(): return lax.ppermute(part, 'gy', [(i, i ^ 1) for i in range(count)])  11.4 us
    pallas_call x1, Pallas kernels, step_and_gram(): pl.pallas_call(functools.partial(step_kernel, scale), out_shape=(jax.Shap...  11.4 us
    ppermute x7, waiting for transfers between devices, shift(): lax.ppermute(part, axis, [(i, (i + step) % count) for i in range(count)])  7.75 us
    ppermute x7, starting transfers between devices, shift(): lax.ppermute(part, axis, [(i, (i + step) % count) for i in range(count)])  7.57 us
    pallas_call x1, Pallas kernels, upper_factor(): pl.pallas_call(factor_kernel, out_shape=jax.ShapeDtypeStruct(shape, jnp.f...  4.04 us
    ppermute x1, waiting for transfers between devices, exchange(): lax.ppermute(jnp.where(first, front, back), 'gy', [(i, (i + 2 * (i % 2) -...  2.1 us
    ppermute x3, waiting for transfers between devices, swap_cores(): return lax.ppermute(part, 'gy', [(i, i ^ 1) for i in range(count)])  1.69 us
  transfers between devices with their start and end apart: 11, of which 8 were waited for; matrix products, arithmetic and copies ran while one was open for 2% of the time, Pallas kernels for 0%

profile of v8, /device:TPU:1, one launch (start us, length us, event | category | flops | bytes accessed | tf_op | source)
XLA Modules:
  0.0 65.0 jit_solution(16355810272963476646)
XLA Ops:
  0.6 1.1 %fusion.8 = (f32[3,2,32,128]{3,2,1,0:T(8,128)S(1)}, f32[3,2,32,128]{3,2,1,0:T(8,128)S(1)}, f32[3,2,32,128]{3,2,1,0:T(8,128)S(1)}, f32[3,2,32,128]{3,2,1,0:T(8,128)S(1)}) fusion(f32[3,8,32,128]{3,2,1,0:T(8,128)} %velocity_ref.1), kind=kLoop, calls=%fused_computation.31 | loop fusion | bytes 786432 | tf_op jit(solution)/shard_map/slice | solution.py:283
  1.7 3.4 %collective-permute-start.3 = (f32[3,2,32,128]{3,2,1,0:T(8,128)S(1)}, f32[3,2,32,128]{3,2,1,0:T(8,128)S(1)}, u32[]{:S(2)}, u32[]{:S(2)}) collective-permute-start(f32[3,2,32,128]{3,2,1,0:T(8,128)S(1)} %get-tuple-element.15), channel_id=1, source_target_pairs={{0,96},{32,0},{64,32},{96,64},{1,97},{33,1},{65,33},{97,65},{2,98}... | collective-permute-start | bytes 294920 | tf_op jit(solution)/shard_map/ppermute | solution.py:276
  5.1 0.0 collective-permute-start.2
  5.1 2.7 %collective-permute-start.1 = (f32[3,2,32,128]{3,2,1,0:T(8,128)S(1)}, f32[3,2,32,128]{3,2,1,0:T(8,128)S(1)}, u32[]{:S(2)}, u32[]{:S(2)}) collective-permute-start(f32[3,2,32,128]{3,2,1,0:T(8,128)S(1)} %get-tuple-element.17), channel_id=1, source_target_pairs={{0,96},{32,0},{64,32},{96,64},{1,97},{33,1},{65,33},{97,65},{2,98}... | collective-permute-start | bytes 294920 | tf_op jit(solution)/shard_map/ppermute | solution.py:276
  7.8 0.0 collective-permute-start
  7.8 1.0 %fusion.7 = (f32[3,8,4,128]{3,2,1,0:T(4,128)S(1)}, f32[3,8,4,128]{3,2,1,0:T(4,128)S(1)}) fusion(f32[3,8,32,128]{3,2,1,0:T(8,128)} %velocity_ref.1), kind=kLoop, calls=%fused_computation.30 | loop fusion | bytes 196608 | tf_op jit(solution)/shard_map/slice | solution.py:284
  8.7 0.1 fusion.5
  8.8 0.6 collective-permute-done.1.right_ref
  9.4 3.0 %collective-permute-done.left_ref = f32[3,2,32,128]{3,2,1,0:T(8,128)S(1)} collective-permute-done((f32[3,2,32,128]{3,2,1,0:T(8,128)S(1)}, f32[3,2,32,128]{3,2,1,0:T(8,128)S(1)}, u32[]{:S(2)}, u32[]{:S(2)}) %collective-permute-start) | collective-permute-done | bytes 98336 | tf_op jit(solution)/shard_map/ppermute | solution.py:276
  12.5 2.7 %collective-permute-start.5 = (f32[3,12,4,128]{3,2,1,0:T(4,128)S(1)}, f32[3,12,4,128]{3,2,1,0:T(4,128)S(1)}, u32[]{:S(2)}, u32[]{:S(2)}) collective-permute-start(f32[3,12,4,128]{3,2,1,0:T(4,128)S(1)} %get-tuple-element.21), channel_id=1, source_target_pairs={{0,1},{1,0},{2,3},{3,2},{4,5},{5,4},{6,7},{7,6},{8,9},{9,8},{10,11... | collective-permute-start | bytes 221192 | tf_op jit(solution)/shard_map/ppermute | solution.py:320
  15.2 1.6 %collective-permute-start.4 = (f32[3,12,4,128]{3,2,1,0:T(4,128)S(1)}, f32[3,12,4,128]{3,2,1,0:T(4,128)S(1)}, u32[]{:S(2)}, u32[]{:S(2)}) collective-permute-start(f32[3,12,4,128]{3,2,1,0:T(4,128)S(1)} %get-tuple-element.22), channel_id=1, source_target_pairs={{0,31},{1,2},{2,1},{3,4},{4,3},{5,6},{6,5},{7,8},{8,7},{9,10},{10,... | collective-permute-start | bytes 221192 | tf_op jit(solution)/shard_map/ppermute | solution.py:289
  16.9 0.0 collective-permute-done.5
  16.9 2.1 %collective-permute-done.4 = f32[3,12,4,128]{3,2,1,0:T(4,128)S(1)} collective-permute-done((f32[3,12,4,128]{3,2,1,0:T(4,128)S(1)}, f32[3,12,4,128]{3,2,1,0:T(4,128)S(1)}, u32[]{:S(2)}, u32[]{:S(2)}) %collective-permute-start.4) | collective-permute-done | bytes 73760 | tf_op jit(solution)/shard_map/ppermute | solution.py:289
  19.0 0.0 collective-permute-done.3.far_right_ref
  19.0 0.0 collective-permute-done.2.far_left_ref
  19.0 11.4 %step_gram.1 = (f32[3,8,32,128]{3,2,1,0:T(8,128)}, f32[80,128]{1,0:T(8,128)S(1)}) custom-call(f32[3,8,32,128]{3,2,1,0:T(8,128)} %velocity_ref.1, f32[3,2,32,128]{3,2,1,0:T(8,128)S(1)} %collective-permute-done.left_ref, f32[3,2,32,128]{3,2,1,0:T(8,128)S(1)} %collective-permute-done.1.right_ref, f32[3,2,32,128]{3,2,1,0:T(8,128)S(1)} %collective-permute-done.2.far_left_ref, ...), custom_call_target="tpu_custom_call" | custom-call | tf_op jit(solution)/shard_map/step_gram/pallas_call | solution.py:250
  30.5 4.9 %collective-permute-start.6 = (f32[40,128]{1,0:T(8,128)S(1)}, f32[40,128]{1,0:T(8,128)S(1)}, u32[]{:S(2)}, u32[]{:S(2)}) collective-permute-start(f32[40,128]{1,0:T(8,128)S(1)} %constant_dynamic-slice_fusion), channel_id=1, source_target_pairs={{0,1},{1,0},{2,3},{3,2},{4,5},{5,4},{6,7},{7,6},{8,9},{9,8},{10,11... | collective-permute-start | bytes 61448 | tf_op jit(solution)/shard_map/ppermute | solution.py:320
  35.4 0.8 %collective-permute-done.6 = f32[40,128]{1,0:T(8,128)S(1)} collective-permute-done((f32[40,128]{1,0:T(8,128)S(1)}, f32[40,128]{1,0:T(8,128)S(1)}, u32[]{:S(2)}, u32[]{:S(2)}) %collective-permute-start.6) | collective-permute-done | bytes 20512 | tf_op jit(solution)/shard_map/ppermute | solution.py:320
  36.3 14.4 %all_to_all.5 = f32[16,40,128]{2,1,0:T(8,128)S(1)} all-to-all(f32[16,40,128]{2,1,0:T(8,128)S(1)} %broadcast_in_dim.14), channel_id=1, replica_groups={{0,2,4,6,8,10,12,14,16,18,20,22,24,26,28,30},{1,3,5,7,9,11,13,15,17,19,..., dimensions={0} | all-to-all | bytes 655360 | tf_op jit(solution)/shard_map/all_to_all | solution.py:325
  50.7 0.1 collective-permute-start.9
  50.7 1.5 %collective-permute-start.8 = (f32[40,128]{1,0:T(8,128)S(1)}, f32[40,128]{1,0:T(8,128)S(1)}, u32[]{:S(2)}, u32[]{:S(2)}) collective-permute-start(f32[40,128]{1,0:T(8,128)S(1)} %reduce_sum.9), channel_id=1, source_target_pairs={{0,32},{32,64},{64,96},{96,0},{1,33},{33,65},{65,97},{97,1},{2,34}... | collective-permute-start | bytes 61448 | tf_op jit(solution)/shard_map/ppermute | solution.py:276
  52.2 0.0 collective-permute-start.7
  52.2 1.2 %collective-permute-done.9 = f32[40,128]{1,0:T(8,128)S(1)} collective-permute-done((f32[40,128]{1,0:T(8,128)S(1)}, f32[40,128]{1,0:T(8,128)S(1)}, u32[]{:S(2)}, u32[]{:S(2)}) %collective-permute-start.9) | collective-permute-done | bytes 20512 | tf_op jit(solution)/shard_map/ppermute | solution.py:276
  53.4 1.3 %collective-permute-done.8 = f32[40,128]{1,0:T(8,128)S(1)} collective-permute-done((f32[40,128]{1,0:T(8,128)S(1)}, f32[40,128]{1,0:T(8,128)S(1)}, u32[]{:S(2)}, u32[]{:S(2)}) %collective-permute-start.8) | collective-permute-done | bytes 20512 | tf_op jit(solution)/shard_map/ppermute | solution.py:276
  54.6 1.7 %collective-permute-done.7 = f32[40,128]{1,0:T(8,128)S(1)} collective-permute-done((f32[40,128]{1,0:T(8,128)S(1)}, f32[40,128]{1,0:T(8,128)S(1)}, u32[]{:S(2)}, u32[]{:S(2)}) %collective-permute-start.7) | collective-permute-done | bytes 20512 | tf_op jit(solution)/shard_map/ppermute | solution.py:276
  56.3 3.7 %collective-permute-start.10 = (f32[40,128]{1,0:T(8,128)S(1)}, f32[40,128]{1,0:T(8,128)S(1)}, u32[]{:S(2)}, u32[]{:S(2)}) collective-permute-start(f32[40,128]{1,0:T(8,128)S(1)} %add_add_fusion), channel_id=1, source_target_pairs={{0,1},{1,0},{2,3},{3,2},{4,5},{5,4},{6,7},{7,6},{8,9},{9,8},{10,11... | collective-permute-start | bytes 61448 | tf_op jit(solution)/shard_map/ppermute | solution.py:320
  60.1 0.8 %collective-permute-done.10 = f32[40,128]{1,0:T(8,128)S(1)} collective-permute-done((f32[40,128]{1,0:T(8,128)S(1)}, f32[40,128]{1,0:T(8,128)S(1)}, u32[]{:S(2)}, u32[]{:S(2)}) %collective-permute-start.10) | collective-permute-done | bytes 20512 | tf_op jit(solution)/shard_map/ppermute | solution.py:320
  60.9 4.0 %upper_factor.1 = f32[128,128]{1,0:T(8,128)} custom-call(f32[80,128]{1,0:T(8,128)S(1)} %pad_maximum_fusion.2.packed_ref), custom_call_target="tpu_custom_call" | custom-call | tf_op jit(solution)/shard_map/upper_factor/pallas_call | solution.py:389
  (15 shorter events, 0.2 us)
Async XLA Ops:
  1.7 17.3 %collective-permute-start.3 = (f32[3,2,32,128]{3,2,1,0:T(8,128)S(1)}, f32[3,2,32,128]{3,2,1,0:T(8,128)S(1)}, u32[]{:S(2)}, u32[]{:S(2)}) collective-permute-start(f32[3,2,32,128]{3,2,1,0:T(8,128)S(1)} %get-tuple-element.15), channel_id=1, source_target_pairs={{0,96},{32,0},{64,32},{96,64},{1,97},{33,1},{65,33},{97,65},{2,98}... | collective-permute-start | bytes 294920 | tf_op jit(solution)/shard_map/ppermute | solution.py:276
  5.1 14.0 %collective-permute-start.2 = (f32[3,2,32,128]{3,2,1,0:T(8,128)S(1)}, f32[3,2,32,128]{3,2,1,0:T(8,128)S(1)}, u32[]{:S(2)}, u32[]{:S(2)}) collective-permute-start(f32[3,2,32,128]{3,2,1,0:T(8,128)S(1)} %get-tuple-element.16), channel_id=1, source_target_pairs={{0,32},{32,64},{64,96},{96,0},{1,33},{33,65},{65,97},{97,1},{2,34}... | collective-permute-start | bytes 294920 | tf_op jit(solution)/shard_map/ppermute | solution.py:276
  5.1 4.3 %collective-permute-start.1 = (f32[3,2,32,128]{3,2,1,0:T(8,128)S(1)}, f32[3,2,32,128]{3,2,1,0:T(8,128)S(1)}, u32[]{:S(2)}, u32[]{:S(2)}) collective-permute-start(f32[3,2,32,128]{3,2,1,0:T(8,128)S(1)} %get-tuple-element.17), channel_id=1, source_target_pairs={{0,96},{32,0},{64,32},{96,64},{1,97},{33,1},{65,33},{97,65},{2,98}... | collective-permute-start | bytes 294920 | tf_op jit(solution)/shard_map/ppermute | solution.py:276
  7.8 4.7 %collective-permute-start = (f32[3,2,32,128]{3,2,1,0:T(8,128)S(1)}, f32[3,2,32,128]{3,2,1,0:T(8,128)S(1)}, u32[]{:S(2)}, u32[]{:S(2)}) collective-permute-start(f32[3,2,32,128]{3,2,1,0:T(8,128)S(1)} %get-tuple-element.18), channel_id=1, source_target_pairs={{0,32},{32,64},{64,96},{96,0},{1,33},{33,65},{65,97},{97,1},{2,34}... | collective-permute-start | bytes 294920 | tf_op jit(solution)/shard_map/ppermute | solution.py:276
  12.5 4.4 %collective-permute-start.5 = (f32[3,12,4,128]{3,2,1,0:T(4,128)S(1)}, f32[3,12,4,128]{3,2,1,0:T(4,128)S(1)}, u32[]{:S(2)}, u32[]{:S(2)}) collective-permute-start(f32[3,12,4,128]{3,2,1,0:T(4,128)S(1)} %get-tuple-element.21), channel_id=1, source_target_pairs={{0,1},{1,0},{2,3},{3,2},{4,5},{5,4},{6,7},{7,6},{8,9},{9,8},{10,11... | collective-permute-start | bytes 221192 | tf_op jit(solution)/shard_map/ppermute | solution.py:320
  15.2 3.8 %collective-permute-start.4 = (f32[3,12,4,128]{3,2,1,0:T(4,128)S(1)}, f32[3,12,4,128]{3,2,1,0:T(4,128)S(1)}, u32[]{:S(2)}, u32[]{:S(2)}) collective-permute-start(f32[3,12,4,128]{3,2,1,0:T(4,128)S(1)} %get-tuple-element.22), channel_id=1, source_target_pairs={{0,31},{1,2},{2,1},{3,4},{4,3},{5,6},{6,5},{7,8},{8,7},{9,10},{10,... | collective-permute-start | bytes 221192 | tf_op jit(solution)/shard_map/ppermute | solution.py:289
  30.5 5.8 %collective-permute-start.6 = (f32[40,128]{1,0:T(8,128)S(1)}, f32[40,128]{1,0:T(8,128)S(1)}, u32[]{:S(2)}, u32[]{:S(2)}) collective-permute-start(f32[40,128]{1,0:T(8,128)S(1)} %constant_dynamic-slice_fusion), channel_id=1, source_target_pairs={{0,1},{1,0},{2,3},{3,2},{4,5},{5,4},{6,7},{7,6},{8,9},{9,8},{10,11... | collective-permute-start | bytes 61448 | tf_op jit(solution)/shard_map/ppermute | solution.py:320
  50.7 2.7 %collective-permute-start.9 = (f32[40,128]{1,0:T(8,128)S(1)}, f32[40,128]{1,0:T(8,128)S(1)}, u32[]{:S(2)}, u32[]{:S(2)}) collective-permute-start(f32[40,128]{1,0:T(8,128)S(1)} %reduce_sum.9), channel_id=1, source_target_pairs={{0,96},{32,0},{64,32},{96,64},{1,97},{33,1},{65,33},{97,65},{2,98}... | collective-permute-start | bytes 61448 | tf_op jit(solution)/shard_map/ppermute | solution.py:276
  50.7 3.9 %collective-permute-start.8 = (f32[40,128]{1,0:T(8,128)S(1)}, f32[40,128]{1,0:T(8,128)S(1)}, u32[]{:S(2)}, u32[]{:S(2)}) collective-permute-start(f32[40,128]{1,0:T(8,128)S(1)} %reduce_sum.9), channel_id=1, source_target_pairs={{0,32},{32,64},{64,96},{96,0},{1,33},{33,65},{65,97},{97,1},{2,34}... | collective-permute-start | bytes 61448 | tf_op jit(solution)/shard_map/ppermute | solution.py:276
  52.2 4.1 %collective-permute-start.7 = (f32[40,128]{1,0:T(8,128)S(1)}, f32[40,128]{1,0:T(8,128)S(1)}, u32[]{:S(2)}, u32[]{:S(2)}) collective-permute-start(f32[40,128]{1,0:T(8,128)S(1)} %reduce_sum.9), channel_id=1, source_target_pairs={{0,64},{32,96},{64,0},{96,32},{1,65},{33,97},{65,1},{97,33},{2,66}... | collective-permute-start | bytes 61448 | tf_op jit(solution)/shard_map/ppermute | solution.py:276
  56.3 4.6 %collective-permute-start.10 = (f32[40,128]{1,0:T(8,128)S(1)}, f32[40,128]{1,0:T(8,128)S(1)}, u32[]{:S(2)}, u32[]{:S(2)}) collective-permute-start(f32[40,128]{1,0:T(8,128)S(1)} %add_add_fusion), channel_id=1, source_target_pairs={{0,1},{1,0},{2,3},{3,2},{4,5},{5,4},{6,7},{7,6},{8,9},{9,8},{10,11... | collective-permute-start | bytes 61448 | tf_op jit(solution)/shard_map/ppermute | solution.py:320
